TPU v7x, 32 devices: a whole 2x2x4 slice. The times are simulated.
32 devices in a mesh: fsdp: 2 (over x), ep: 16 (over z, y, core).
Axes of the slice: x: 2, y: 2, z: 4, core: 2. Of those that a mesh axis runs over, the one named last changes fastest.
Arguments:
- x_resid: bfloat16 [32, 64, 2048], P(('fsdp', 'ep')), may hold values from -1.5 to 1.5
- q_latent: bfloat16 [32, 64, 8, 512], P(('fsdp', 'ep')), may hold values from -3 to 3
- q_rope: bfloat16 [32, 64, 8, 64], P(('fsdp', 'ep')), may hold values from -27 to 27
- cache_latent: bfloat16 [32, 64, 512], P(('fsdp', 'ep')), may hold values from -6 to 6
- cache_rope: bfloat16 [32, 64, 64], P(('fsdp', 'ep')), may hold values from -6 to 6
- new_latent: bfloat16 [32, 64, 512], P(('fsdp', 'ep')), may hold values from -6 to 6
- new_rope: bfloat16 [32, 64, 64], P(('fsdp', 'ep')), may hold values from -6 to 6
- w_uv: bfloat16 [512, 8, 128], P('fsdp'), may hold values from -0.25 to 0.25
- w_out: bfloat16 [1024, 2048], P('fsdp'), may hold values from -0.1875 to 0.1875
- norm_gain: float32 [2048], replicated, may hold values from 0.5 to 2
- router: bfloat16 [2048, 16], replicated, may hold values from -0.026516504 to 0.026516504
- expert_ids: int32 [32, 64, 6], P(('fsdp', 'ep')), may hold values from 0 to 15, all different within a row; in each aligned block of 64 rows (0 to 63, 64 to 127, ..., all dimensions but the last counted through in order) at most 24 rows name the same one
- w_gate: bfloat16 [16, 2048, 704], P('ep'), may hold values from -0.125 to 0.125
- w_up: bfloat16 [16, 2048, 704], P('ep'), may hold values from -0.125 to 0.125
- w_down: bfloat16 [16, 704, 2048], P('ep'), may hold values from -0.21875 to 0.21875
Outputs:
- attended: bfloat16 [32, 64, 2048], P(('fsdp', 'ep'))
- layer_out: bfloat16 [32, 64, 2048], P(('fsdp', 'ep'))
Inputs may be any that keep to these rules, and one draw needn't show every extreme that they name: `expert_ids`: within the 64 tokens of one sequence every expert is named exactly 24 times.
All inputs are finite; a program needn't handle non-finite values.
Results may differ from a plain program's by a relative error of at most 0.008.
Values may be sent and summed in bfloat16 or wider, within the bound.
No kernel may reach another device: no remote copies, remote signals or barrier semaphores. Data moves between devices by JAX's collectives and lax.ppermute only.
A program may use at most 64 MiB of HBM per device.

v0:
```python
import functools

import jax
import jax.numpy as jnp
from jax import lax
from jax.experimental import pallas as pl
from jax.experimental.pallas import tpu as pltpu
from jax.sharding import PartitionSpec as P


softmax_scale = 0.07216878364870323
epsilon = 1e-06


def attend_local(q_latent, q_rope, cache_latent, cache_rope, new_latent, new_rope):
    new_count, head_count, latent_width = q_latent.shape
    cache_count = cache_latent.shape[0]
    keys_latent = jnp.concatenate([cache_latent, new_latent], 0)
    keys_rope = jnp.concatenate([cache_rope, new_rope], 0)
    query_rows = q_latent.reshape(new_count * head_count, latent_width)
    rope_rows = q_rope.reshape(new_count * head_count, q_rope.shape[2])
    scores = jnp.dot(query_rows, keys_latent.T, preferred_element_type=jnp.float32)
    scores = (
        scores + jnp.dot(rope_rows, keys_rope.T, preferred_element_type=jnp.float32)
    ) * softmax_scale
    token_of_row = jnp.arange(new_count * head_count, dtype=jnp.int32) // head_count
    key_index = jnp.arange(keys_latent.shape[0], dtype=jnp.int32)
    visible = key_index[None, :] <= token_of_row[:, None] + cache_count
    row_top = jnp.max(jnp.where(visible, scores, -jnp.inf), axis=1, keepdims=True)
    exponent = jnp.where(visible, jnp.exp(scores - row_top), 0.0)
    weights_att = (exponent / jnp.sum(exponent, axis=1, keepdims=True)).astype(jnp.bfloat16)
    mixed_latent = jnp.dot(weights_att, keys_latent, preferred_element_type=jnp.float32).astype(
        jnp.bfloat16
    )
    return mixed_latent.reshape(new_count, head_count, latent_width)


def up_project(mixed_latent, w_uv):
    heads_out = jnp.einsum(
        "thl,lhv->thv", mixed_latent, w_uv, preferred_element_type=jnp.float32
    )
    return heads_out.astype(jnp.bfloat16).reshape(mixed_latent.shape[0], -1)


def project_gathered(mixed_latent, w_uv, w_out):
    heads_flat = up_project(mixed_latent, lax.all_gather(w_uv, "fsdp", axis=0, tiled=True))
    column_width = w_out.shape[1] // lax.axis_size("ep")
    own_columns = lax.dynamic_slice_in_dim(
        w_out, lax.axis_index("ep") * column_width, column_width, 1
    )
    column_block = lax.all_gather(own_columns, "fsdp", axis=0, tiled=True)
    return jnp.dot(
        heads_flat,
        lax.all_gather(column_block, "ep", axis=1, tiled=True),
        preferred_element_type=jnp.float32,
    )


def project_paired(mixed_latent, w_uv, w_out):
    pair = [(0, 1), (1, 0)]
    ep = lax.axis_size("ep")
    twins = [(i, i ^ 1) for i in range(ep)]
    side = lax.axis_index("fsdp")
    lane = lax.axis_index("ep") % 2
    rows = w_uv.shape[0] // 2
    mine = lax.ppermute(
        lax.dynamic_slice_in_dim(w_uv, lane * rows, rows, 0), "fsdp", pair
    )
    theirs = lax.ppermute(mine, "ep", twins)
    far = jnp.where(
        lane == 0, jnp.concatenate([mine, theirs], 0), jnp.concatenate([theirs, mine], 0)
    )
    full = jnp.where(side == 0, jnp.concatenate([w_uv, far], 0), jnp.concatenate([far, w_uv], 0))
    heads_flat = up_project(mixed_latent, full)
    width = w_out.shape[0]
    count = heads_flat.shape[0]
    keep = lax.dynamic_slice_in_dim(heads_flat, side * width, width, 1)
    give = lax.dynamic_slice_in_dim(heads_flat, (1 - side) * width, width, 1)
    other = lax.ppermute(give, "fsdp", pair)
    both = jnp.dot(
        jnp.concatenate([other, keep], 0), w_out, preferred_element_type=jnp.float32
    )
    back = lax.ppermute(both[:count].astype(jnp.bfloat16), "fsdp", pair)
    return both, back


def experts(rows, w_gate, w_up, w_down):
    gate_proj = jnp.dot(rows, w_gate, preferred_element_type=jnp.float32)
    up_proj = jnp.dot(rows, w_up, preferred_element_type=jnp.float32)
    activated = (jax.nn.silu(gate_proj) * up_proj).astype(jnp.bfloat16)
    return jnp.dot(activated, w_down, preferred_element_type=jnp.float32).astype(jnp.bfloat16)


def slots_of(own_ids, expert_count, capacity):
    choose = (own_ids[..., None] == jnp.arange(expert_count, dtype=jnp.int32)).astype(jnp.float32)
    assigned = choose.reshape(-1, expert_count)
    earlier = jnp.cumsum(assigned, axis=0) - assigned
    slot_index = jnp.sum(earlier * assigned, axis=-1).reshape(own_ids.shape).astype(jnp.int32)
    return own_ids * capacity + slot_index


def gates_of(normed, router, ids):
    logits = jnp.dot(normed, router, preferred_element_type=jnp.float32)
    choose = ids[..., None] == jnp.arange(router.shape[1], dtype=jnp.int32)
    picked = jnp.sum(jnp.where(choose, logits[:, None, :], 0.0), axis=-1)
    return jax.nn.softmax(picked, axis=-1)


def weighted_rows(weights, rows):
    high = weights.astype(jnp.bfloat16)
    low = (weights - high.astype(jnp.float32)).astype(jnp.bfloat16)
    return jnp.dot(
        jnp.concatenate([high, low], 1),
        jnp.concatenate([rows, rows], 0),
        preferred_element_type=jnp.float32,
    )


def routed_exchanged(normed, target, capacity, router, w_gate, w_up, w_down):
    expert_count = lax.axis_size("ep")
    gate_weights = gates_of(normed, router, target // capacity)
    here = target[..., None] == jnp.arange(expert_count * capacity, dtype=jnp.int32)
    placed = jnp.sum(here.astype(jnp.bfloat16), axis=1)
    combine = jnp.sum(jnp.where(here, gate_weights[..., None], 0.0), axis=1)
    buffers = jnp.einsum("tp,td->pd", placed, normed, preferred_element_type=jnp.float32).astype(
        jnp.bfloat16
    )
    buffers = buffers.reshape(expert_count, capacity, -1)
    received = lax.all_to_all(buffers, "ep", split_axis=0, concat_axis=0, tiled=True)
    result = experts(received.reshape(expert_count * capacity, -1), w_gate, w_up, w_down)
    result = result.reshape(expert_count, capacity, -1)
    returned = lax.all_to_all(result, "ep", split_axis=0, concat_axis=0, tiled=True)
    return weighted_rows(combine, returned.reshape(expert_count * capacity, -1))


def fused(body, outs, *args, vmem=8, flops=0, bytes_accessed=0):
    whole = pl.BlockSpec(memory_space=pltpu.VMEM)
    return pl.pallas_call(
        body,
        out_shape=[jax.ShapeDtypeStruct(shape, dtype) for shape, dtype in outs],
        in_specs=[whole] * len(args),
        out_specs=[whole] * len(outs),
        cost_estimate=pl.CostEstimate(
            flops=flops, bytes_accessed=bytes_accessed, transcendentals=0
        ),
        compiler_params=pltpu.CompilerParams(vmem_limit_bytes=vmem << 20),
    )(*args)


def slot_kernel(expert_count, capacity, *refs):
    sources = len(refs) // 2
    for ids_ref, target_ref in zip(refs[:sources], refs[sources:]):
        ids = ids_ref[...]
        top, count = ids.shape
        level = lax.broadcasted_iota(jnp.int32, (expert_count, count), 0)
        chosen = jnp.zeros((expert_count, count), jnp.float32)
        for k in range(top):
            chosen += (ids[k : k + 1] == level).astype(jnp.float32)
        rows = lax.broadcasted_iota(jnp.int32, (count, count), 0)
        columns = lax.broadcasted_iota(jnp.int32, (count, count), 1)
        ahead = (rows < columns).astype(jnp.float32).astype(jnp.bfloat16)
        earlier = jnp.dot(
            chosen.astype(jnp.bfloat16), ahead, preferred_element_type=jnp.float32
        )
        for k in range(top):
            own = ids[k : k + 1]
            slot = jnp.sum(jnp.where(own == level, earlier, 0.0), axis=0, keepdims=True)
            target_ref[k : k + 1] = own * capacity + slot.astype(jnp.int32)


def matches(target, capacity, place):
    top, count = target.shape
    row = lax.broadcasted_iota(jnp.int32, (4 * capacity, count), 0)
    slot = jnp.zeros_like(row)
    for j in range(4):
        inside = (row >= j * capacity) & (row < (j + 1) * capacity)
        slot = jnp.where(inside, (place ^ j) * capacity + row - j * capacity, slot)
    found = jnp.zeros(row.shape, jnp.float32)
    for k in range(top):
        found += (target[k : k + 1] == slot).astype(jnp.float32)
    return found


def pick_kernel(capacity, sources, *refs):
    place = lax.axis_index("ep")
    position = 0
    out = refs[-4:]
    for n, pieces in enumerate(sources):
        found = matches(refs[position][...], capacity, place).astype(jnp.bfloat16)
        offset = 0
        for ref in refs[position + 1 : position + 1 + pieces]:
            rows = jnp.dot(found, ref[...], preferred_element_type=jnp.float32)
            rows = rows.astype(jnp.bfloat16)
            columns = slice(offset, offset + ref.shape[1])
            offset += ref.shape[1]
            for j in range(4):
                out[j][n * capacity : (n + 1) * capacity, columns] = rows[
                    j * capacity : (j + 1) * capacity
                ]
        position += 1 + pieces


def dot_rows(a, b):
    return lax.dot_general(a, b, (((1,), (1,)), ((), ())), preferred_element_type=jnp.float32)


def gate_kernel(capacity, router_ref, *refs):
    place = lax.axis_index("ep")
    expert_count = router_ref.shape[0]
    out = refs[12:]
    half = refs[1].shape[1]
    for n in range(4):
        target_ref, low_ref, high_ref = refs[3 * n : 3 * n + 3]
        target = target_ref[...]
        top, count = target.shape
        logits = dot_rows(router_ref[:, :half], low_ref[...])
        logits += dot_rows(router_ref[:, half:], high_ref[...])
        level = lax.broadcasted_iota(jnp.int32, (expert_count, count), 0)
        first = level * capacity
        chosen = jnp.zeros((expert_count, count), jnp.float32)
        for k in range(top):
            own = target[k : k + 1]
            chosen += ((own >= first) & (own < first + capacity)).astype(jnp.float32)
        inside = chosen > 0
        peak = jnp.max(jnp.where(inside, logits, -jnp.inf), axis=0, keepdims=True)
        power = jnp.where(inside, jnp.exp(logits - peak), 0.0)
        gate = power / jnp.sum(power, axis=0, keepdims=True)
        found = matches(target, capacity, place)
        row = lax.broadcasted_iota(jnp.int32, found.shape, 0)
        for j in range(4):
            own = jnp.sum(jnp.where(level == (place ^ j), gate, 0.0), axis=0, keepdims=True)
            within = (row >= j * capacity) & (row < (j + 1) * capacity)
            found = jnp.where(within, found * own, found)
        out[n][...] = found.T


def norm_kernel(x_ref, both_ref, back_ref, gain_ref, hidden_ref, attended_ref, low_ref, high_ref):
    count, width = hidden_ref.shape
    hidden = x_ref[0].astype(jnp.float32) + (
        both_ref[count:] + back_ref[...].astype(jnp.float32)
    )
    hidden_ref[...] = hidden
    attended_ref[0] = hidden.astype(jnp.bfloat16)
    square = jnp.mean(hidden * hidden, axis=-1, keepdims=True)
    normed = hidden * lax.rsqrt(square + epsilon) * gain_ref[...]
    low_ref[...] = normed[:, : width // 2].astype(jnp.bfloat16)
    high_ref[...] = normed[:, width // 2 :].astype(jnp.bfloat16)


def hidden_units(rows, gate_ref, up_ref):
    active = []
    for start in range(0, gate_ref.shape[0], 256):
        part = slice(start, min(start + 256, gate_ref.shape[0]))
        gate = dot_rows(rows, gate_ref[part])
        up = dot_rows(rows, up_ref[part])
        active.append((gate / (1.0 + jnp.exp(-gate)) * up).astype(jnp.bfloat16))
    return jnp.concatenate(active, 1)


def near_expert_kernel(capacity, *refs):
    first, second, own = refs[0:4], refs[4:8], refs[8:12]
    gate_ref, up_ref, down_ref = refs[12:15]
    out_first, out_second, out_own = refs[15:19], refs[19:23], refs[23:27]
    rows = [
        jnp.concatenate([a[:capacity], b[:capacity]], 1) for a, b in zip(first, second)
    ]
    rows += [
        jnp.concatenate([b[capacity:], a[capacity:]], 1) for a, b in zip(first, second)
    ]
    rows += [ref[...] for ref in own]
    active = hidden_units(jnp.concatenate(rows, 0), gate_ref, up_ref)
    width = down_ref.shape[1]
    step = width // 4
    for start in range(0, width, step):
        result = jnp.dot(
            active, down_ref[:, start : start + step], preferred_element_type=jnp.float32
        ).astype(jnp.bfloat16)
        low = start < width // 2
        columns = slice(start % (width // 2), start % (width // 2) + step)
        for j in range(4):
            blocks = [
                result[(4 * n + j) * capacity : (4 * n + j + 1) * capacity] for n in range(3)
            ]
            before_out, after_out = (out_first, out_second) if low else (out_second, out_first)
            before_out[j][:capacity, columns] = blocks[0]
            after_out[j][capacity:, columns] = blocks[1]
            out_own[j][:, start : start + step] = blocks[2]


def far_expert_kernel(*refs):
    gate_ref, up_ref, down_ref = refs[4:7]
    rows = jnp.concatenate([ref[...] for ref in refs[:4]], 0)
    active = hidden_units(rows, gate_ref, up_ref)
    capacity = refs[0].shape[0]
    for start in range(0, down_ref.shape[1], 512):
        part = slice(start, start + 512)
        result = jnp.dot(active, down_ref[:, part], preferred_element_type=jnp.float32)
        result = result.astype(jnp.bfloat16)
        for j in range(4):
            refs[7 + j][:, part] = result[j * capacity : (j + 1) * capacity]


def weigh(weights, rows):
    high = weights.astype(jnp.bfloat16)
    low = (weights - high.astype(jnp.float32)).astype(jnp.bfloat16)
    return jnp.dot(high, rows, preferred_element_type=jnp.float32) + jnp.dot(
        low, rows, preferred_element_type=jnp.float32
    )


def far_kernel(weights_ref, r0, r1, r2, r3, low_ref, high_ref):
    rows = jnp.concatenate([r[...] for r in (r0, r1, r2, r3)], 0)
    total = weigh(weights_ref[...], rows)
    half = low_ref.shape[1]
    low_ref[...] = total[:, :half].astype(jnp.bfloat16)
    high_ref[...] = total[:, half:].astype(jnp.bfloat16)


def near_kernel(capacity, before_w, after_w, r0, r1, r2, r3, *refs):
    blocks = (r0, r1, r2, r3)
    adds = refs[:-2]
    for n, weights in enumerate((before_w, after_w)):
        rows = jnp.concatenate([r[n * capacity : (n + 1) * capacity] for r in blocks], 0)
        total = weigh(weights[...], rows)
        if adds:
            total += adds[n][...].astype(jnp.float32)
        refs[len(adds) + n][...] = total.astype(jnp.bfloat16)


def last_kernel(hidden_ref, weights_ref, r0, r1, r2, r3, x_low, x_high, y_low, y_high, out_ref):
    rows = jnp.concatenate([r[...] for r in (r0, r1, r2, r3)], 0)
    total = hidden_ref[...] + weigh(weights_ref[...], rows)
    half = x_low.shape[1]
    low = x_low[...].astype(jnp.float32) + y_low[...].astype(jnp.float32)
    high = x_high[...].astype(jnp.float32) + y_high[...].astype(jnp.float32)
    out_ref[:, :half] = (total[:, :half] + low).astype(jnp.bfloat16)
    out_ref[:, half:] = (total[:, half:] + high).astype(jnp.bfloat16)


def routed_ringed(hidden, low, high, targets, capacity, router, w_gate, w_up, w_down):
    onward, backward = ring_steps()
    traded = [[(i, i ^ j) for i in range(16)] for j in range(4)]
    count, half = low.shape
    width = 2 * half
    bf16 = jnp.bfloat16

    def send(value, steps):
        return lax.ppermute(value, "ep", steps)

    def pick(*sources):
        n = len(sources)
        columns = sum(part.shape[1] for part in sources[0][1:])
        return fused(
            functools.partial(pick_kernel, capacity, [len(source) - 1 for source in sources]),
            [((n * capacity, columns), bf16)] * 4,
            *[part for source in sources for part in source],
            flops=n * 2 * 4 * capacity * count * columns,
            bytes_accessed=n * 4 * columns * (count + 4 * capacity),
        )

    def trade(blocks):
        return [blocks[0]] + [send(blocks[j], traded[j]) for j in (1, 2, 3)]

    own_slots, before_slots, after_slots, far_slots = targets
    before_low, after_high = send(low, onward), send(high, backward)
    before_high, after_low = send(high, onward), send(low, backward)
    own_rows = trade(pick((own_slots, low, high)))
    far_low, far_high = send(before_low, onward), send(after_high, backward)
    first_rows = trade(pick((before_slots, before_low), (after_slots, after_high)))
    before_high, after_low, own_rows, first_rows[0] = lax.optimization_barrier(
        (before_high, after_low, own_rows, first_rows[0])
    )
    second_rows = trade(pick((before_slots, before_high), (after_slots, after_low)))
    far_rows = trade(pick((far_slots, far_low, far_high)))
    expert_weights = (jnp.swapaxes(w_gate[0], 0, 1), jnp.swapaxes(w_up[0], 0, 1), w_down[0])
    hidden_width = w_gate.shape[2]
    unit = width * hidden_width
    far_rows[0], far_low, far_high = lax.optimization_barrier((far_rows[0], far_low, far_high))
    slots = (count, 4 * capacity)
    weights = fused(
        functools.partial(gate_kernel, capacity),
        [(slots, jnp.float32)] * 4,
        router.T,
        *(own_slots, low, high),
        *(before_slots, before_low, before_high),
        *(after_slots, after_low, after_high),
        *(far_slots, far_low, far_high),
        flops=8 * count * width * 16,
        bytes_accessed=16 * count * width,
    )
    own_rows, weights = lax.optimization_barrier((own_rows, weights))
    blocks = first_rows + second_rows + own_rows
    near = fused(
        functools.partial(near_expert_kernel, capacity),
        [(b.shape, bf16) for b in blocks],
        *blocks,
        *expert_weights,
        vmem=16,
        flops=6 * 12 * capacity * unit,
        bytes_accessed=6 * unit + 4 * 12 * capacity * width,
    )
    near, far_rows = lax.optimization_barrier((near, far_rows))
    result = fused(
        far_expert_kernel,
        [(b.shape, bf16) for b in far_rows],
        *far_rows,
        *expert_weights,
        vmem=16,
        flops=6 * 4 * capacity * unit,
        bytes_accessed=6 * unit + 4 * 4 * capacity * width,
    )
    spent = 2 * 4 * 4 * capacity * count * width
    moved = 4 * width * (count + 4 * capacity)
    piece = ((count, half), bf16)
    far_low, far_high = fused(
        far_kernel,
        [piece] * 2,
        weights[3],
        *trade(result),
        flops=spent,
        bytes_accessed=moved,
    )
    add_low, add_high = send(far_low, onward), send(far_high, backward)

    def near_sums(rows, *adds):
        return fused(
            functools.partial(near_kernel, capacity),
            [piece] * 2,
            weights[1],
            weights[2],
            *trade(rows),
            *adds,
            flops=spent,
            bytes_accessed=moved,
        )

    before_sum, after_sum = near_sums(near[0:4])
    from_after_low = send(before_sum, backward)
    from_before_high = send(after_sum, onward)
    before_sum, after_sum = near_sums(near[4:8], add_high, add_low)
    from_after_high = send(before_sum, backward)
    from_before_low = send(after_sum, onward)
    return fused(
        last_kernel,
        [((count, width), bf16)],
        hidden,
        weights[0],
        *trade(near[8:12]),
        from_before_low,
        from_before_high,
        from_after_low,
        from_after_high,
        flops=spent,
        bytes_accessed=2 * moved,
    )[0]


def ring_steps():
    order = (0, 1, 3, 2)
    onward = [
        (order[i] * 4 + j, order[(i + 1) % 4] * 4 + j) for i in range(4) for j in range(4)
    ]
    return onward, [(b, a) for a, b in onward]


def per_device(
    x_resid,
    q_latent,
    q_rope,
    cache_latent,
    cache_rope,
    new_latent,
    new_rope,
    w_uv,
    w_out,
    norm_gain,
    router,
    expert_ids,
    w_gate,
    w_up,
    w_down,
):
    mixed_latent = attend_local(
        q_latent[0], q_rope[0], cache_latent[0], cache_rope[0], new_latent[0], new_rope[0]
    )
    new_count = mixed_latent.shape[0]
    expert_count = lax.axis_size("ep")
    capacity = new_count * expert_ids.shape[2] // expert_count
    if lax.axis_size("fsdp") != 2 or expert_count != 16:
        projected = project_gathered(mixed_latent, w_uv, w_out)
        hidden = x_resid[0].astype(jnp.float32) + projected
        normed = hidden * lax.rsqrt(jnp.mean(hidden * hidden, axis=-1, keepdims=True) + epsilon)
        normed = (normed * norm_gain).astype(jnp.bfloat16)
        target = slots_of(expert_ids[0], expert_count, capacity)
        routed_sum = routed_exchanged(
            normed, target, capacity, router, w_gate[0], w_up[0], w_down[0]
        )
        layer_out = (hidden + routed_sum).astype(jnp.bfloat16)
        return (hidden.astype(jnp.bfloat16)[None], layer_out[None])
    onward, backward = ring_steps()
    ids = [expert_ids[0].T]
    across = [(i, i ^ 12) for i in range(16)]
    ids += [lax.ppermute(ids[0], "ep", steps) for steps in (onward, backward, across)]
    targets = fused(
        functools.partial(slot_kernel, expert_count, capacity),
        [(part.shape, jnp.int32) for part in ids],
        *ids,
    )
    both, back = project_paired(mixed_latent, w_uv, w_out)
    back, targets = lax.optimization_barrier((back, targets))
    width = both.shape[1]
    halves = (new_count, width // 2)
    hidden, attended, low, high = fused(
        norm_kernel,
        [
            ((new_count, width), jnp.float32),
            ((1, new_count, width), jnp.bfloat16),
            (halves, jnp.bfloat16),
            (halves, jnp.bfloat16),
        ],
        x_resid,
        both,
        back,
        norm_gain[None],
        flops=8 * new_count * width,
        bytes_accessed=20 * new_count * width,
    )
    layer_out = routed_ringed(
        hidden, low, high, targets, capacity, router, w_gate, w_up, w_down
    )
    return (attended, layer_out[None])


def solution(mesh):
    placed = (
        P(("fsdp", "ep"), None, None),
        P(("fsdp", "ep"), None, None, None),
        P(("fsdp", "ep"), None, None, None),
        P(("fsdp", "ep"), None, None),
        P(("fsdp", "ep"), None, None),
        P(("fsdp", "ep"), None, None),
        P(("fsdp", "ep"), None, None),
        P("fsdp", None, None),
        P("fsdp", None),
        P(),
        P(),
        P(("fsdp", "ep"), None, None),
        P("ep", None, None),
        P("ep", None, None),
        P("ep", None, None),
    )

    return jax.shard_map(
        per_device,
        mesh=mesh,
        in_specs=placed,
        out_specs=(P(("fsdp", "ep"), None, None), P(("fsdp", "ep"), None, None)),
        check_vma=False,
    )
```

profile of v0, /device:TPU:0, one launch (start us, length us, event | category | flops | bytes accessed | tf_op | source)
XLA Modules:
  0.0 92.8 jit_solution(13700754187785031376)
XLA Ops:
  0.7 1.1 %constant_dynamic-slice_fusion.2 = bf16[128,8,128]{2,1,0:T(8,128)(2,1)S(1)} fusion(bf16[256,8,128]{2,1,0:T(8,128)(2,1)} %param.22, s32[]{:T(128)S(6)} %select_n.53), kind=kLoop, calls=%fused_computation.44 | loop fusion | bytes 524292 | tf_op jit(solution)/shard_map/dynamic_slice | solution.py:67
  1.8 3.0 %collective-permute-start = (bf16[128,8,128]{2,1,0:T(8,128)(2,1)S(1)}, bf16[128,8,128]{2,1,0:T(8,128)(2,1)S(1)}, u32[]{:S(2)}, u32[]{:S(2)}) collective-permute-start(bf16[128,8,128]{2,1,0:T(8,128)(2,1)S(1)} %constant_dynamic-slice_fusion.2), channel_id=1, source_target_pairs={{0,16},{16,0},{1,17},{17,1},{2,18},{18,2},{3,19},{19,3},{4,20},{20... | collective-permute-start | bytes 786440 | tf_op jit(solution)/shard_map/ppermute | solution.py:66
  4.8 1.5 %fusion.5 = f32[128,512]{1,0:T(8,128)S(1)} fusion(bf16[1,64,8,512]{3,2,1,0:T(8,128)(2,1)} %param.16, bf16[64,512]{1,0:T(8,128)(2,1)} %bitcast.52, bf16[64,512]{1,0:T(8,128)(2,1)} %bitcast.54), kind=kOutput, calls=%fused_computation.11 | convolution fusion | flops 67371008 | bytes 917504 | tf_op jit(solution)/shard_map/dot_general | solution.py:22
  6.3 1.2 %select_reduce_fusion = (f32[512]{0:T(512)S(1)}, f32[512,128]{0,1:T(8,128)S(1)}) fusion(s32[512]{0:T(512)S(1)} %fusion.21, f32[128,512]{1,0:T(8,128)S(1)} %fusion.5, bf16[1,64,8,64]{3,2,1,0:T(8,128)(2,1)} %param.17, bf16[64,64]{1,0:T(8,128)(2,1)} %bitcast.56, bf16[64,64]{1,0:T(8,128)(2,1)} %bitcast.57), kind=kOutput, calls=%fused_computation.16 | convolution fusion | flops 8748544 | bytes 610304 | tf_op jit(solution)/shard_map/dot_general | solution.py:24
  7.5 3.6 %collective-permute-done = bf16[128,8,128]{2,1,0:T(8,128)(2,1)S(1)} collective-permute-done((bf16[128,8,128]{2,1,0:T(8,128)(2,1)S(1)}, bf16[128,8,128]{2,1,0:T(8,128)(2,1)S(1)}, u32[]{:S(2)}, u32[]{:S(2)}) %collective-permute-start) | collective-permute-done | bytes 262176 | tf_op jit(solution)/shard_map/ppermute | solution.py:66
  11.2 0.3 fusion
  11.6 1.1 %collective-permute-done.1 = bf16[128,8,128]{2,1,0:T(8,128)(2,1)S(1)} collective-permute-done((bf16[128,8,128]{2,1,0:T(8,128)(2,1)S(1)}, bf16[128,8,128]{2,1,0:T(8,128)(2,1)S(1)}, u32[]{:S(2)}, u32[]{:S(2)}) %collective-permute-start.1) | collective-permute-done | bytes 262176 | tf_op jit(solution)/shard_map/ppermute | solution.py:69
  13.0 0.5 fusion.3
  13.5 1.8 %collective-permute-start.2 = (bf16[64,512]{1,0:T(8,128)(2,1)S(1)}, bf16[64,512]{1,0:T(8,128)(2,1)S(1)}, u32[]{:S(2)}, u32[]{:S(2)}) collective-permute-start(bf16[64,512]{1,0:T(8,128)(2,1)S(1)} %get-tuple-element.180), channel_id=1, source_target_pairs={{0,16},{16,0},{1,17},{17,1},{2,18},{18,2},{3,19},{19,3},{4,20},{20... | collective-permute-start | bytes 196616 | tf_op jit(solution)/shard_map/ppermute | solution.py:79
  15.3 2.5 %collective-permute-done.2 = bf16[64,512]{1,0:T(8,128)(2,1)S(1)} collective-permute-done((bf16[64,512]{1,0:T(8,128)(2,1)S(1)}, bf16[64,512]{1,0:T(8,128)(2,1)S(1)}, u32[]{:S(2)}, u32[]{:S(2)}) %collective-permute-start.2) | collective-permute-done | bytes 65568 | tf_op jit(solution)/shard_map/ppermute | solution.py:79
  17.9 0.4 fusion.9.both_ref
  18.4 1.8 %collective-permute-start.3 = (bf16[64,2048]{1,0:T(8,128)(2,1)S(1)}, bf16[64,2048]{1,0:T(8,128)(2,1)S(1)}, u32[]{:S(2)}, u32[]{:S(2)}) collective-permute-start(bf16[64,2048]{1,0:T(8,128)(2,1)S(1)} %slice.7), channel_id=1, source_target_pairs={{0,16},{16,0},{1,17},{17,1},{2,18},{18,2},{3,19},{19,3},{4,20},{20... | collective-permute-start | bytes 786440 | tf_op jit(solution)/shard_map/ppermute | solution.py:83
  20.2 3.6 %collective-permute-start.6 = (s32[6,64]{1,0:T(8,128)S(1)}, s32[6,64]{1,0:T(8,128)S(1)}, u32[]{:S(2)}, u32[]{:S(2)}) collective-permute-start(s32[6,64]{1,0:T(8,128)S(1)} %bitcast.45), channel_id=1, source_target_pairs={{0,12},{1,13},{2,14},{3,15},{4,8},{5,9},{6,10},{7,11},{8,4},{9,5},... | collective-permute-start | bytes 4616 | tf_op jit(solution)/shard_map/ppermute | solution.py:503
  23.8 2.0 %collective-permute-start.4 = (s32[6,64]{1,0:T(8,128)S(1)}, s32[6,64]{1,0:T(8,128)S(1)}, u32[]{:S(2)}, u32[]{:S(2)}) collective-permute-start(s32[6,64]{1,0:T(8,128)S(1)} %bitcast.47), channel_id=1, source_target_pairs={{0,4},{1,5},{2,6},{3,7},{4,12},{5,13},{6,14},{7,15},{12,8},{13,9},... | collective-permute-start | bytes 4616 | tf_op jit(solution)/shard_map/ppermute | solution.py:503
  25.8 1.6 %collective-permute-done.5.refs_2_ = s32[6,64]{1,0:T(8,128)S(1)} collective-permute-done((s32[6,64]{1,0:T(8,128)S(1)}, s32[6,64]{1,0:T(8,128)S(1)}, u32[]{:S(2)}, u32[]{:S(2)}) %collective-permute-start.5) | collective-permute-done | bytes 1568 | tf_op jit(solution)/shard_map/ppermute | solution.py:503
  27.4 0.9 collective-permute-done.4.refs_1_
  28.5 0.9 shard_map.159
  29.4 2.0 %collective-permute-start.12 = (bf16[64,1024]{1,0:T(8,128)(2,1)S(1)}, bf16[64,1024]{1,0:T(8,128)(2,1)S(1)}, u32[]{:S(2)}, u32[]{:S(2)}) collective-permute-start(bf16[64,1024]{1,0:T(8,128)(2,1)S(1)} %get-tuple-element.99.refs_1_), channel_id=1, source_target_pairs={{0,4},{1,5},{2,6},{3,7},{4,12},{5,13},{6,14},{7,15},{12,8},{13,9},... | collective-permute-start | bytes 393224 | tf_op jit(solution)/shard_map/ppermute | solution.py:348
  31.7 1.6 %collective-permute-start.10 = (bf16[24,2048]{1,0:T(8,128)(2,1)S(1)}, bf16[24,2048]{1,0:T(8,128)(2,1)S(1)}, u32[]{:S(2)}, u32[]{:S(2)}) collective-permute-start(bf16[24,2048]{1,0:T(8,128)(2,1)S(1)} %get-tuple-element.103), channel_id=1, source_target_pairs={{0,2},{1,3},{2,0},{3,1},{4,6},{5,7},{6,4},{7,5},{8,10},{9,11},{10,... | collective-permute-start | bytes 294920 | tf_op jit(solution)/shard_map/ppermute | solution.py:348
  33.6 2.0 %collective-permute-start.7 = (bf16[64,1024]{1,0:T(8,128)(2,1)S(1)}, bf16[64,1024]{1,0:T(8,128)(2,1)S(1)}, u32[]{:S(2)}, u32[]{:S(2)}) collective-permute-start(bf16[64,1024]{1,0:T(8,128)(2,1)S(1)} %get-tuple-element.98.refs_2_), channel_id=1, source_target_pairs={{0,4},{1,5},{2,6},{3,7},{4,12},{5,13},{6,14},{7,15},{12,8},{13,9},... | collective-permute-start | bytes 393224 | tf_op jit(solution)/shard_map/ppermute | solution.py:348
  35.6 1.9 %collective-permute-done.10.refs_10_ = bf16[24,2048]{1,0:T(8,128)(2,1)S(1)} collective-permute-done((bf16[24,2048]{1,0:T(8,128)(2,1)S(1)}, bf16[24,2048]{1,0:T(8,128)(2,1)S(1)}, u32[]{:S(2)}, u32[]{:S(2)}) %collective-permute-start.10) | collective-permute-done | bytes 98336 | tf_op jit(solution)/shard_map/ppermute | solution.py:348
  37.5 0.9 %collective-permute-start.8 = (bf16[64,1024]{1,0:T(8,128)(2,1)S(1)}, bf16[64,1024]{1,0:T(8,128)(2,1)S(1)}, u32[]{:S(2)}, u32[]{:S(2)}) collective-permute-start(bf16[64,1024]{1,0:T(8,128)(2,1)S(1)} %get-tuple-element.99.refs_1_), channel_id=1, source_target_pairs={{4,0},{5,1},{6,2},{7,3},{12,4},{13,5},{14,6},{15,7},{8,12},{9,13},... | collective-permute-start | bytes 393224 | tf_op jit(solution)/shard_map/ppermute | solution.py:348
  38.4 1.5 %collective-permute-start.15 = (bf16[64,1024]{1,0:T(8,128)(2,1)S(1)}, bf16[64,1024]{1,0:T(8,128)(2,1)S(1)}, u32[]{:S(2)}, u32[]{:S(2)}) collective-permute-start(bf16[64,1024]{1,0:T(8,128)(2,1)S(1)} %collective-permute-done.13.refs_3_.refs_8_), channel_id=1, source_target_pairs={{4,0},{5,1},{6,2},{7,3},{12,4},{13,5},{14,6},{15,7},{8,12},{9,13},... | collective-permute-start | bytes 393224 | tf_op jit(solution)/shard_map/ppermute | solution.py:348
  40.0 0.5 collective-permute-start.14
  40.8 1.6 %collective-permute-start.17 = (bf16[48,1024]{1,0:T(8,128)(2,1)S(1)}, bf16[48,1024]{1,0:T(8,128)(2,1)S(1)}, u32[]{:S(2)}, u32[]{:S(2)}) collective-permute-start(bf16[48,1024]{1,0:T(8,128)(2,1)S(1)} %get-tuple-element.125), channel_id=1, source_target_pairs={{0,2},{1,3},{2,0},{3,1},{4,6},{5,7},{6,4},{7,5},{8,10},{9,11},{10,... | collective-permute-start | bytes 294920 | tf_op jit(solution)/shard_map/ppermute | solution.py:348
  42.4 1.5 %collective-permute-done.8.refs_7_.refs_3_ = bf16[64,1024]{1,0:T(8,128)(2,1)S(1)} collective-permute-done((bf16[64,1024]{1,0:T(8,128)(2,1)S(1)}, bf16[64,1024]{1,0:T(8,128)(2,1)S(1)}, u32[]{:S(2)}, u32[]{:S(2)}) %collective-permute-start.8) | collective-permute-done | bytes 131104 | tf_op jit(solution)/shard_map/ppermute | solution.py:348
  44.2 1.7 %collective-permute-start.19 = (bf16[48,1024]{1,0:T(8,128)(2,1)S(1)}, bf16[48,1024]{1,0:T(8,128)(2,1)S(1)}, u32[]{:S(2)}, u32[]{:S(2)}) collective-permute-start(bf16[48,1024]{1,0:T(8,128)(2,1)S(1)} %get-tuple-element.128), channel_id=1, source_target_pairs={{0,1},{1,0},{2,3},{3,2},{4,5},{5,4},{6,7},{7,6},{8,9},{9,8},{10,11... | collective-permute-start | bytes 294920 | tf_op jit(solution)/shard_map/ppermute | solution.py:348
  45.9 0.7 collective-permute-done.15.refs_2_.refs_11_
  46.6 1.5 %collective-permute-start.20 = (bf16[48,1024]{1,0:T(8,128)(2,1)S(1)}, bf16[48,1024]{1,0:T(8,128)(2,1)S(1)}, u32[]{:S(2)}, u32[]{:S(2)}) collective-permute-start(bf16[48,1024]{1,0:T(8,128)(2,1)S(1)} %get-tuple-element.129), channel_id=1, source_target_pairs={{0,2},{1,3},{2,0},{3,1},{4,6},{5,7},{6,4},{7,5},{8,10},{9,11},{10,... | collective-permute-start | bytes 294920 | tf_op jit(solution)/shard_map/ppermute | solution.py:348
  48.2 1.7 %collective-permute-done.14.refs_1_.refs_10_ = bf16[64,1024]{1,0:T(8,128)(2,1)S(1)} collective-permute-done((bf16[64,1024]{1,0:T(8,128)(2,1)S(1)}, bf16[64,1024]{1,0:T(8,128)(2,1)S(1)}, u32[]{:S(2)}, u32[]{:S(2)}) %collective-permute-start.14) | collective-permute-done | bytes 131104 | tf_op jit(solution)/shard_map/ppermute | solution.py:348
  49.9 1.1 %collective-permute-start.21 = (bf16[48,1024]{1,0:T(8,128)(2,1)S(1)}, bf16[48,1024]{1,0:T(8,128)(2,1)S(1)}, u32[]{:S(2)}, u32[]{:S(2)}) collective-permute-start(bf16[48,1024]{1,0:T(8,128)(2,1)S(1)} %get-tuple-element.130), channel_id=1, source_target_pairs={{0,3},{1,2},{2,1},{3,0},{4,7},{5,6},{6,5},{7,4},{8,11},{9,10},{10,... | collective-permute-start | bytes 294920 | tf_op jit(solution)/shard_map/ppermute | solution.py:348
  51.3 0.5 shard_map.163
  51.9 0.6 collective-permute-start.22
  52.4 0.5 collective-permute-start.23
  52.9 0.9 collective-permute-start.24
  53.9 0.9 %collective-permute-done.21.refs_7_ = bf16[48,1024]{1,0:T(8,128)(2,1)S(1)} collective-permute-done((bf16[48,1024]{1,0:T(8,128)(2,1)S(1)}, bf16[48,1024]{1,0:T(8,128)(2,1)S(1)}, u32[]{:S(2)}, u32[]{:S(2)}) %collective-permute-start.21) | collective-permute-done | bytes 98336 | tf_op jit(solution)/shard_map/ppermute | solution.py:348
  54.8 3.0 %shard_map.165 = (bf16[48,1024]{1,0:T(8,128)(2,1)S(1)}, bf16[48,1024]{1,0:T(8,128)(2,1)S(1)}, bf16[48,1024]{1,0:T(8,128)(2,1)S(1)}, bf16[48,1024]{1,0:T(8,128)(2...) custom-call(bf16[48,1024]{1,0:T(8,128)(2,1)S(1)} %get-tuple-element., ...), custom_call_target="tpu_custom_call" | custom-call | flops 2491416576 | bytes 11010048 | tf_op jit(solution)/shard_map/pallas_call | solution.py:138
  57.8 0.3 collective-permute-done.23.refs_2_
  58.1 0.3 collective-permute-done.24.refs_3_
  58.4 2.4 %shard_map.166 = (bf16[24,2048]{1,0:T(8,128)(2,1)S(1)}, bf16[24,2048]{1,0:T(8,128)(2,1)S(1)}, bf16[24,2048]{1,0:T(8,128)(2,1)S(1)}, bf16[24,2048]{1,0:T(8,128)(2,1)S(1)}) custom-call(bf16[24,2048]{1,0:T(8,128)(2,1)S(1)} %get-tuple-element.162.refs_0_, bf16[24,2048]{1,0:T(8,128)(2,1)S(1)} %collective-permute-done.22.refs_1_, ...), custom_call_target="tpu_custom_call" | custom-call | flops 830472192 | bytes 9437184 | tf_op jit(solution)/shard_map/pallas_call | solution.py:138
  60.8 0.8 collective-permute-start.31
  61.6 1.5 %collective-permute-start.32 = (bf16[24,2048]{1,0:T(8,128)(2,1)S(1)}, bf16[24,2048]{1,0:T(8,128)(2,1)S(1)}, u32[]{:S(2)}, u32[]{:S(2)}) collective-permute-start(bf16[24,2048]{1,0:T(8,128)(2,1)S(1)} %get-tuple-element.168), channel_id=1, source_target_pairs={{0,2},{1,3},{2,0},{3,1},{4,6},{5,7},{6,4},{7,5},{8,10},{9,11},{10,... | collective-permute-start | bytes 294920 | tf_op jit(solution)/shard_map/ppermute | solution.py:348
  63.1 0.6 collective-permute-start.28
  63.7 1.5 %collective-permute-start.29 = (bf16[48,1024]{1,0:T(8,128)(2,1)S(1)}, bf16[48,1024]{1,0:T(8,128)(2,1)S(1)}, u32[]{:S(2)}, u32[]{:S(2)}) collective-permute-start(bf16[48,1024]{1,0:T(8,128)(2,1)S(1)} %get-tuple-element.159), channel_id=1, source_target_pairs={{0,2},{1,3},{2,0},{3,1},{4,6},{5,7},{6,4},{7,5},{8,10},{9,11},{10,... | collective-permute-start | bytes 294920 | tf_op jit(solution)/shard_map/ppermute | solution.py:348
  65.3 1.6 %collective-permute-done.32.r2 = bf16[24,2048]{1,0:T(8,128)(2,1)S(1)} collective-permute-done((bf16[24,2048]{1,0:T(8,128)(2,1)S(1)}, bf16[24,2048]{1,0:T(8,128)(2,1)S(1)}, u32[]{:S(2)}, u32[]{:S(2)}) %collective-permute-start.32) | collective-permute-done | bytes 98336 | tf_op jit(solution)/shard_map/ppermute | solution.py:348
  66.8 2.0 %collective-permute-start.38 = (bf16[48,1024]{1,0:T(8,128)(2,1)S(1)}, bf16[48,1024]{1,0:T(8,128)(2,1)S(1)}, u32[]{:S(2)}, u32[]{:S(2)}) collective-permute-start(bf16[48,1024]{1,0:T(8,128)(2,1)S(1)} %get-tuple-element.175), channel_id=1, source_target_pairs={{0,2},{1,3},{2,0},{3,1},{4,6},{5,7},{6,4},{7,5},{8,10},{9,11},{10,... | collective-permute-start | bytes 294920 | tf_op jit(solution)/shard_map/ppermute | solution.py:348
  68.8 1.5 %collective-permute-start.39 = (bf16[48,1024]{1,0:T(8,128)(2,1)S(1)}, bf16[48,1024]{1,0:T(8,128)(2,1)S(1)}, u32[]{:S(2)}, u32[]{:S(2)}) collective-permute-start(bf16[48,1024]{1,0:T(8,128)(2,1)S(1)} %get-tuple-element.176), channel_id=1, source_target_pairs={{0,3},{1,2},{2,1},{3,0},{4,7},{5,6},{6,5},{7,4},{8,11},{9,10},{10,... | collective-permute-start | bytes 294920 | tf_op jit(solution)/shard_map/ppermute | solution.py:348
  70.3 0.3 shard_map.167
  71.0 1.6 %collective-permute-start.35 = (bf16[64,1024]{1,0:T(8,128)(2,1)S(1)}, bf16[64,1024]{1,0:T(8,128)(2,1)S(1)}, u32[]{:S(2)}, u32[]{:S(2)}) collective-permute-start(bf16[64,1024]{1,0:T(8,128)(2,1)S(1)} %get-tuple-element.171), channel_id=1, source_target_pairs={{0,4},{1,5},{2,6},{3,7},{4,12},{5,13},{6,14},{7,15},{12,8},{13,9},... | collective-permute-start | bytes 393224 | tf_op jit(solution)/shard_map/ppermute | solution.py:348
  72.7 0.5 collective-permute-done.38.r2
  73.1 0.7 collective-permute-start.25
  73.8 0.7 collective-permute-done.39.r3
  74.5 1.5 %collective-permute-start.26 = (bf16[24,2048]{1,0:T(8,128)(2,1)S(1)}, bf16[24,2048]{1,0:T(8,128)(2,1)S(1)}, u32[]{:S(2)}, u32[]{:S(2)}) collective-permute-start(bf16[24,2048]{1,0:T(8,128)(2,1)S(1)} %get-tuple-element.153), channel_id=1, source_target_pairs={{0,2},{1,3},{2,0},{3,1},{4,6},{5,7},{6,4},{7,5},{8,10},{9,11},{10,... | collective-permute-start | bytes 294920 | tf_op jit(solution)/shard_map/ppermute | solution.py:348
  76.1 0.3 shard_map.169
  76.3 1.0 %collective-permute-done.30.r3 = bf16[48,1024]{1,0:T(8,128)(2,1)S(1)} collective-permute-done((bf16[48,1024]{1,0:T(8,128)(2,1)S(1)}, bf16[48,1024]{1,0:T(8,128)(2,1)S(1)}, u32[]{:S(2)}, u32[]{:S(2)}) %collective-permute-start.30) | collective-permute-done | bytes 98336 | tf_op jit(solution)/shard_map/ppermute | solution.py:348
  77.4 1.5 %collective-permute-start.40 = (bf16[64,1024]{1,0:T(8,128)(2,1)S(1)}, bf16[64,1024]{1,0:T(8,128)(2,1)S(1)}, u32[]{:S(2)}, u32[]{:S(2)}) collective-permute-start(bf16[64,1024]{1,0:T(8,128)(2,1)S(1)} %get-tuple-element.177), channel_id=1, source_target_pairs={{0,4},{1,5},{2,6},{3,7},{4,12},{5,13},{6,14},{7,15},{12,8},{13,9},... | collective-permute-start | bytes 393224 | tf_op jit(solution)/shard_map/ppermute | solution.py:348
  78.9 1.4 %collective-permute-start.41 = (bf16[64,1024]{1,0:T(8,128)(2,1)S(1)}, bf16[64,1024]{1,0:T(8,128)(2,1)S(1)}, u32[]{:S(2)}, u32[]{:S(2)}) collective-permute-start(bf16[64,1024]{1,0:T(8,128)(2,1)S(1)} %get-tuple-element.178), channel_id=1, source_target_pairs={{4,0},{5,1},{6,2},{7,3},{12,4},{13,5},{14,6},{15,7},{8,12},{9,13},... | collective-permute-start | bytes 393224 | tf_op jit(solution)/shard_map/ppermute | solution.py:348
  80.3 0.3 shard_map.168
  80.6 0.7 collective-permute-start.36
  81.3 2.3 %collective-permute-start.42 = (bf16[64,1024]{1,0:T(8,128)(2,1)S(1)}, bf16[64,1024]{1,0:T(8,128)(2,1)S(1)}, u32[]{:S(2)}, u32[]{:S(2)}) collective-permute-start(bf16[64,1024]{1,0:T(8,128)(2,1)S(1)} %get-tuple-element.179), channel_id=1, source_target_pairs={{4,0},{5,1},{6,2},{7,3},{12,4},{13,5},{14,6},{15,7},{8,12},{9,13},... | collective-permute-start | bytes 393224 | tf_op jit(solution)/shard_map/ppermute | solution.py:348
  83.6 5.0 %collective-permute-done.27.r3 = bf16[24,2048]{1,0:T(8,128)(2,1)S(1)} collective-permute-done((bf16[24,2048]{1,0:T(8,128)(2,1)S(1)}, bf16[24,2048]{1,0:T(8,128)(2,1)S(1)}, u32[]{:S(2)}, u32[]{:S(2)}) %collective-permute-start.27) | collective-permute-done | bytes 98336 | tf_op jit(solution)/shard_map/ppermute | solution.py:348
  88.6 0.5 collective-permute-done.36.x_low
  89.1 2.7 %collective-permute-done.42.y_high = bf16[64,1024]{1,0:T(8,128)(2,1)S(1)} collective-permute-done((bf16[64,1024]{1,0:T(8,128)(2,1)S(1)}, bf16[64,1024]{1,0:T(8,128)(2,1)S(1)}, u32[]{:S(2)}, u32[]{:S(2)}) %collective-permute-start.42) | collective-permute-done | bytes 131104 | tf_op jit(solution)/shard_map/ppermute | solution.py:348
  91.8 1.0 %shard_map.170 = bf16[64,2048]{1,0:T(8,128)(2,1)} custom-call(f32[64,2048]{1,0:T(8,128)S(1)} %get-tuple-element.97.hidden_ref, f32[64,96]{1,0:T(8,128)S(1)} %get-tuple-element.122.weights_ref, bf16[24,2048]{1,0:T(8,128)(2,1)S(1)} %get-tuple-element.151.r0, bf16[24,2048]{1,0:T(8,128)(2,1)S(1)} %collective-permute-done.25.r1, ...), custom_call_target="tpu_custom_call" | custom-call | flops 100663296 | bytes 2621440 | tf_op jit(solution)/shard_map/pallas_call | solution.py:138
  (71 shorter events, 2.7 us)
Async XLA Ops:
  0.6 17.2 %copy-start = (bf16[512,2048]{1,0:T(8,128)(2,1)S(1)}, bf16[512,2048]{1,0:T(8,128)(2,1)}, u32[]{:S(2)}) copy-start(bf16[512,2048]{1,0:T(8,128)(2,1)} %param.23) | copy-start | bytes 6291460
  0.6 10.6 %copy-start.8 = (bf16[1,64,512]{2,1,0:T(8,128)(2,1)S(1)}, bf16[1,64,512]{2,1,0:T(8,128)(2,1)}, u32[]{:S(2)}) copy-start(bf16[1,64,512]{2,1,0:T(8,128)(2,1)} %param.20) | copy-start | bytes 196612
  0.7 10.6 %copy-start.9 = (bf16[1,64,512]{2,1,0:T(8,128)(2,1)S(1)}, bf16[1,64,512]{2,1,0:T(8,128)(2,1)}, u32[]{:S(2)}) copy-start(bf16[1,64,512]{2,1,0:T(8,128)(2,1)} %param.18) | copy-start | bytes 196612
  1.8 9.3 %collective-permute-start = (bf16[128,8,128]{2,1,0:T(8,128)(2,1)S(1)}, bf16[128,8,128]{2,1,0:T(8,128)(2,1)S(1)}, u32[]{:S(2)}, u32[]{:S(2)}) collective-permute-start(bf16[128,8,128]{2,1,0:T(8,128)(2,1)S(1)} %constant_dynamic-slice_fusion.2), channel_id=1, source_target_pairs={{0,16},{16,0},{1,17},{17,1},{2,18},{18,2},{3,19},{19,3},{4,20},{20... | collective-permute-start | bytes 786440 | tf_op jit(solution)/shard_map/ppermute | solution.py:66
  4.8 7.9 %copy-start.7 = (bf16[256,8,128]{2,1,0:T(8,128)(2,1)S(1)}, bf16[256,8,128]{2,1,0:T(8,128)(2,1)}, u32[]{:S(2)}) copy-start(bf16[256,8,128]{2,1,0:T(8,128)(2,1)} %param.22) | copy-start | bytes 1572868
  11.1 1.5 %collective-permute-start.1 = (bf16[128,8,128]{2,1,0:T(8,128)(2,1)S(1)}, bf16[128,8,128]{2,1,0:T(8,128)(2,1)S(1)}, u32[]{:S(2)}, u32[]{:S(2)}) collective-permute-start(bf16[128,8,128]{2,1,0:T(8,128)(2,1)S(1)} %collective-permute-done), channel_id=1, source_target_pairs={{0,1},{1,0},{2,3},{3,2},{4,5},{5,4},{6,7},{7,6},{8,9},{9,8},{10,11... | collective-permute-start | bytes 786440 | tf_op jit(solution)/shard_map/ppermute | solution.py:69
  13.0 41.9 %copy-start.3 = (bf16[1,704,2048]{2,1,0:T(8,128)(2,1)S(1)}, bf16[1,704,2048]{2,1,0:T(8,128)(2,1)}, u32[]{:S(2)}) copy-start(bf16[1,704,2048]{2,1,0:T(8,128)(2,1)} %param.29) | copy-start | bytes 8650756
  13.5 6.7 %copy-start.10 = (s32[1,64,6]{1,0,2:T(1,128)S(1)}, s32[1,64,6]{1,0,2:T(1,128)}, u32[]{:S(2)}) copy-start(s32[1,64,6]{1,0,2:T(1,128)} %param.26) | copy-start | bytes 4612
  13.5 15.0 %copy-start.4 = (bf16[1,64,2048]{2,1,0:T(8,128)(2,1)S(1)}, bf16[1,64,2048]{2,1,0:T(8,128)(2,1)}, u32[]{:S(2)}) copy-start(bf16[1,64,2048]{2,1,0:T(8,128)(2,1)} %x_ref.1) | copy-start | bytes 786436
  13.5 15.0 %copy-start.6 = (f32[2048]{0:T(1024)S(1)}, f32[2048]{0:T(1024)}, u32[]{:S(2)}) copy-start(f32[2048]{0:T(1024)} %param.24) | copy-start | bytes 24580
  13.5 4.3 %collective-permute-start.2 = (bf16[64,512]{1,0:T(8,128)(2,1)S(1)}, bf16[64,512]{1,0:T(8,128)(2,1)S(1)}, u32[]{:S(2)}, u32[]{:S(2)}) collective-permute-start(bf16[64,512]{1,0:T(8,128)(2,1)S(1)} %get-tuple-element.180), channel_id=1, source_target_pairs={{0,16},{16,0},{1,17},{17,1},{2,18},{18,2},{3,19},{19,3},{4,20},{20... | collective-permute-start | bytes 196616 | tf_op jit(solution)/shard_map/ppermute | solution.py:79
  17.9 36.9 %copy-start.2 = (bf16[1,2048,704]{1,2,0:T(8,128)(2,1)S(1)}, bf16[1,2048,704]{1,2,0:T(8,128)(2,1)}, u32[]{:S(2)}) copy-start(bf16[1,2048,704]{1,2,0:T(8,128)(2,1)} %param.28) | copy-start | bytes 8650756
  18.3 33.0 %copy-start.5 = (bf16[2048,16]{0,1:T(8,128)(2,1)S(1)}, bf16[2048,16]{0,1:T(8,128)(2,1)}, u32[]{:S(2)}) copy-start(bf16[2048,16]{0,1:T(8,128)(2,1)} %param.25) | copy-start | bytes 196612
  18.3 36.5 %copy-start.1 = (bf16[1,2048,704]{1,2,0:T(8,128)(2,1)S(1)}, bf16[1,2048,704]{1,2,0:T(8,128)(2,1)}, u32[]{:S(2)}) copy-start(bf16[1,2048,704]{1,2,0:T(8,128)(2,1)} %param.27) | copy-start | bytes 8650756
  18.4 10.1 %collective-permute-start.3 = (bf16[64,2048]{1,0:T(8,128)(2,1)S(1)}, bf16[64,2048]{1,0:T(8,128)(2,1)S(1)}, u32[]{:S(2)}, u32[]{:S(2)}) collective-permute-start(bf16[64,2048]{1,0:T(8,128)(2,1)S(1)} %slice.7), channel_id=1, source_target_pairs={{0,16},{16,0},{1,17},{17,1},{2,18},{18,2},{3,19},{19,3},{4,20},{20... | collective-permute-start | bytes 786440 | tf_op jit(solution)/shard_map/ppermute | solution.py:83
  20.2 5.6 %collective-permute-start.6 = (s32[6,64]{1,0:T(8,128)S(1)}, s32[6,64]{1,0:T(8,128)S(1)}, u32[]{:S(2)}, u32[]{:S(2)}) collective-permute-start(s32[6,64]{1,0:T(8,128)S(1)} %bitcast.45), channel_id=1, source_target_pairs={{0,12},{1,13},{2,14},{3,15},{4,8},{5,9},{6,10},{7,11},{8,4},{9,5},... | collective-permute-start | bytes 4616 | tf_op jit(solution)/shard_map/ppermute | solution.py:503
  23.8 3.6 %collective-permute-start.5 = (s32[6,64]{1,0:T(8,128)S(1)}, s32[6,64]{1,0:T(8,128)S(1)}, u32[]{:S(2)}, u32[]{:S(2)}) collective-permute-start(s32[6,64]{1,0:T(8,128)S(1)} %bitcast.46), channel_id=1, source_target_pairs={{4,0},{5,1},{6,2},{7,3},{12,4},{13,5},{14,6},{15,7},{8,12},{9,13},... | collective-permute-start | bytes 4616 | tf_op jit(solution)/shard_map/ppermute | solution.py:503
  23.8 4.5 %collective-permute-start.4 = (s32[6,64]{1,0:T(8,128)S(1)}, s32[6,64]{1,0:T(8,128)S(1)}, u32[]{:S(2)}, u32[]{:S(2)}) collective-permute-start(s32[6,64]{1,0:T(8,128)S(1)} %bitcast.47), channel_id=1, source_target_pairs={{0,4},{1,5},{2,6},{3,7},{4,12},{5,13},{6,14},{7,15},{12,8},{13,9},... | collective-permute-start | bytes 4616 | tf_op jit(solution)/shard_map/ppermute | solution.py:503
  29.4 9.1 %collective-permute-start.13 = (bf16[64,1024]{1,0:T(8,128)(2,1)S(1)}, bf16[64,1024]{1,0:T(8,128)(2,1)S(1)}, u32[]{:S(2)}, u32[]{:S(2)}) collective-permute-start(bf16[64,1024]{1,0:T(8,128)(2,1)S(1)} %get-tuple-element.98.refs_2_), channel_id=1, source_target_pairs={{4,0},{5,1},{6,2},{7,3},{12,4},{13,5},{14,6},{15,7},{8,12},{9,13},... | collective-permute-start | bytes 393224 | tf_op jit(solution)/shard_map/ppermute | solution.py:348
  29.4 10.5 %collective-permute-start.12 = (bf16[64,1024]{1,0:T(8,128)(2,1)S(1)}, bf16[64,1024]{1,0:T(8,128)(2,1)S(1)}, u32[]{:S(2)}, u32[]{:S(2)}) collective-permute-start(bf16[64,1024]{1,0:T(8,128)(2,1)S(1)} %get-tuple-element.99.refs_1_), channel_id=1, source_target_pairs={{0,4},{1,5},{2,6},{3,7},{4,12},{5,13},{6,14},{7,15},{12,8},{13,9},... | collective-permute-start | bytes 393224 | tf_op jit(solution)/shard_map/ppermute | solution.py:348
  31.7 1.9 %collective-permute-start.9 = (bf16[24,2048]{1,0:T(8,128)(2,1)S(1)}, bf16[24,2048]{1,0:T(8,128)(2,1)S(1)}, u32[]{:S(2)}, u32[]{:S(2)}) collective-permute-start(bf16[24,2048]{1,0:T(8,128)(2,1)S(1)} %get-tuple-element.102), channel_id=1, source_target_pairs={{0,1},{1,0},{2,3},{3,2},{4,5},{5,4},{6,7},{7,6},{8,9},{9,8},{10,11... | collective-permute-start | bytes 294920 | tf_op jit(solution)/shard_map/ppermute | solution.py:348
  31.7 5.7 %collective-permute-start.10 = (bf16[24,2048]{1,0:T(8,128)(2,1)S(1)}, bf16[24,2048]{1,0:T(8,128)(2,1)S(1)}, u32[]{:S(2)}, u32[]{:S(2)}) collective-permute-start(bf16[24,2048]{1,0:T(8,128)(2,1)S(1)} %get-tuple-element.103), channel_id=1, source_target_pairs={{0,2},{1,3},{2,0},{3,1},{4,6},{5,7},{6,4},{7,5},{8,10},{9,11},{10,... | collective-permute-start | bytes 294920 | tf_op jit(solution)/shard_map/ppermute | solution.py:348
  33.3 7.4 %collective-permute-start.11 = (bf16[24,2048]{1,0:T(8,128)(2,1)S(1)}, bf16[24,2048]{1,0:T(8,128)(2,1)S(1)}, u32[]{:S(2)}, u32[]{:S(2)}) collective-permute-start(bf16[24,2048]{1,0:T(8,128)(2,1)S(1)} %get-tuple-element.104), channel_id=1, source_target_pairs={{0,3},{1,2},{2,1},{3,0},{4,7},{5,6},{6,5},{7,4},{8,11},{9,10},{10,... | collective-permute-start | bytes 294920 | tf_op jit(solution)/shard_map/ppermute | solution.py:348
  33.6 7.2 %collective-permute-start.7 = (bf16[64,1024]{1,0:T(8,128)(2,1)S(1)}, bf16[64,1024]{1,0:T(8,128)(2,1)S(1)}, u32[]{:S(2)}, u32[]{:S(2)}) collective-permute-start(bf16[64,1024]{1,0:T(8,128)(2,1)S(1)} %get-tuple-element.98.refs_2_), channel_id=1, source_target_pairs={{0,4},{1,5},{2,6},{3,7},{4,12},{5,13},{6,14},{7,15},{12,8},{13,9},... | collective-permute-start | bytes 393224 | tf_op jit(solution)/shard_map/ppermute | solution.py:348
  37.5 6.5 %collective-permute-start.8 = (bf16[64,1024]{1,0:T(8,128)(2,1)S(1)}, bf16[64,1024]{1,0:T(8,128)(2,1)S(1)}, u32[]{:S(2)}, u32[]{:S(2)}) collective-permute-start(bf16[64,1024]{1,0:T(8,128)(2,1)S(1)} %get-tuple-element.99.refs_1_), channel_id=1, source_target_pairs={{4,0},{5,1},{6,2},{7,3},{12,4},{13,5},{14,6},{15,7},{8,12},{9,13},... | collective-permute-start | bytes 393224 | tf_op jit(solution)/shard_map/ppermute | solution.py:348
  38.4 8.2 %collective-permute-start.15 = (bf16[64,1024]{1,0:T(8,128)(2,1)S(1)}, bf16[64,1024]{1,0:T(8,128)(2,1)S(1)}, u32[]{:S(2)}, u32[]{:S(2)}) collective-permute-start(bf16[64,1024]{1,0:T(8,128)(2,1)S(1)} %collective-permute-done.13.refs_3_.refs_8_), channel_id=1, source_target_pairs={{4,0},{5,1},{6,2},{7,3},{12,4},{13,5},{14,6},{15,7},{8,12},{9,13},... | collective-permute-start | bytes 393224 | tf_op jit(solution)/shard_map/ppermute | solution.py:348
  40.0 9.9 %collective-permute-start.14 = (bf16[64,1024]{1,0:T(8,128)(2,1)S(1)}, bf16[64,1024]{1,0:T(8,128)(2,1)S(1)}, u32[]{:S(2)}, u32[]{:S(2)}) collective-permute-start(bf16[64,1024]{1,0:T(8,128)(2,1)S(1)} %collective-permute-done.12.refs_1_.refs_4_), channel_id=1, source_target_pairs={{0,4},{1,5},{2,6},{3,7},{4,12},{5,13},{6,14},{7,15},{12,8},{13,9},... | collective-permute-start | bytes 393224 | tf_op jit(solution)/shard_map/ppermute | solution.py:348
  40.7 3.5 %collective-permute-start.16 = (bf16[48,1024]{1,0:T(8,128)(2,1)S(1)}, bf16[48,1024]{1,0:T(8,128)(2,1)S(1)}, u32[]{:S(2)}, u32[]{:S(2)}) collective-permute-start(bf16[48,1024]{1,0:T(8,128)(2,1)S(1)} %get-tuple-element.124), channel_id=1, source_target_pairs={{0,1},{1,0},{2,3},{3,2},{4,5},{5,4},{6,7},{7,6},{8,9},{9,8},{10,11... | collective-permute-start | bytes 294920 | tf_op jit(solution)/shard_map/ppermute | solution.py:348
  40.8 11.0 %collective-permute-start.17 = (bf16[48,1024]{1,0:T(8,128)(2,1)S(1)}, bf16[48,1024]{1,0:T(8,128)(2,1)S(1)}, u32[]{:S(2)}, u32[]{:S(2)}) collective-permute-start(bf16[48,1024]{1,0:T(8,128)(2,1)S(1)} %get-tuple-element.125), channel_id=1, source_target_pairs={{0,2},{1,3},{2,0},{3,1},{4,6},{5,7},{6,4},{7,5},{8,10},{9,11},{10,... | collective-permute-start | bytes 294920 | tf_op jit(solution)/shard_map/ppermute | solution.py:348
  44.0 8.5 %collective-permute-start.18 = (bf16[48,1024]{1,0:T(8,128)(2,1)S(1)}, bf16[48,1024]{1,0:T(8,128)(2,1)S(1)}, u32[]{:S(2)}, u32[]{:S(2)}) collective-permute-start(bf16[48,1024]{1,0:T(8,128)(2,1)S(1)} %get-tuple-element.126), channel_id=1, source_target_pairs={{0,3},{1,2},{2,1},{3,0},{4,7},{5,6},{6,5},{7,4},{8,11},{9,10},{10,... | collective-permute-start | bytes 294920 | tf_op jit(solution)/shard_map/ppermute | solution.py:348
  44.2 8.7 %collective-permute-start.19 = (bf16[48,1024]{1,0:T(8,128)(2,1)S(1)}, bf16[48,1024]{1,0:T(8,128)(2,1)S(1)}, u32[]{:S(2)}, u32[]{:S(2)}) collective-permute-start(bf16[48,1024]{1,0:T(8,128)(2,1)S(1)} %get-tuple-element.128), channel_id=1, source_target_pairs={{0,1},{1,0},{2,3},{3,2},{4,5},{5,4},{6,7},{7,6},{8,9},{9,8},{10,11... | collective-permute-start | bytes 294920 | tf_op jit(solution)/shard_map/ppermute | solution.py:348
  46.6 7.2 %collective-permute-start.20 = (bf16[48,1024]{1,0:T(8,128)(2,1)S(1)}, bf16[48,1024]{1,0:T(8,128)(2,1)S(1)}, u32[]{:S(2)}, u32[]{:S(2)}) collective-permute-start(bf16[48,1024]{1,0:T(8,128)(2,1)S(1)} %get-tuple-element.129), channel_id=1, source_target_pairs={{0,2},{1,3},{2,0},{3,1},{4,6},{5,7},{6,4},{7,5},{8,10},{9,11},{10,... | collective-permute-start | bytes 294920 | tf_op jit(solution)/shard_map/ppermute | solution.py:348
  49.9 4.9 %collective-permute-start.21 = (bf16[48,1024]{1,0:T(8,128)(2,1)S(1)}, bf16[48,1024]{1,0:T(8,128)(2,1)S(1)}, u32[]{:S(2)}, u32[]{:S(2)}) collective-permute-start(bf16[48,1024]{1,0:T(8,128)(2,1)S(1)} %get-tuple-element.130), channel_id=1, source_target_pairs={{0,3},{1,2},{2,1},{3,0},{4,7},{5,6},{6,5},{7,4},{8,11},{9,10},{10,... | collective-permute-start | bytes 294920 | tf_op jit(solution)/shard_map/ppermute | solution.py:348
  51.9 5.9 %collective-permute-start.22 = (bf16[24,2048]{1,0:T(8,128)(2,1)S(1)}, bf16[24,2048]{1,0:T(8,128)(2,1)S(1)}, u32[]{:S(2)}, u32[]{:S(2)}) collective-permute-start(bf16[24,2048]{1,0:T(8,128)(2,1)S(1)} %get-tuple-element.148), channel_id=1, source_target_pairs={{0,1},{1,0},{2,3},{3,2},{4,5},{5,4},{6,7},{7,6},{8,9},{9,8},{10,11... | collective-permute-start | bytes 294920 | tf_op jit(solution)/shard_map/ppermute | solution.py:348
  52.4 5.7 %collective-permute-start.23 = (bf16[24,2048]{1,0:T(8,128)(2,1)S(1)}, bf16[24,2048]{1,0:T(8,128)(2,1)S(1)}, u32[]{:S(2)}, u32[]{:S(2)}) collective-permute-start(bf16[24,2048]{1,0:T(8,128)(2,1)S(1)} %get-tuple-element.149), channel_id=1, source_target_pairs={{0,2},{1,3},{2,0},{3,1},{4,6},{5,7},{6,4},{7,5},{8,10},{9,11},{10,... | collective-permute-start | bytes 294920 | tf_op jit(solution)/shard_map/ppermute | solution.py:348
  52.9 5.5 %collective-permute-start.24 = (bf16[24,2048]{1,0:T(8,128)(2,1)S(1)}, bf16[24,2048]{1,0:T(8,128)(2,1)S(1)}, u32[]{:S(2)}, u32[]{:S(2)}) collective-permute-start(bf16[24,2048]{1,0:T(8,128)(2,1)S(1)} %get-tuple-element.150), channel_id=1, source_target_pairs={{0,3},{1,2},{2,1},{3,0},{4,7},{5,6},{6,5},{7,4},{8,11},{9,10},{10,... | collective-permute-start | bytes 294920 | tf_op jit(solution)/shard_map/ppermute | solution.py:348
  60.8 4.4 %collective-permute-start.31 = (bf16[24,2048]{1,0:T(8,128)(2,1)S(1)}, bf16[24,2048]{1,0:T(8,128)(2,1)S(1)}, u32[]{:S(2)}, u32[]{:S(2)}) collective-permute-start(bf16[24,2048]{1,0:T(8,128)(2,1)S(1)} %get-tuple-element.167), channel_id=1, source_target_pairs={{0,1},{1,0},{2,3},{3,2},{4,5},{5,4},{6,7},{7,6},{8,9},{9,8},{10,11... | collective-permute-start | bytes 294920 | tf_op jit(solution)/shard_map/ppermute | solution.py:348
  61.6 5.2 %collective-permute-start.32 = (bf16[24,2048]{1,0:T(8,128)(2,1)S(1)}, bf16[24,2048]{1,0:T(8,128)(2,1)S(1)}, u32[]{:S(2)}, u32[]{:S(2)}) collective-permute-start(bf16[24,2048]{1,0:T(8,128)(2,1)S(1)} %get-tuple-element.168), channel_id=1, source_target_pairs={{0,2},{1,3},{2,0},{3,1},{4,6},{5,7},{6,4},{7,5},{8,10},{9,11},{10,... | collective-permute-start | bytes 294920 | tf_op jit(solution)/shard_map/ppermute | solution.py:348
  63.1 5.7 %collective-permute-start.33 = (bf16[24,2048]{1,0:T(8,128)(2,1)S(1)}, bf16[24,2048]{1,0:T(8,128)(2,1)S(1)}, u32[]{:S(2)}, u32[]{:S(2)}) collective-permute-start(bf16[24,2048]{1,0:T(8,128)(2,1)S(1)} %get-tuple-element.169), channel_id=1, source_target_pairs={{0,3},{1,2},{2,1},{3,0},{4,7},{5,6},{6,5},{7,4},{8,11},{9,10},{10,... | collective-permute-start | bytes 294920 | tf_op jit(solution)/shard_map/ppermute | solution.py:348
  63.1 7.5 %collective-permute-start.28 = (bf16[48,1024]{1,0:T(8,128)(2,1)S(1)}, bf16[48,1024]{1,0:T(8,128)(2,1)S(1)}, u32[]{:S(2)}, u32[]{:S(2)}) collective-permute-start(bf16[48,1024]{1,0:T(8,128)(2,1)S(1)} %get-tuple-element.158), channel_id=1, source_target_pairs={{0,1},{1,0},{2,3},{3,2},{4,5},{5,4},{6,7},{7,6},{8,9},{9,8},{10,11... | collective-permute-start | bytes 294920 | tf_op jit(solution)/shard_map/ppermute | solution.py:348
  63.7 7.3 %collective-permute-start.29 = (bf16[48,1024]{1,0:T(8,128)(2,1)S(1)}, bf16[48,1024]{1,0:T(8,128)(2,1)S(1)}, u32[]{:S(2)}, u32[]{:S(2)}) collective-permute-start(bf16[48,1024]{1,0:T(8,128)(2,1)S(1)} %get-tuple-element.159), channel_id=1, source_target_pairs={{0,2},{1,3},{2,0},{3,1},{4,6},{5,7},{6,4},{7,5},{8,10},{9,11},{10,... | collective-permute-start | bytes 294920 | tf_op jit(solution)/shard_map/ppermute | solution.py:348
  65.3 7.4 %collective-permute-start.37 = (bf16[48,1024]{1,0:T(8,128)(2,1)S(1)}, bf16[48,1024]{1,0:T(8,128)(2,1)S(1)}, u32[]{:S(2)}, u32[]{:S(2)}) collective-permute-start(bf16[48,1024]{1,0:T(8,128)(2,1)S(1)} %get-tuple-element.174), channel_id=1, source_target_pairs={{0,1},{1,0},{2,3},{3,2},{4,5},{5,4},{6,7},{7,6},{8,9},{9,8},{10,11... | collective-permute-start | bytes 294920 | tf_op jit(solution)/shard_map/ppermute | solution.py:348
  66.8 6.3 %collective-permute-start.38 = (bf16[48,1024]{1,0:T(8,128)(2,1)S(1)}, bf16[48,1024]{1,0:T(8,128)(2,1)S(1)}, u32[]{:S(2)}, u32[]{:S(2)}) collective-permute-start(bf16[48,1024]{1,0:T(8,128)(2,1)S(1)} %get-tuple-element.175), channel_id=1, source_target_pairs={{0,2},{1,3},{2,0},{3,1},{4,6},{5,7},{6,4},{7,5},{8,10},{9,11},{10,... | collective-permute-start | bytes 294920 | tf_op jit(solution)/shard_map/ppermute | solution.py:348
  68.8 5.7 %collective-permute-start.39 = (bf16[48,1024]{1,0:T(8,128)(2,1)S(1)}, bf16[48,1024]{1,0:T(8,128)(2,1)S(1)}, u32[]{:S(2)}, u32[]{:S(2)}) collective-permute-start(bf16[48,1024]{1,0:T(8,128)(2,1)S(1)} %get-tuple-element.176), channel_id=1, source_target_pairs={{0,3},{1,2},{2,1},{3,0},{4,7},{5,6},{6,5},{7,4},{8,11},{9,10},{10,... | collective-permute-start | bytes 294920 | tf_op jit(solution)/shard_map/ppermute | solution.py:348
  70.6 8.3 %collective-permute-start.34 = (bf16[64,1024]{1,0:T(8,128)(2,1)S(1)}, bf16[64,1024]{1,0:T(8,128)(2,1)S(1)}, u32[]{:S(2)}, u32[]{:S(2)}) collective-permute-start(bf16[64,1024]{1,0:T(8,128)(2,1)S(1)} %get-tuple-element.170), channel_id=1, source_target_pairs={{4,0},{5,1},{6,2},{7,3},{12,4},{13,5},{14,6},{15,7},{8,12},{9,13},... | collective-permute-start | bytes 393224 | tf_op jit(solution)/shard_map/ppermute | solution.py:348
  71.0 9.3 %collective-permute-start.35 = (bf16[64,1024]{1,0:T(8,128)(2,1)S(1)}, bf16[64,1024]{1,0:T(8,128)(2,1)S(1)}, u32[]{:S(2)}, u32[]{:S(2)}) collective-permute-start(bf16[64,1024]{1,0:T(8,128)(2,1)S(1)} %get-tuple-element.171), channel_id=1, source_target_pairs={{0,4},{1,5},{2,6},{3,7},{4,12},{5,13},{6,14},{7,15},{12,8},{13,9},... | collective-permute-start | bytes 393224 | tf_op jit(solution)/shard_map/ppermute | solution.py:348
  72.7 4.7 %collective-permute-start.30 = (bf16[48,1024]{1,0:T(8,128)(2,1)S(1)}, bf16[48,1024]{1,0:T(8,128)(2,1)S(1)}, u32[]{:S(2)}, u32[]{:S(2)}) collective-permute-start(bf16[48,1024]{1,0:T(8,128)(2,1)S(1)} %get-tuple-element.160), channel_id=1, source_target_pairs={{0,3},{1,2},{2,1},{3,0},{4,7},{5,6},{6,5},{7,4},{8,11},{9,10},{10,... | collective-permute-start | bytes 294920 | tf_op jit(solution)/shard_map/ppermute | solution.py:348
  73.1 8.2 %collective-permute-start.25 = (bf16[24,2048]{1,0:T(8,128)(2,1)S(1)}, bf16[24,2048]{1,0:T(8,128)(2,1)S(1)}, u32[]{:S(2)}, u32[]{:S(2)}) collective-permute-start(bf16[24,2048]{1,0:T(8,128)(2,1)S(1)} %get-tuple-element.152), channel_id=1, source_target_pairs={{0,1},{1,0},{2,3},{3,2},{4,5},{5,4},{6,7},{7,6},{8,9},{9,8},{10,11... | collective-permute-start | bytes 294920 | tf_op jit(solution)/shard_map/ppermute | solution.py:348
  74.5 9.1 %collective-permute-start.26 = (bf16[24,2048]{1,0:T(8,128)(2,1)S(1)}, bf16[24,2048]{1,0:T(8,128)(2,1)S(1)}, u32[]{:S(2)}, u32[]{:S(2)}) collective-permute-start(bf16[24,2048]{1,0:T(8,128)(2,1)S(1)} %get-tuple-element.153), channel_id=1, source_target_pairs={{0,2},{1,3},{2,0},{3,1},{4,6},{5,7},{6,4},{7,5},{8,10},{9,11},{10,... | collective-permute-start | bytes 294920 | tf_op jit(solution)/shard_map/ppermute | solution.py:348
  77.4 11.2 %collective-permute-start.40 = (bf16[64,1024]{1,0:T(8,128)(2,1)S(1)}, bf16[64,1024]{1,0:T(8,128)(2,1)S(1)}, u32[]{:S(2)}, u32[]{:S(2)}) collective-permute-start(bf16[64,1024]{1,0:T(8,128)(2,1)S(1)} %get-tuple-element.177), channel_id=1, source_target_pairs={{0,4},{1,5},{2,6},{3,7},{4,12},{5,13},{6,14},{7,15},{12,8},{13,9},... | collective-permute-start | bytes 393224 | tf_op jit(solution)/shard_map/ppermute | solution.py:348
  78.9 9.7 %collective-permute-start.41 = (bf16[64,1024]{1,0:T(8,128)(2,1)S(1)}, bf16[64,1024]{1,0:T(8,128)(2,1)S(1)}, u32[]{:S(2)}, u32[]{:S(2)}) collective-permute-start(bf16[64,1024]{1,0:T(8,128)(2,1)S(1)} %get-tuple-element.178), channel_id=1, source_target_pairs={{4,0},{5,1},{6,2},{7,3},{12,4},{13,5},{14,6},{15,7},{8,12},{9,13},... | collective-permute-start | bytes 393224 | tf_op jit(solution)/shard_map/ppermute | solution.py:348
  80.6 8.5 %collective-permute-start.36 = (bf16[64,1024]{1,0:T(8,128)(2,1)S(1)}, bf16[64,1024]{1,0:T(8,128)(2,1)S(1)}, u32[]{:S(2)}, u32[]{:S(2)}) collective-permute-start(bf16[64,1024]{1,0:T(8,128)(2,1)S(1)} %get-tuple-element.172), channel_id=1, source_target_pairs={{0,4},{1,5},{2,6},{3,7},{4,12},{5,13},{6,14},{7,15},{12,8},{13,9},... | collective-permute-start | bytes 393224 | tf_op jit(solution)/shard_map/ppermute | solution.py:348
  81.3 10.5 %collective-permute-start.42 = (bf16[64,1024]{1,0:T(8,128)(2,1)S(1)}, bf16[64,1024]{1,0:T(8,128)(2,1)S(1)}, u32[]{:S(2)}, u32[]{:S(2)}) collective-permute-start(bf16[64,1024]{1,0:T(8,128)(2,1)S(1)} %get-tuple-element.179), channel_id=1, source_target_pairs={{4,0},{5,1},{6,2},{7,3},{12,4},{13,5},{14,6},{15,7},{8,12},{9,13},... | collective-permute-start | bytes 393224 | tf_op jit(solution)/shard_map/ppermute | solution.py:348
  83.6 5.0 %collective-permute-start.27 = (bf16[24,2048]{1,0:T(8,128)(2,1)S(1)}, bf16[24,2048]{1,0:T(8,128)(2,1)S(1)}, u32[]{:S(2)}, u32[]{:S(2)}) collective-permute-start(bf16[24,2048]{1,0:T(8,128)(2,1)S(1)} %get-tuple-element.154), channel_id=1, source_target_pairs={{0,3},{1,2},{2,1},{3,0},{4,7},{5,6},{6,5},{7,4},{8,11},{9,10},{10,... | collective-permute-start | bytes 294920 | tf_op jit(solution)/shard_map/ppermute | solution.py:348
where the time goes:
time: 93 us; the launch traced here: 92.8 us
  starting transfers between devices  47.1 us (51%)
  waiting for transfers between devices  29.3 us (32%)
  Pallas kernels  9.81 us (11%)
  matrix products  3.86 us (4%)
  local copies, waits for them, and re-layouts  1.26 us (1%)
  between operations  1.05 us (1%)
    ppermute x36, starting transfers between devices, send(): return lax.ppermute(value, 'ep', steps)  34.9 us
    ppermute x36, waiting for transfers between devices, send(): return lax.ppermute(value, 'ep', steps)  19.6 us
    pallas_call x13, Pallas kernels, fused(): pl.pallas_call(body, out_shape=[jax.ShapeDtypeStruct(shape, dtype) for sh...  9.81 us
    ppermute x3, starting transfers between devices, per_device(): lax.ppermute(ids[0], 'ep', steps)  5.63 us
    ppermute x1, waiting for transfers between devices, project_paired(): lax.ppermute(lax.dynamic_slice_in_dim(w_uv, lane * rows, rows, 0), 'fsdp'...  3.65 us
    ppermute x1, starting transfers between devices, project_paired(): lax.ppermute(lax.dynamic_slice_in_dim(w_uv, lane * rows, rows, 0), 'fsdp'...  3.03 us
    ppermute x1, waiting for transfers between devices, project_paired(): other = lax.ppermute(give, 'fsdp', pair)  2.53 us
    ppermute x3, waiting for transfers between devices, per_device(): lax.ppermute(ids[0], 'ep', steps)  2.48 us
  transfers between devices with their start and end apart: 43, of which 20 were waited for; matrix products, arithmetic and copies ran while one was open for 3% of the time, Pallas kernels for 6%

commit v1 on v0

--- a/solution.py
+++ b/solution.py
@@ -62,26 +62,30 @@
     twins = [(i, i ^ 1) for i in range(ep)]
     side = lax.axis_index("fsdp")
     lane = lax.axis_index("ep") % 2
-    rows = w_uv.shape[0] // 2
+    rows, depth = w_uv.shape[0] // 2, w_uv.shape[2]
+    heads = w_out.shape[0] // depth
+
+    def own_heads(array, which):
+        return lax.dynamic_slice_in_dim(array, which * heads, heads, 1)
+
     mine = lax.ppermute(
-        lax.dynamic_slice_in_dim(w_uv, lane * rows, rows, 0), "fsdp", pair
-    )
+        lax.dynamic_slice(
+            w_uv, (lane * rows, (1 - side) * heads, 0), (rows, heads, depth)
+        ),
+        "fsdp",
+        pair,
+    )
+    other = lax.ppermute(own_heads(mixed_latent, 1 - side), "fsdp", pair)
     theirs = lax.ppermute(mine, "ep", twins)
     far = jnp.where(
         lane == 0, jnp.concatenate([mine, theirs], 0), jnp.concatenate([theirs, mine], 0)
     )
-    full = jnp.where(side == 0, jnp.concatenate([w_uv, far], 0), jnp.concatenate([far, w_uv], 0))
-    heads_flat = up_project(mixed_latent, full)
-    width = w_out.shape[0]
-    count = heads_flat.shape[0]
-    keep = lax.dynamic_slice_in_dim(heads_flat, side * width, width, 1)
-    give = lax.dynamic_slice_in_dim(heads_flat, (1 - side) * width, width, 1)
-    other = lax.ppermute(give, "fsdp", pair)
-    both = jnp.dot(
-        jnp.concatenate([other, keep], 0), w_out, preferred_element_type=jnp.float32
-    )
-    back = lax.ppermute(both[:count].astype(jnp.bfloat16), "fsdp", pair)
-    return both, back
+    near = own_heads(w_uv, side)
+    full = jnp.where(side == 0, jnp.concatenate([near, far], 0), jnp.concatenate([far, near], 0))
+    partial = jnp.dot(up_project(other, full), w_out, preferred_element_type=jnp.float32)
+    back = lax.ppermute(partial.astype(jnp.bfloat16), "fsdp", pair)
+    kept = up_project(own_heads(mixed_latent, side), full)
+    return jnp.dot(kept, w_out, preferred_element_type=jnp.float32), back
 
 
 def experts(rows, w_gate, w_up, w_down):
@@ -184,20 +188,28 @@
 def pick_kernel(capacity, sources, *refs):
     place = lax.axis_index("ep")
     position = 0
-    out = refs[-4:]
+    local_ref, twin_ref, cross_ref = refs[-3:]
+    count = len(sources)
     for n, pieces in enumerate(sources):
         found = matches(refs[position][...], capacity, place).astype(jnp.bfloat16)
         offset = 0
+        spots = ((local_ref, n), (twin_ref, n), (cross_ref, n), (cross_ref, count + n))
         for ref in refs[position + 1 : position + 1 + pieces]:
             rows = jnp.dot(found, ref[...], preferred_element_type=jnp.float32)
             rows = rows.astype(jnp.bfloat16)
             columns = slice(offset, offset + ref.shape[1])
             offset += ref.shape[1]
-            for j in range(4):
-                out[j][n * capacity : (n + 1) * capacity, columns] = rows[
+            for j, (out, spot) in enumerate(spots):
+                out[spot * capacity : (spot + 1) * capacity, columns] = rows[
                     j * capacity : (j + 1) * capacity
                 ]
         position += 1 + pieces
+
+
+def join_kernel(own_ref, got_ref, out_ref):
+    count = own_ref.shape[0]
+    out_ref[:count] = own_ref[...]
+    out_ref[count:] = got_ref[count:]
 
 
 def dot_rows(a, b):
@@ -234,10 +246,10 @@
         out[n][...] = found.T
 
 
-def norm_kernel(x_ref, both_ref, back_ref, gain_ref, hidden_ref, attended_ref, low_ref, high_ref):
-    count, width = hidden_ref.shape
+def norm_kernel(x_ref, part_ref, back_ref, gain_ref, hidden_ref, attended_ref, low_ref, high_ref):
+    width = hidden_ref.shape[1]
     hidden = x_ref[0].astype(jnp.float32) + (
-        both_ref[count:] + back_ref[...].astype(jnp.float32)
+        part_ref[...] + back_ref[...].astype(jnp.float32)
     )
     hidden_ref[...] = hidden
     attended_ref[0] = hidden.astype(jnp.bfloat16)
@@ -257,47 +269,51 @@
     return jnp.concatenate(active, 1)
 
 
+def arrived(local_ref, got_ref, traded_ref):
+    count = local_ref.shape[0]
+    return jnp.concatenate([local_ref[...], got_ref[:count], traded_ref[...]], 0)
+
+
 def near_expert_kernel(capacity, *refs):
-    first, second, own = refs[0:4], refs[4:8], refs[8:12]
-    gate_ref, up_ref, down_ref = refs[12:15]
-    out_first, out_second, out_own = refs[15:19], refs[19:23], refs[23:27]
-    rows = [
-        jnp.concatenate([a[:capacity], b[:capacity]], 1) for a, b in zip(first, second)
-    ]
-    rows += [
-        jnp.concatenate([b[capacity:], a[capacity:]], 1) for a, b in zip(first, second)
-    ]
-    rows += [ref[...] for ref in own]
-    active = hidden_units(jnp.concatenate(rows, 0), gate_ref, up_ref)
+    first, second, own = (arrived(*refs[n : n + 3]) for n in (0, 3, 6))
+    gate_ref, up_ref, down_ref = refs[9:12]
+    first_out, second_out, own_out = refs[12:15], refs[15:18], refs[18:21]
+    rows = []
+    for n in range(8):
+        part = slice(n * capacity, (n + 1) * capacity)
+        pieces = (first[part], second[part]) if n % 2 == 0 else (second[part], first[part])
+        rows.append(jnp.concatenate(pieces, 1))
+    active = hidden_units(jnp.concatenate(rows + [own], 0), gate_ref, up_ref)
     width = down_ref.shape[1]
     step = width // 4
     for start in range(0, width, step):
         result = jnp.dot(
             active, down_ref[:, start : start + step], preferred_element_type=jnp.float32
         ).astype(jnp.bfloat16)
-        low = start < width // 2
         columns = slice(start % (width // 2), start % (width // 2) + step)
-        for j in range(4):
-            blocks = [
-                result[(4 * n + j) * capacity : (4 * n + j + 1) * capacity] for n in range(3)
-            ]
-            before_out, after_out = (out_first, out_second) if low else (out_second, out_first)
-            before_out[j][:capacity, columns] = blocks[0]
-            after_out[j][capacity:, columns] = blocks[1]
-            out_own[j][:, start : start + step] = blocks[2]
-
-
-def far_expert_kernel(*refs):
-    gate_ref, up_ref, down_ref = refs[4:7]
-    rows = jnp.concatenate([ref[...] for ref in refs[:4]], 0)
-    active = hidden_units(rows, gate_ref, up_ref)
-    capacity = refs[0].shape[0]
+        for n in range(8):
+            block = result[n * capacity : (n + 1) * capacity]
+            outs = first_out if (start < width // 2) == (n % 2 == 0) else second_out
+            out = outs[min(n // 2, 2)]
+            spot = n % 2 if n < 6 else n - 4
+            out[spot * capacity : (spot + 1) * capacity, columns] = block
+        for n in range(4):
+            block = result[(8 + n) * capacity : (9 + n) * capacity]
+            out = own_out[min(n, 2)]
+            spot = max(n - 2, 0)
+            out[spot * capacity : (spot + 1) * capacity, start : start + step] = block
+
+
+def far_expert_kernel(local_ref, got_ref, traded_ref, gate_ref, up_ref, down_ref, *outs):
+    active = hidden_units(arrived(local_ref, got_ref, traded_ref), gate_ref, up_ref)
+    capacity = local_ref.shape[0]
     for start in range(0, down_ref.shape[1], 512):
         part = slice(start, start + 512)
         result = jnp.dot(active, down_ref[:, part], preferred_element_type=jnp.float32)
         result = result.astype(jnp.bfloat16)
-        for j in range(4):
-            refs[7 + j][:, part] = result[j * capacity : (j + 1) * capacity]
+        outs[0][:, part] = result[:capacity]
+        outs[1][:, part] = result[capacity : 2 * capacity]
+        outs[2][:, part] = result[2 * capacity :]
 
 
 def weigh(weights, rows):
@@ -308,27 +324,45 @@
     )
 
 
-def far_kernel(weights_ref, r0, r1, r2, r3, low_ref, high_ref):
-    rows = jnp.concatenate([r[...] for r in (r0, r1, r2, r3)], 0)
+def returned(local_ref, got_ref, cross_ref, n, capacity):
+    count = local_ref.shape[0]
+    part = slice(n * capacity, (n + 1) * capacity)
+    late = slice(count + n * capacity, count + (n + 1) * capacity)
+    return jnp.concatenate(
+        [local_ref[part], got_ref[part], cross_ref[part], cross_ref[late]], 0
+    )
+
+
+def far_kernel(weights_ref, local_ref, got_ref, cross_ref, low_ref, high_ref):
+    rows = returned(local_ref, got_ref, cross_ref, 0, local_ref.shape[0])
     total = weigh(weights_ref[...], rows)
     half = low_ref.shape[1]
     low_ref[...] = total[:, :half].astype(jnp.bfloat16)
     high_ref[...] = total[:, half:].astype(jnp.bfloat16)
 
 
-def near_kernel(capacity, before_w, after_w, r0, r1, r2, r3, *refs):
-    blocks = (r0, r1, r2, r3)
+def near_kernel(capacity, before_w, after_w, local_ref, got_ref, cross_ref, *refs):
     adds = refs[:-2]
     for n, weights in enumerate((before_w, after_w)):
-        rows = jnp.concatenate([r[n * capacity : (n + 1) * capacity] for r in blocks], 0)
-        total = weigh(weights[...], rows)
+        total = weigh(weights[...], returned(local_ref, got_ref, cross_ref, n, capacity))
         if adds:
             total += adds[n][...].astype(jnp.float32)
         refs[len(adds) + n][...] = total.astype(jnp.bfloat16)
 
 
-def last_kernel(hidden_ref, weights_ref, r0, r1, r2, r3, x_low, x_high, y_low, y_high, out_ref):
-    rows = jnp.concatenate([r[...] for r in (r0, r1, r2, r3)], 0)
+def last_kernel(
+    hidden_ref,
+    weights_ref,
+    local_ref,
+    got_ref,
+    cross_ref,
+    x_low,
+    x_high,
+    y_low,
+    y_high,
+    out_ref,
+):
+    rows = returned(local_ref, got_ref, cross_ref, 0, local_ref.shape[0])
     total = hidden_ref[...] + weigh(weights_ref[...], rows)
     half = x_low.shape[1]
     low = x_low[...].astype(jnp.float32) + y_low[...].astype(jnp.float32)
@@ -339,7 +373,7 @@
 
 def routed_ringed(hidden, low, high, targets, capacity, router, w_gate, w_up, w_down):
     onward, backward = ring_steps()
-    traded = [[(i, i ^ j) for i in range(16)] for j in range(4)]
+    over_core, over_y = ([(i, i ^ j) for i in range(16)] for j in (1, 2))
     count, half = low.shape
     width = 2 * half
     bf16 = jnp.bfloat16
@@ -352,14 +386,30 @@
         columns = sum(part.shape[1] for part in sources[0][1:])
         return fused(
             functools.partial(pick_kernel, capacity, [len(source) - 1 for source in sources]),
-            [((n * capacity, columns), bf16)] * 4,
+            [((m * capacity, columns), bf16) for m in (n, n, 2 * n)],
             *[part for source in sources for part in source],
             flops=n * 2 * 4 * capacity * count * columns,
             bytes_accessed=n * 4 * columns * (count + 4 * capacity),
         )
 
+    def join(own, got):
+        return fused(
+            join_kernel,
+            [(got.shape, bf16)],
+            own,
+            got,
+            bytes_accessed=4 * got.shape[0] * got.shape[1],
+        )[0]
+
     def trade(blocks):
-        return [blocks[0]] + [send(blocks[j], traded[j]) for j in (1, 2, 3)]
+        local, twin, cross = blocks
+        got = send(cross, over_y)
+        return [local, got, send(join(twin, got), over_core)]
+
+    def untrade(blocks):
+        local, cross, twin = blocks
+        got = send(twin, over_core)
+        return [local, got, send(join(cross, got), over_y)]
 
     own_slots, before_slots, after_slots, far_slots = targets
     before_low, after_high = send(low, onward), send(high, backward)
@@ -367,9 +417,6 @@
     own_rows = trade(pick((own_slots, low, high)))
     far_low, far_high = send(before_low, onward), send(after_high, backward)
     first_rows = trade(pick((before_slots, before_low), (after_slots, after_high)))
-    before_high, after_low, own_rows, first_rows[0] = lax.optimization_barrier(
-        (before_high, after_low, own_rows, first_rows[0])
-    )
     second_rows = trade(pick((before_slots, before_high), (after_slots, after_low)))
     far_rows = trade(pick((far_slots, far_low, far_high)))
     expert_weights = (jnp.swapaxes(w_gate[0], 0, 1), jnp.swapaxes(w_up[0], 0, 1), w_down[0])
@@ -390,19 +437,21 @@
     )
     own_rows, weights = lax.optimization_barrier((own_rows, weights))
     blocks = first_rows + second_rows + own_rows
+    outs = []
+    for local, _, twin in (first_rows, second_rows, own_rows):
+        outs += [(local.shape, bf16), (local.shape, bf16), (twin.shape, bf16)]
     near = fused(
         functools.partial(near_expert_kernel, capacity),
-        [(b.shape, bf16) for b in blocks],
+        outs,
         *blocks,
         *expert_weights,
         vmem=16,
         flops=6 * 12 * capacity * unit,
         bytes_accessed=6 * unit + 4 * 12 * capacity * width,
     )
-    near, far_rows = lax.optimization_barrier((near, far_rows))
     result = fused(
         far_expert_kernel,
-        [(b.shape, bf16) for b in far_rows],
+        [(far_rows[n].shape, bf16) for n in (0, 0, 2)],
         *far_rows,
         *expert_weights,
         vmem=16,
@@ -416,7 +465,7 @@
         far_kernel,
         [piece] * 2,
         weights[3],
-        *trade(result),
+        *untrade(result),
         flops=spent,
         bytes_accessed=moved,
     )
@@ -428,16 +477,16 @@
             [piece] * 2,
             weights[1],
             weights[2],
-            *trade(rows),
+            *untrade(rows),
             *adds,
             flops=spent,
             bytes_accessed=moved,
         )
 
-    before_sum, after_sum = near_sums(near[0:4])
+    before_sum, after_sum = near_sums(near[0:3])
     from_after_low = send(before_sum, backward)
     from_before_high = send(after_sum, onward)
-    before_sum, after_sum = near_sums(near[4:8], add_high, add_low)
+    before_sum, after_sum = near_sums(near[3:6], add_high, add_low)
     from_after_high = send(before_sum, backward)
     from_before_low = send(after_sum, onward)
     return fused(
@@ -445,7 +494,7 @@
         [((count, width), bf16)],
         hidden,
         weights[0],
-        *trade(near[8:12]),
+        *untrade(near[6:9]),
         from_before_low,
         from_before_high,
         from_after_low,
@@ -506,9 +555,9 @@
         [(part.shape, jnp.int32) for part in ids],
         *ids,
     )
-    both, back = project_paired(mixed_latent, w_uv, w_out)
+    part, back = project_paired(mixed_latent, w_uv, w_out)
     back, targets = lax.optimization_barrier((back, targets))
-    width = both.shape[1]
+    width = part.shape[1]
     halves = (new_count, width // 2)
     hidden, attended, low, high = fused(
         norm_kernel,
@@ -519,7 +568,7 @@
             (halves, jnp.bfloat16),
         ],
         x_resid,
-        both,
+        part,
         back,
         norm_gain[None],
         flops=8 * new_count * width,

time: 93 us -> 101 us (1.086)
  waiting for transfers between devices: 29.3 us -> 45.5 us
  starting transfers between devices: 47.1 us -> 36.8 us
  local copies, waits for them, and re-layouts: 1.26 us -> 2.38 us
    ppermute x36 -> x28, waiting for transfers between devices: 19.6 us -> 33.5 us  [send(): return lax.ppermute(value, 'ep', steps)]
    ppermute x36 -> x28, starting transfers between devices: 34.9 us -> 25 us  [send(): return lax.ppermute(value, 'ep', steps)]
    ppermute x3, waiting for transfers between devices: 6.18 us -> 12 us  [the longest x1 5.88 us: project_paired(): back = lax.ppermute(partial.astype(jnp.bfloat16), 'fsdp', pair)]
    ppermute x3, waiting for transfers between devices: 2.48 us -> 0.01 us  [per_device(): lax.ppermute(ids[0], 'ep', steps)]
    ppermute x3, starting transfers between devices: 6.64 us -> 4.66 us  [the longest x1 1.56 us: project_paired(): lax.ppermute(lax.dynamic_slice(w_uv, (lane * rows, (1 - side) * heads, 0)...]
    ppermute x3, starting transfers between devices: 5.63 us -> 7.1 us  [per_device(): lax.ppermute(ids[0], 'ep', steps)]
    ppermute x1, waiting for transfers between devices: 1.1 us -> 0.01 us  [project_paired(): theirs = lax.ppermute(mine, 'ep', twins)]
    pallas_call x13 -> x21, Pallas kernels: 9.81 us -> 9.91 us  [fused(): pl.pallas_call(body, out_shape=[jax.ShapeDtypeStruct(shape, dtype) for sh...]
  transfers between devices with their start and end apart: 43 -> 35, of which waited for: 20 -> 15; matrix products, arithmetic and copies ran while one was open for 3% -> 6% of each run, Pallas kernels for 6% -> 8%
where the time goes in v1:
time: 101 us
  waiting for transfers between devices  45.5 us (45%)
  starting transfers between devices  36.8 us (36%)
  Pallas kernels  9.91 us (10%)
  matrix products  4.38 us (4%)
  local copies, waits for them, and re-layouts  2.38 us (2%)
  between operations  1.07 us (1%)
    ppermute x28, waiting for transfers between devices, send(): return lax.ppermute(value, 'ep', steps)  33.5 us
    ppermute x28, starting transfers between devices, send(): return lax.ppermute(value, 'ep', steps)  25 us
    pallas_call x21, Pallas kernels, fused(): pl.pallas_call(body, out_shape=[jax.ShapeDtypeStruct(shape, dtype) for sh...  9.91 us
    ppermute x3, starting transfers between devices, per_device(): lax.ppermute(ids[0], 'ep', steps)  7.1 us
    ppermute x1, waiting for transfers between devices, project_paired(): back = lax.ppermute(partial.astype(jnp.bfloat16), 'fsdp', pair)  5.88 us
    ppermute x1, waiting for transfers between devices, project_paired(): other = lax.ppermute(own_heads(mixed_latent, 1 - side), 'fsdp', pair)  5.7 us
  transfers between devices with their start and end apart: 35, of which 15 were waited for; matrix products, arithmetic and copies ran while one was open for 6% of the time, Pallas kernels for 8%

profile of v1, /device:TPU:0, one launch (start us, length us, event | category | flops | bytes accessed | tf_op | source)
XLA Modules:
  0.0 100.9 jit_solution(7071535579592754372)
XLA Ops:
  0.7 0.8 copy.47
  1.5 5.1 %collective-permute-start.6 = (s32[6,64]{1,0:T(8,128)S(1)}, s32[6,64]{1,0:T(8,128)S(1)}, u32[]{:S(2)}, u32[]{:S(2)}) collective-permute-start(s32[6,64]{1,0:T(8,128)S(1)} %bitcast.53), channel_id=1, source_target_pairs={{0,12},{1,13},{2,14},{3,15},{4,8},{5,9},{6,10},{7,11},{8,4},{9,5},... | collective-permute-start | bytes 4616 | tf_op jit(solution)/shard_map/ppermute | solution.py:552
  6.6 2.0 %collective-permute-start.4 = (s32[6,64]{1,0:T(8,128)S(1)}, s32[6,64]{1,0:T(8,128)S(1)}, u32[]{:S(2)}, u32[]{:S(2)}) collective-permute-start(s32[6,64]{1,0:T(8,128)S(1)} %bitcast.55), channel_id=1, source_target_pairs={{0,4},{1,5},{2,6},{3,7},{4,12},{5,13},{6,14},{7,15},{12,8},{13,9},... | collective-permute-start | bytes 4616 | tf_op jit(solution)/shard_map/ppermute | solution.py:552
  8.6 1.0 %constant_dynamic-slice_fusion.2 = bf16[128,4,128]{2,1,0:T(4,128)(2,1)S(1)} fusion(bf16[256,8,128]{2,1,0:T(8,128)(2,1)} %param.22, s32[]{:T(128)S(6)} %select_n.56, s32[]{:T(128)S(6)} %select_n.57), kind=kLoop, calls=%fused_computation.47 | loop fusion | bytes 262152 | tf_op jit(solution)/shard_map/dynamic_slice | solution.py:72
  9.6 1.6 %collective-permute-start = (bf16[128,4,128]{2,1,0:T(4,128)(2,1)S(1)}, bf16[128,4,128]{2,1,0:T(4,128)(2,1)S(1)}, u32[]{:S(2)}, u32[]{:S(2)}) collective-permute-start(bf16[128,4,128]{2,1,0:T(4,128)(2,1)S(1)} %constant_dynamic-slice_fusion.2), channel_id=1, source_target_pairs={{0,16},{16,0},{1,17},{17,1},{2,18},{18,2},{3,19},{19,3},{4,20},{20... | collective-permute-start | bytes 393224 | tf_op jit(solution)/shard_map/ppermute | solution.py:71
  11.2 1.4 %fusion.5 = f32[128,512]{1,0:T(8,128)S(1)} fusion(bf16[1,64,8,512]{3,2,1,0:T(8,128)(2,1)} %param.16, bf16[64,512]{1,0:T(8,128)(2,1)} %bitcast.59, bf16[64,512]{1,0:T(8,128)(2,1)} %bitcast.61), kind=kOutput, calls=%fused_computation.11 | convolution fusion | flops 67371008 | bytes 917504 | tf_op jit(solution)/shard_map/dot_general | solution.py:22
  12.6 1.2 %select_reduce_fusion = (f32[512]{0:T(512)S(1)}, f32[512,128]{0,1:T(8,128)S(1)}) fusion(s32[512]{0:T(512)S(1)} %fusion.24, f32[128,512]{1,0:T(8,128)S(1)} %fusion.5, bf16[1,64,8,64]{3,2,1,0:T(8,128)(2,1)} %param.17, bf16[64,64]{1,0:T(8,128)(2,1)} %bitcast.63, bf16[64,64]{1,0:T(8,128)(2,1)} %bitcast.64), kind=kOutput, calls=%fused_computation.19 | convolution fusion | flops 8748544 | bytes 610304 | tf_op jit(solution)/shard_map/dot_general | solution.py:24
  13.9 0.3 fusion
  14.3 0.4 collective-permute-done
  14.7 0.3 constant_dynamic-slice_fusion
  15.0 1.6 %collective-permute-start.2 = (bf16[64,4,512]{2,0,1:T(8,128)(2,1)S(1)}, bf16[64,4,512]{2,0,1:T(8,128)(2,1)S(1)}, u32[]{:S(2)}, u32[]{:S(2)}) collective-permute-start(bf16[64,4,512]{2,0,1:T(8,128)(2,1)S(1)} %copy.29), channel_id=1, source_target_pairs={{0,16},{16,0},{1,17},{17,1},{2,18},{18,2},{3,19},{19,3},{4,20},{20... | collective-permute-start | bytes 786440 | tf_op jit(solution)/shard_map/ppermute | solution.py:78
  16.6 0.1 constant_dynamic-slice_fusion.3
  16.7 0.2 shard_map.158
  16.9 0.3 maximum_select_fusion.1
  17.3 0.6 maximum_select_fusion
  17.8 0.2 fusion.3
  18.1 5.7 %collective-permute-done.2 = bf16[64,4,512]{2,0,1:T(8,128)(2,1)S(1)} collective-permute-done((bf16[64,4,512]{2,0,1:T(8,128)(2,1)S(1)}, bf16[64,4,512]{2,0,1:T(8,128)(2,1)S(1)}, u32[]{:S(2)}, u32[]{:S(2)}) %collective-permute-start.2) | collective-permute-done | bytes 262176 | tf_op jit(solution)/shard_map/ppermute | solution.py:78
  23.8 0.2 fusion.4
  24.1 0.5 convolution_convert_fusion
  24.6 1.5 %collective-permute-start.3 = (bf16[64,2048]{1,0:T(8,128)(2,1)S(1)}, bf16[64,2048]{1,0:T(8,128)(2,1)S(1)}, u32[]{:S(2)}, u32[]{:S(2)}) collective-permute-start(bf16[64,2048]{1,0:T(8,128)(2,1)S(1)} %convolution_convert_fusion), channel_id=1, source_target_pairs={{0,16},{16,0},{1,17},{17,1},{2,18},{18,2},{3,19},{19,3},{4,20},{20... | collective-permute-start | bytes 786440 | tf_op jit(solution)/shard_map/ppermute | solution.py:86
  26.1 0.5 fusion.18.part_ref
  26.6 5.9 %collective-permute-done.3.back_ref = bf16[64,2048]{1,0:T(8,128)(2,1)S(1)} collective-permute-done((bf16[64,2048]{1,0:T(8,128)(2,1)S(1)}, bf16[64,2048]{1,0:T(8,128)(2,1)S(1)}, u32[]{:S(2)}, u32[]{:S(2)}) %collective-permute-start.3) | collective-permute-done | bytes 262176 | tf_op jit(solution)/shard_map/ppermute | solution.py:86
  32.5 0.8 shard_map.159
  33.3 0.4 collective-permute-start.9
  33.8 2.5 %collective-permute-start.12 = (bf16[64,1024]{1,0:T(8,128)(2,1)S(1)}, bf16[64,1024]{1,0:T(8,128)(2,1)S(1)}, u32[]{:S(2)}, u32[]{:S(2)}) collective-permute-start(bf16[64,1024]{1,0:T(8,128)(2,1)S(1)} %get-tuple-element.68.refs_2_), channel_id=1, source_target_pairs={{4,0},{5,1},{6,2},{7,3},{12,4},{13,5},{14,6},{15,7},{8,12},{9,13},... | collective-permute-start | bytes 393224 | tf_op jit(solution)/shard_map/ppermute | solution.py:382
  36.3 5.0 %collective-permute-done.9.refs_4_.refs_1_ = bf16[64,1024]{1,0:T(8,128)(2,1)S(1)} collective-permute-done((bf16[64,1024]{1,0:T(8,128)(2,1)S(1)}, bf16[64,1024]{1,0:T(8,128)(2,1)S(1)}, u32[]{:S(2)}, u32[]{:S(2)}) %collective-permute-start.9) | collective-permute-done | bytes 131104 | tf_op jit(solution)/shard_map/ppermute | solution.py:382
  41.2 2.9 %collective-permute-start.14 = (bf16[64,1024]{1,0:T(8,128)(2,1)S(1)}, bf16[64,1024]{1,0:T(8,128)(2,1)S(1)}, u32[]{:S(2)}, u32[]{:S(2)}) collective-permute-start(bf16[64,1024]{1,0:T(8,128)(2,1)S(1)} %collective-permute-done.12.refs_8_.refs_3_), channel_id=1, source_target_pairs={{4,0},{5,1},{6,2},{7,3},{12,4},{13,5},{14,6},{15,7},{8,12},{9,13},... | collective-permute-start | bytes 393224 | tf_op jit(solution)/shard_map/ppermute | solution.py:382
  44.2 2.0 %collective-permute-start.10 = (bf16[64,1024]{1,0:T(8,128)(2,1)S(1)}, bf16[64,1024]{1,0:T(8,128)(2,1)S(1)}, u32[]{:S(2)}, u32[]{:S(2)}) collective-permute-start(bf16[64,1024]{1,0:T(8,128)(2,1)S(1)} %get-tuple-element.68.refs_2_), channel_id=1, source_target_pairs={{0,4},{1,5},{2,6},{3,7},{4,12},{5,13},{6,14},{7,15},{12,8},{13,9},... | collective-permute-start | bytes 393224 | tf_op jit(solution)/shard_map/ppermute | solution.py:382
  46.2 0.3 shard_map.160
  46.5 1.6 %collective-permute-start.7 = (bf16[48,2048]{1,0:T(8,128)(2,1)S(1)}, bf16[48,2048]{1,0:T(8,128)(2,1)S(1)}, u32[]{:S(2)}, u32[]{:S(2)}) collective-permute-start(bf16[48,2048]{1,0:T(8,128)(2,1)S(1)} %get-tuple-element.70), channel_id=1, source_target_pairs={{0,2},{1,3},{2,0},{3,1},{4,6},{5,7},{6,4},{7,5},{8,10},{9,11},{10,... | collective-permute-start | bytes 589832 | tf_op jit(solution)/shard_map/ppermute | solution.py:382
  48.0 3.6 %collective-permute-done.13.refs_1_.refs_10_ = bf16[64,1024]{1,0:T(8,128)(2,1)S(1)} collective-permute-done((bf16[64,1024]{1,0:T(8,128)(2,1)S(1)}, bf16[64,1024]{1,0:T(8,128)(2,1)S(1)}, u32[]{:S(2)}, u32[]{:S(2)}) %collective-permute-start.13) | collective-permute-done | bytes 131104 | tf_op jit(solution)/shard_map/ppermute | solution.py:382
  51.7 0.3 shard_map.162
  51.9 1.6 %collective-permute-start.23 = (bf16[48,2048]{1,0:T(8,128)(2,1)S(1)}, bf16[48,2048]{1,0:T(8,128)(2,1)S(1)}, u32[]{:S(2)}, u32[]{:S(2)}) collective-permute-start(bf16[48,2048]{1,0:T(8,128)(2,1)S(1)} %get-tuple-element.102), channel_id=1, source_target_pairs={{0,2},{1,3},{2,0},{3,1},{4,6},{5,7},{6,4},{7,5},{8,10},{9,11},{10,... | collective-permute-start | bytes 589832 | tf_op jit(solution)/shard_map/ppermute | solution.py:382
  53.5 0.3 shard_map.166
  53.8 1.6 %collective-permute-start.17 = (bf16[96,1024]{1,0:T(8,128)(2,1)S(1)}, bf16[96,1024]{1,0:T(8,128)(2,1)S(1)}, u32[]{:S(2)}, u32[]{:S(2)}) collective-permute-start(bf16[96,1024]{1,0:T(8,128)(2,1)S(1)} %get-tuple-element.87), channel_id=1, source_target_pairs={{0,2},{1,3},{2,0},{3,1},{4,6},{5,7},{6,4},{7,5},{8,10},{9,11},{10,... | collective-permute-start | bytes 589832 | tf_op jit(solution)/shard_map/ppermute | solution.py:382
  55.4 0.3 shard_map.164
  55.6 0.6 collective-permute-start.15
  56.3 3.5 %collective-permute-done.23.got_ref = bf16[48,2048]{1,0:T(8,128)(2,1)S(1)} collective-permute-done((bf16[48,2048]{1,0:T(8,128)(2,1)S(1)}, bf16[48,2048]{1,0:T(8,128)(2,1)S(1)}, u32[]{:S(2)}, u32[]{:S(2)}) %collective-permute-start.23) | collective-permute-done | bytes 196640 | tf_op jit(solution)/shard_map/ppermute | solution.py:382
  59.9 3.9 %collective-permute-done.17.got_ref.refs_4_ = bf16[96,1024]{1,0:T(8,128)(2,1)S(1)} collective-permute-done((bf16[96,1024]{1,0:T(8,128)(2,1)S(1)}, bf16[96,1024]{1,0:T(8,128)(2,1)S(1)}, u32[]{:S(2)}, u32[]{:S(2)}) %collective-permute-start.17) | collective-permute-done | bytes 196640 | tf_op jit(solution)/shard_map/ppermute | solution.py:382
  63.9 2.0 %collective-permute-done.15.got_ref.refs_1_ = bf16[96,1024]{1,0:T(8,128)(2,1)S(1)} collective-permute-done((bf16[96,1024]{1,0:T(8,128)(2,1)S(1)}, bf16[96,1024]{1,0:T(8,128)(2,1)S(1)}, u32[]{:S(2)}, u32[]{:S(2)}) %collective-permute-start.15) | collective-permute-done | bytes 196640 | tf_op jit(solution)/shard_map/ppermute | solution.py:382
  66.0 0.5 shard_map.163
  66.6 2.4 %shard_map.172 = (bf16[24,2048]{1,0:T(8,128)(2,1)S(1)}, bf16[24,2048]{1,0:T(8,128)(2,1)S(1)}, bf16[48,2048]{1,0:T(8,128)(2,1)S(1)}) custom-call(bf16[24,2048]{1,0:T(8,128)(2,1)S(1)} %get-tuple-element.101.local_ref, bf16[48,2048]{1,0:T(8,128)(2,1)S(1)} %collective-permute-done.23.got_ref, bf16[48,2048]{1,0:T(8,128)(2,1)S(1)} %collective-permute-done.24.traded_ref, ...), custom_call_target="tpu_custom_call" | custom-call | flops 830472192 | bytes 9437184 | tf_op jit(solution)/shard_map/pallas_call | solution.py:142
  69.0 0.5 collective-permute-start.25
  69.5 3.0 %shard_map.168 = (bf16[48,1024]{1,0:T(8,128)(2,1)S(1)}, bf16[48,1024]{1,0:T(8,128)(2,1)S(1)}, bf16[96,1024]{1,0:T(8,128)(2,1)S(1)}, bf16[48,1024]{1,0:T(8,128)(2...) custom-call(bf16[48,1024]{1,0:T(8,128)(2,1)S(1)} %get-tuple-element., ...), custom_call_target="tpu_custom_call" | custom-call | flops 2491416576 | bytes 11010048 | tf_op jit(solution)/shard_map/pallas_call | solution.py:142
  72.5 0.1 collective-permute-start.30
  72.6 0.5 collective-permute-start.21
  73.1 1.6 %collective-permute-start.26 = (bf16[48,2048]{1,0:T(8,128)(2,1)S(1)}, bf16[48,2048]{1,0:T(8,128)(2,1)S(1)}, u32[]{:S(2)}, u32[]{:S(2)}) collective-permute-start(bf16[48,2048]{1,0:T(8,128)(2,1)S(1)} %shard_map.173), channel_id=1, source_target_pairs={{0,2},{1,3},{2,0},{3,1},{4,6},{5,7},{6,4},{7,5},{8,10},{9,11},{10,... | collective-permute-start | bytes 589832 | tf_op jit(solution)/shard_map/ppermute | solution.py:382
  74.7 0.9 collective-permute-start.31
  75.6 1.3 %collective-permute-start.22 = (bf16[96,1024]{1,0:T(8,128)(2,1)S(1)}, bf16[96,1024]{1,0:T(8,128)(2,1)S(1)}, u32[]{:S(2)}, u32[]{:S(2)}) collective-permute-start(bf16[96,1024]{1,0:T(8,128)(2,1)S(1)} %shard_map.170), channel_id=1, source_target_pairs={{0,2},{1,3},{2,0},{3,1},{4,6},{5,7},{6,4},{7,5},{8,10},{9,11},{10,... | collective-permute-start | bytes 589832 | tf_op jit(solution)/shard_map/ppermute | solution.py:382
  76.9 4.1 %collective-permute-done.26.cross_ref = bf16[48,2048]{1,0:T(8,128)(2,1)S(1)} collective-permute-done((bf16[48,2048]{1,0:T(8,128)(2,1)S(1)}, bf16[48,2048]{1,0:T(8,128)(2,1)S(1)}, u32[]{:S(2)}, u32[]{:S(2)}) %collective-permute-start.26) | collective-permute-done | bytes 196640 | tf_op jit(solution)/shard_map/ppermute | solution.py:382
  80.9 0.3 shard_map.174
  81.3 2.0 %collective-permute-start.28 = (bf16[64,1024]{1,0:T(8,128)(2,1)S(1)}, bf16[64,1024]{1,0:T(8,128)(2,1)S(1)}, u32[]{:S(2)}, u32[]{:S(2)}) collective-permute-start(bf16[64,1024]{1,0:T(8,128)(2,1)S(1)} %get-tuple-element.108), channel_id=1, source_target_pairs={{0,4},{1,5},{2,6},{3,7},{4,12},{5,13},{6,14},{7,15},{12,8},{13,9},... | collective-permute-start | bytes 393224 | tf_op jit(solution)/shard_map/ppermute | solution.py:382
  83.3 1.6 %collective-permute-start.20 = (bf16[48,2048]{1,0:T(8,128)(2,1)S(1)}, bf16[48,2048]{1,0:T(8,128)(2,1)S(1)}, u32[]{:S(2)}, u32[]{:S(2)}) collective-permute-start(bf16[48,2048]{1,0:T(8,128)(2,1)S(1)} %shard_map.169), channel_id=1, source_target_pairs={{0,2},{1,3},{2,0},{3,1},{4,6},{5,7},{6,4},{7,5},{8,10},{9,11},{10,... | collective-permute-start | bytes 589832 | tf_op jit(solution)/shard_map/ppermute | solution.py:382
  84.9 0.3 collective-permute-done.31.cross_ref
  85.1 0.3 shard_map.177
  85.5 3.9 %collective-permute-done.22.cross_ref = bf16[96,1024]{1,0:T(8,128)(2,1)S(1)} collective-permute-done((bf16[96,1024]{1,0:T(8,128)(2,1)S(1)}, bf16[96,1024]{1,0:T(8,128)(2,1)S(1)}, u32[]{:S(2)}, u32[]{:S(2)}) %collective-permute-start.22) | collective-permute-done | bytes 196640 | tf_op jit(solution)/shard_map/ppermute | solution.py:382
  89.4 0.6 collective-permute-done.27.refs_0_
  89.9 0.3 shard_map.175
  90.2 1.5 %collective-permute-start.29 = (bf16[64,1024]{1,0:T(8,128)(2,1)S(1)}, bf16[64,1024]{1,0:T(8,128)(2,1)S(1)}, u32[]{:S(2)}, u32[]{:S(2)}) collective-permute-start(bf16[64,1024]{1,0:T(8,128)(2,1)S(1)} %get-tuple-element.109), channel_id=1, source_target_pairs={{0,4},{1,5},{2,6},{3,7},{4,12},{5,13},{6,14},{7,15},{12,8},{13,9},... | collective-permute-start | bytes 393224 | tf_op jit(solution)/shard_map/ppermute | solution.py:382
  91.7 1.5 %collective-permute-start.34 = (bf16[64,1024]{1,0:T(8,128)(2,1)S(1)}, bf16[64,1024]{1,0:T(8,128)(2,1)S(1)}, u32[]{:S(2)}, u32[]{:S(2)}) collective-permute-start(bf16[64,1024]{1,0:T(8,128)(2,1)S(1)} %get-tuple-element.115), channel_id=1, source_target_pairs={{4,0},{5,1},{6,2},{7,3},{12,4},{13,5},{14,6},{15,7},{8,12},{9,13},... | collective-permute-start | bytes 393224 | tf_op jit(solution)/shard_map/ppermute | solution.py:382
  93.2 4.5 %collective-permute-done.33.y_low = bf16[64,1024]{1,0:T(8,128)(2,1)S(1)} collective-permute-done((bf16[64,1024]{1,0:T(8,128)(2,1)S(1)}, bf16[64,1024]{1,0:T(8,128)(2,1)S(1)}, u32[]{:S(2)}, u32[]{:S(2)}) %collective-permute-start.33) | collective-permute-done | bytes 131104 | tf_op jit(solution)/shard_map/ppermute | solution.py:382
  97.7 1.4 %collective-permute-done.29.x_low = bf16[64,1024]{1,0:T(8,128)(2,1)S(1)} collective-permute-done((bf16[64,1024]{1,0:T(8,128)(2,1)S(1)}, bf16[64,1024]{1,0:T(8,128)(2,1)S(1)}, u32[]{:S(2)}, u32[]{:S(2)}) %collective-permute-start.29) | collective-permute-done | bytes 131104 | tf_op jit(solution)/shard_map/ppermute | solution.py:382
  99.2 0.8 collective-permute-done.34.y_high
  99.9 1.0 shard_map.178
  (63 shorter events, 0.8 us)
Async XLA Ops:
  0.6 23.4 %copy-start = (bf16[512,2048]{1,0:T(8,128)(2,1)S(1)}, bf16[512,2048]{1,0:T(8,128)(2,1)}, u32[]{:S(2)}) copy-start(bf16[512,2048]{1,0:T(8,128)(2,1)} %param.23) | copy-start | bytes 6291460
  0.6 13.3 %copy-start.8 = (bf16[1,64,512]{2,1,0:T(8,128)(2,1)S(1)}, bf16[1,64,512]{2,1,0:T(8,128)(2,1)}, u32[]{:S(2)}) copy-start(bf16[1,64,512]{2,1,0:T(8,128)(2,1)} %param.20) | copy-start | bytes 196612
  0.7 13.3 %copy-start.9 = (bf16[1,64,512]{2,1,0:T(8,128)(2,1)S(1)}, bf16[1,64,512]{2,1,0:T(8,128)(2,1)}, u32[]{:S(2)}) copy-start(bf16[1,64,512]{2,1,0:T(8,128)(2,1)} %param.18) | copy-start | bytes 196612
  1.5 15.2 %collective-permute-start.6 = (s32[6,64]{1,0:T(8,128)S(1)}, s32[6,64]{1,0:T(8,128)S(1)}, u32[]{:S(2)}, u32[]{:S(2)}) collective-permute-start(s32[6,64]{1,0:T(8,128)S(1)} %bitcast.53), channel_id=1, source_target_pairs={{0,12},{1,13},{2,14},{3,15},{4,8},{5,9},{6,10},{7,11},{8,4},{9,5},... | collective-permute-start | bytes 4616 | tf_op jit(solution)/shard_map/ppermute | solution.py:552
  6.6 10.1 %collective-permute-start.5 = (s32[6,64]{1,0:T(8,128)S(1)}, s32[6,64]{1,0:T(8,128)S(1)}, u32[]{:S(2)}, u32[]{:S(2)}) collective-permute-start(s32[6,64]{1,0:T(8,128)S(1)} %bitcast.54), channel_id=1, source_target_pairs={{4,0},{5,1},{6,2},{7,3},{12,4},{13,5},{14,6},{15,7},{8,12},{9,13},... | collective-permute-start | bytes 4616 | tf_op jit(solution)/shard_map/ppermute | solution.py:552
  6.6 10.2 %collective-permute-start.4 = (s32[6,64]{1,0:T(8,128)S(1)}, s32[6,64]{1,0:T(8,128)S(1)}, u32[]{:S(2)}, u32[]{:S(2)}) collective-permute-start(s32[6,64]{1,0:T(8,128)S(1)} %bitcast.55), channel_id=1, source_target_pairs={{0,4},{1,5},{2,6},{3,7},{4,12},{5,13},{6,14},{7,15},{12,8},{13,9},... | collective-permute-start | bytes 4616 | tf_op jit(solution)/shard_map/ppermute | solution.py:552
  9.6 5.0 %collective-permute-start = (bf16[128,4,128]{2,1,0:T(4,128)(2,1)S(1)}, bf16[128,4,128]{2,1,0:T(4,128)(2,1)S(1)}, u32[]{:S(2)}, u32[]{:S(2)}) collective-permute-start(bf16[128,4,128]{2,1,0:T(4,128)(2,1)S(1)} %constant_dynamic-slice_fusion.2), channel_id=1, source_target_pairs={{0,16},{16,0},{1,17},{17,1},{2,18},{18,2},{3,19},{19,3},{4,20},{20... | collective-permute-start | bytes 393224 | tf_op jit(solution)/shard_map/ppermute | solution.py:71
  12.6 3.9 %copy-start.7 = (bf16[256,8,128]{2,1,0:T(8,128)(2,1)S(1)}, bf16[256,8,128]{2,1,0:T(8,128)(2,1)}, u32[]{:S(2)}) copy-start(bf16[256,8,128]{2,1,0:T(8,128)(2,1)} %param.22) | copy-start | bytes 1572868
  14.7 2.3 %collective-permute-start.1 = (bf16[128,4,128]{2,1,0:T(4,128)(2,1)S(1)}, bf16[128,4,128]{2,1,0:T(4,128)(2,1)S(1)}, u32[]{:S(2)}, u32[]{:S(2)}) collective-permute-start(bf16[128,4,128]{2,1,0:T(4,128)(2,1)S(1)} %collective-permute-done), channel_id=1, source_target_pairs={{0,1},{1,0},{2,3},{3,2},{4,5},{5,4},{6,7},{7,6},{8,9},{9,8},{10,11... | collective-permute-start | bytes 393224 | tf_op jit(solution)/shard_map/ppermute | solution.py:79
  15.0 8.8 %collective-permute-start.2 = (bf16[64,4,512]{2,0,1:T(8,128)(2,1)S(1)}, bf16[64,4,512]{2,0,1:T(8,128)(2,1)S(1)}, u32[]{:S(2)}, u32[]{:S(2)}) collective-permute-start(bf16[64,4,512]{2,0,1:T(8,128)(2,1)S(1)} %copy.29), channel_id=1, source_target_pairs={{0,16},{16,0},{1,17},{17,1},{2,18},{18,2},{3,19},{19,3},{4,20},{20... | collective-permute-start | bytes 786440 | tf_op jit(solution)/shard_map/ppermute | solution.py:78
  24.0 8.5 %copy-start.4 = (bf16[1,64,2048]{2,1,0:T(8,128)(2,1)S(1)}, bf16[1,64,2048]{2,1,0:T(8,128)(2,1)}, u32[]{:S(2)}) copy-start(bf16[1,64,2048]{2,1,0:T(8,128)(2,1)} %x_ref.1) | copy-start | bytes 786436
  24.0 8.4 %copy-start.6 = (f32[2048]{0:T(1024)S(1)}, f32[2048]{0:T(1024)}, u32[]{:S(2)}) copy-start(f32[2048]{0:T(1024)} %param.24) | copy-start | bytes 24580
  24.1 42.5 %copy-start.3 = (bf16[1,704,2048]{2,1,0:T(8,128)(2,1)S(1)}, bf16[1,704,2048]{2,1,0:T(8,128)(2,1)}, u32[]{:S(2)}) copy-start(bf16[1,704,2048]{2,1,0:T(8,128)(2,1)} %param.29) | copy-start | bytes 8650756
  24.6 7.9 %collective-permute-start.3 = (bf16[64,2048]{1,0:T(8,128)(2,1)S(1)}, bf16[64,2048]{1,0:T(8,128)(2,1)S(1)}, u32[]{:S(2)}, u32[]{:S(2)}) collective-permute-start(bf16[64,2048]{1,0:T(8,128)(2,1)S(1)} %convolution_convert_fusion), channel_id=1, source_target_pairs={{0,16},{16,0},{1,17},{17,1},{2,18},{18,2},{3,19},{19,3},{4,20},{20... | collective-permute-start | bytes 786440 | tf_op jit(solution)/shard_map/ppermute | solution.py:86
  26.1 40.5 %copy-start.2 = (bf16[1,2048,704]{1,2,0:T(8,128)(2,1)S(1)}, bf16[1,2048,704]{1,2,0:T(8,128)(2,1)}, u32[]{:S(2)}) copy-start(bf16[1,2048,704]{1,2,0:T(8,128)(2,1)} %param.28) | copy-start | bytes 8650756
  26.6 39.4 %copy-start.5 = (bf16[2048,16]{0,1:T(8,128)(2,1)S(1)}, bf16[2048,16]{0,1:T(8,128)(2,1)}, u32[]{:S(2)}) copy-start(bf16[2048,16]{0,1:T(8,128)(2,1)} %param.25) | copy-start | bytes 196612
  33.3 7.9 %collective-permute-start.9 = (bf16[64,1024]{1,0:T(8,128)(2,1)S(1)}, bf16[64,1024]{1,0:T(8,128)(2,1)S(1)}, u32[]{:S(2)}, u32[]{:S(2)}) collective-permute-start(bf16[64,1024]{1,0:T(8,128)(2,1)S(1)} %get-tuple-element.67.refs_1_), channel_id=1, source_target_pairs={{0,4},{1,5},{2,6},{3,7},{4,12},{5,13},{6,14},{7,15},{12,8},{13,9},... | collective-permute-start | bytes 393224 | tf_op jit(solution)/shard_map/ppermute | solution.py:382
  33.8 32.8 %copy-start.1 = (bf16[1,2048,704]{1,2,0:T(8,128)(2,1)S(1)}, bf16[1,2048,704]{1,2,0:T(8,128)(2,1)}, u32[]{:S(2)}) copy-start(bf16[1,2048,704]{1,2,0:T(8,128)(2,1)} %param.27) | copy-start | bytes 8650756
  33.8 7.5 %collective-permute-start.12 = (bf16[64,1024]{1,0:T(8,128)(2,1)S(1)}, bf16[64,1024]{1,0:T(8,128)(2,1)S(1)}, u32[]{:S(2)}, u32[]{:S(2)}) collective-permute-start(bf16[64,1024]{1,0:T(8,128)(2,1)S(1)} %get-tuple-element.68.refs_2_), channel_id=1, source_target_pairs={{4,0},{5,1},{6,2},{7,3},{12,4},{13,5},{14,6},{15,7},{8,12},{9,13},... | collective-permute-start | bytes 393224 | tf_op jit(solution)/shard_map/ppermute | solution.py:382
  41.2 10.4 %collective-permute-start.13 = (bf16[64,1024]{1,0:T(8,128)(2,1)S(1)}, bf16[64,1024]{1,0:T(8,128)(2,1)S(1)}, u32[]{:S(2)}, u32[]{:S(2)}) collective-permute-start(bf16[64,1024]{1,0:T(8,128)(2,1)S(1)} %collective-permute-done.9.refs_4_.refs_1_), channel_id=1, source_target_pairs={{0,4},{1,5},{2,6},{3,7},{4,12},{5,13},{6,14},{7,15},{12,8},{13,9},... | collective-permute-start | bytes 393224 | tf_op jit(solution)/shard_map/ppermute | solution.py:382
  41.2 10.4 %collective-permute-start.14 = (bf16[64,1024]{1,0:T(8,128)(2,1)S(1)}, bf16[64,1024]{1,0:T(8,128)(2,1)S(1)}, u32[]{:S(2)}, u32[]{:S(2)}) collective-permute-start(bf16[64,1024]{1,0:T(8,128)(2,1)S(1)} %collective-permute-done.12.refs_8_.refs_3_), channel_id=1, source_target_pairs={{4,0},{5,1},{6,2},{7,3},{12,4},{13,5},{14,6},{15,7},{8,12},{9,13},... | collective-permute-start | bytes 393224 | tf_op jit(solution)/shard_map/ppermute | solution.py:382
  44.2 9.4 %collective-permute-start.11 = (bf16[64,1024]{1,0:T(8,128)(2,1)S(1)}, bf16[64,1024]{1,0:T(8,128)(2,1)S(1)}, u32[]{:S(2)}, u32[]{:S(2)}) collective-permute-start(bf16[64,1024]{1,0:T(8,128)(2,1)S(1)} %get-tuple-element.67.refs_1_), channel_id=1, source_target_pairs={{4,0},{5,1},{6,2},{7,3},{12,4},{13,5},{14,6},{15,7},{8,12},{9,13},... | collective-permute-start | bytes 393224 | tf_op jit(solution)/shard_map/ppermute | solution.py:382
  44.2 9.3 %collective-permute-start.10 = (bf16[64,1024]{1,0:T(8,128)(2,1)S(1)}, bf16[64,1024]{1,0:T(8,128)(2,1)S(1)}, u32[]{:S(2)}, u32[]{:S(2)}) collective-permute-start(bf16[64,1024]{1,0:T(8,128)(2,1)S(1)} %get-tuple-element.68.refs_2_), channel_id=1, source_target_pairs={{0,4},{1,5},{2,6},{3,7},{4,12},{5,13},{6,14},{7,15},{12,8},{13,9},... | collective-permute-start | bytes 393224 | tf_op jit(solution)/shard_map/ppermute | solution.py:382
  46.5 9.8 %collective-permute-start.7 = (bf16[48,2048]{1,0:T(8,128)(2,1)S(1)}, bf16[48,2048]{1,0:T(8,128)(2,1)S(1)}, u32[]{:S(2)}, u32[]{:S(2)}) collective-permute-start(bf16[48,2048]{1,0:T(8,128)(2,1)S(1)} %get-tuple-element.70), channel_id=1, source_target_pairs={{0,2},{1,3},{2,0},{3,1},{4,6},{5,7},{6,4},{7,5},{8,10},{9,11},{10,... | collective-permute-start | bytes 589832 | tf_op jit(solution)/shard_map/ppermute | solution.py:382
  51.9 7.8 %collective-permute-start.23 = (bf16[48,2048]{1,0:T(8,128)(2,1)S(1)}, bf16[48,2048]{1,0:T(8,128)(2,1)S(1)}, u32[]{:S(2)}, u32[]{:S(2)}) collective-permute-start(bf16[48,2048]{1,0:T(8,128)(2,1)S(1)} %get-tuple-element.102), channel_id=1, source_target_pairs={{0,2},{1,3},{2,0},{3,1},{4,6},{5,7},{6,4},{7,5},{8,10},{9,11},{10,... | collective-permute-start | bytes 589832 | tf_op jit(solution)/shard_map/ppermute | solution.py:382
  53.8 10.0 %collective-permute-start.17 = (bf16[96,1024]{1,0:T(8,128)(2,1)S(1)}, bf16[96,1024]{1,0:T(8,128)(2,1)S(1)}, u32[]{:S(2)}, u32[]{:S(2)}) collective-permute-start(bf16[96,1024]{1,0:T(8,128)(2,1)S(1)} %get-tuple-element.87), channel_id=1, source_target_pairs={{0,2},{1,3},{2,0},{3,1},{4,6},{5,7},{6,4},{7,5},{8,10},{9,11},{10,... | collective-permute-start | bytes 589832 | tf_op jit(solution)/shard_map/ppermute | solution.py:382
  55.6 10.2 %collective-permute-start.15 = (bf16[96,1024]{1,0:T(8,128)(2,1)S(1)}, bf16[96,1024]{1,0:T(8,128)(2,1)S(1)}, u32[]{:S(2)}, u32[]{:S(2)}) collective-permute-start(bf16[96,1024]{1,0:T(8,128)(2,1)S(1)} %get-tuple-element.84), channel_id=1, source_target_pairs={{0,2},{1,3},{2,0},{3,1},{4,6},{5,7},{6,4},{7,5},{8,10},{9,11},{10,... | collective-permute-start | bytes 589832 | tf_op jit(solution)/shard_map/ppermute | solution.py:382
  56.2 10.3 %collective-permute-start.8 = (bf16[48,2048]{1,0:T(8,128)(2,1)S(1)}, bf16[48,2048]{1,0:T(8,128)(2,1)S(1)}, u32[]{:S(2)}, u32[]{:S(2)}) collective-permute-start(bf16[48,2048]{1,0:T(8,128)(2,1)S(1)} %shard_map.161), channel_id=1, source_target_pairs={{0,1},{1,0},{2,3},{3,2},{4,5},{5,4},{6,7},{7,6},{8,9},{9,8},{10,11... | collective-permute-start | bytes 589832 | tf_op jit(solution)/shard_map/ppermute | solution.py:382
  59.8 6.8 %collective-permute-start.24 = (bf16[48,2048]{1,0:T(8,128)(2,1)S(1)}, bf16[48,2048]{1,0:T(8,128)(2,1)S(1)}, u32[]{:S(2)}, u32[]{:S(2)}) collective-permute-start(bf16[48,2048]{1,0:T(8,128)(2,1)S(1)} %shard_map.171), channel_id=1, source_target_pairs={{0,1},{1,0},{2,3},{3,2},{4,5},{5,4},{6,7},{7,6},{8,9},{9,8},{10,11... | collective-permute-start | bytes 589832 | tf_op jit(solution)/shard_map/ppermute | solution.py:382
  63.8 5.7 %collective-permute-start.18 = (bf16[96,1024]{1,0:T(8,128)(2,1)S(1)}, bf16[96,1024]{1,0:T(8,128)(2,1)S(1)}, u32[]{:S(2)}, u32[]{:S(2)}) collective-permute-start(bf16[96,1024]{1,0:T(8,128)(2,1)S(1)} %shard_map.167), channel_id=1, source_target_pairs={{0,1},{1,0},{2,3},{3,2},{4,5},{5,4},{6,7},{7,6},{8,9},{9,8},{10,11... | collective-permute-start | bytes 589832 | tf_op jit(solution)/shard_map/ppermute | solution.py:382
  65.9 3.6 %collective-permute-start.16 = (bf16[96,1024]{1,0:T(8,128)(2,1)S(1)}, bf16[96,1024]{1,0:T(8,128)(2,1)S(1)}, u32[]{:S(2)}, u32[]{:S(2)}) collective-permute-start(bf16[96,1024]{1,0:T(8,128)(2,1)S(1)} %shard_map.165), channel_id=1, source_target_pairs={{0,1},{1,0},{2,3},{3,2},{4,5},{5,4},{6,7},{7,6},{8,9},{9,8},{10,11... | collective-permute-start | bytes 589832 | tf_op jit(solution)/shard_map/ppermute | solution.py:382
  69.0 4.1 %collective-permute-start.25 = (bf16[48,2048]{1,0:T(8,128)(2,1)S(1)}, bf16[48,2048]{1,0:T(8,128)(2,1)S(1)}, u32[]{:S(2)}, u32[]{:S(2)}) collective-permute-start(bf16[48,2048]{1,0:T(8,128)(2,1)S(1)} %get-tuple-element.105), channel_id=1, source_target_pairs={{0,1},{1,0},{2,3},{3,2},{4,5},{5,4},{6,7},{7,6},{8,9},{9,8},{10,11... | collective-permute-start | bytes 589832 | tf_op jit(solution)/shard_map/ppermute | solution.py:382
  72.5 2.2 %collective-permute-start.30 = (bf16[96,1024]{1,0:T(8,128)(2,1)S(1)}, bf16[96,1024]{1,0:T(8,128)(2,1)S(1)}, u32[]{:S(2)}, u32[]{:S(2)}) collective-permute-start(bf16[96,1024]{1,0:T(8,128)(2,1)S(1)} %get-tuple-element.111), channel_id=1, source_target_pairs={{0,1},{1,0},{2,3},{3,2},{4,5},{5,4},{6,7},{7,6},{8,9},{9,8},{10,11... | collective-permute-start | bytes 589832 | tf_op jit(solution)/shard_map/ppermute | solution.py:382
  72.6 3.0 %collective-permute-start.21 = (bf16[96,1024]{1,0:T(8,128)(2,1)S(1)}, bf16[96,1024]{1,0:T(8,128)(2,1)S(1)}, u32[]{:S(2)}, u32[]{:S(2)}) collective-permute-start(bf16[96,1024]{1,0:T(8,128)(2,1)S(1)} %get-tuple-element.98), channel_id=1, source_target_pairs={{0,1},{1,0},{2,3},{3,2},{4,5},{5,4},{6,7},{7,6},{8,9},{9,8},{10,11... | collective-permute-start | bytes 589832 | tf_op jit(solution)/shard_map/ppermute | solution.py:382
  73.1 7.8 %collective-permute-start.26 = (bf16[48,2048]{1,0:T(8,128)(2,1)S(1)}, bf16[48,2048]{1,0:T(8,128)(2,1)S(1)}, u32[]{:S(2)}, u32[]{:S(2)}) collective-permute-start(bf16[48,2048]{1,0:T(8,128)(2,1)S(1)} %shard_map.173), channel_id=1, source_target_pairs={{0,2},{1,3},{2,0},{3,1},{4,6},{5,7},{6,4},{7,5},{8,10},{9,11},{10,... | collective-permute-start | bytes 589832 | tf_op jit(solution)/shard_map/ppermute | solution.py:382
  74.7 8.6 %collective-permute-start.19 = (bf16[48,2048]{1,0:T(8,128)(2,1)S(1)}, bf16[48,2048]{1,0:T(8,128)(2,1)S(1)}, u32[]{:S(2)}, u32[]{:S(2)}) collective-permute-start(bf16[48,2048]{1,0:T(8,128)(2,1)S(1)} %get-tuple-element.93), channel_id=1, source_target_pairs={{0,1},{1,0},{2,3},{3,2},{4,5},{5,4},{6,7},{7,6},{8,9},{9,8},{10,11... | collective-permute-start | bytes 589832 | tf_op jit(solution)/shard_map/ppermute | solution.py:382
  74.7 10.5 %collective-permute-start.31 = (bf16[96,1024]{1,0:T(8,128)(2,1)S(1)}, bf16[96,1024]{1,0:T(8,128)(2,1)S(1)}, u32[]{:S(2)}, u32[]{:S(2)}) collective-permute-start(bf16[96,1024]{1,0:T(8,128)(2,1)S(1)} %shard_map.176), channel_id=1, source_target_pairs={{0,2},{1,3},{2,0},{3,1},{4,6},{5,7},{6,4},{7,5},{8,10},{9,11},{10,... | collective-permute-start | bytes 589832 | tf_op jit(solution)/shard_map/ppermute | solution.py:382
  75.6 13.7 %collective-permute-start.22 = (bf16[96,1024]{1,0:T(8,128)(2,1)S(1)}, bf16[96,1024]{1,0:T(8,128)(2,1)S(1)}, u32[]{:S(2)}, u32[]{:S(2)}) collective-permute-start(bf16[96,1024]{1,0:T(8,128)(2,1)S(1)} %shard_map.170), channel_id=1, source_target_pairs={{0,2},{1,3},{2,0},{3,1},{4,6},{5,7},{6,4},{7,5},{8,10},{9,11},{10,... | collective-permute-start | bytes 589832 | tf_op jit(solution)/shard_map/ppermute | solution.py:382
  81.2 8.7 %collective-permute-start.27 = (bf16[64,1024]{1,0:T(8,128)(2,1)S(1)}, bf16[64,1024]{1,0:T(8,128)(2,1)S(1)}, u32[]{:S(2)}, u32[]{:S(2)}) collective-permute-start(bf16[64,1024]{1,0:T(8,128)(2,1)S(1)} %get-tuple-element.107), channel_id=1, source_target_pairs={{4,0},{5,1},{6,2},{7,3},{12,4},{13,5},{14,6},{15,7},{8,12},{9,13},... | collective-permute-start | bytes 393224 | tf_op jit(solution)/shard_map/ppermute | solution.py:382
  81.3 8.6 %collective-permute-start.28 = (bf16[64,1024]{1,0:T(8,128)(2,1)S(1)}, bf16[64,1024]{1,0:T(8,128)(2,1)S(1)}, u32[]{:S(2)}, u32[]{:S(2)}) collective-permute-start(bf16[64,1024]{1,0:T(8,128)(2,1)S(1)} %get-tuple-element.108), channel_id=1, source_target_pairs={{0,4},{1,5},{2,6},{3,7},{4,12},{5,13},{6,14},{7,15},{12,8},{13,9},... | collective-permute-start | bytes 393224 | tf_op jit(solution)/shard_map/ppermute | solution.py:382
  83.3 9.9 %collective-permute-start.20 = (bf16[48,2048]{1,0:T(8,128)(2,1)S(1)}, bf16[48,2048]{1,0:T(8,128)(2,1)S(1)}, u32[]{:S(2)}, u32[]{:S(2)}) collective-permute-start(bf16[48,2048]{1,0:T(8,128)(2,1)S(1)} %shard_map.169), channel_id=1, source_target_pairs={{0,2},{1,3},{2,0},{3,1},{4,6},{5,7},{6,4},{7,5},{8,10},{9,11},{10,... | collective-permute-start | bytes 589832 | tf_op jit(solution)/shard_map/ppermute | solution.py:382
  85.4 7.8 %collective-permute-start.32 = (bf16[64,1024]{1,0:T(8,128)(2,1)S(1)}, bf16[64,1024]{1,0:T(8,128)(2,1)S(1)}, u32[]{:S(2)}, u32[]{:S(2)}) collective-permute-start(bf16[64,1024]{1,0:T(8,128)(2,1)S(1)} %get-tuple-element.113), channel_id=1, source_target_pairs={{0,4},{1,5},{2,6},{3,7},{4,12},{5,13},{6,14},{7,15},{12,8},{13,9},... | collective-permute-start | bytes 393224 | tf_op jit(solution)/shard_map/ppermute | solution.py:382
  89.4 8.4 %collective-permute-start.33 = (bf16[64,1024]{1,0:T(8,128)(2,1)S(1)}, bf16[64,1024]{1,0:T(8,128)(2,1)S(1)}, u32[]{:S(2)}, u32[]{:S(2)}) collective-permute-start(bf16[64,1024]{1,0:T(8,128)(2,1)S(1)} %get-tuple-element.114), channel_id=1, source_target_pairs={{4,0},{5,1},{6,2},{7,3},{12,4},{13,5},{14,6},{15,7},{8,12},{9,13},... | collective-permute-start | bytes 393224 | tf_op jit(solution)/shard_map/ppermute | solution.py:382
  90.2 8.9 %collective-permute-start.29 = (bf16[64,1024]{1,0:T(8,128)(2,1)S(1)}, bf16[64,1024]{1,0:T(8,128)(2,1)S(1)}, u32[]{:S(2)}, u32[]{:S(2)}) collective-permute-start(bf16[64,1024]{1,0:T(8,128)(2,1)S(1)} %get-tuple-element.109), channel_id=1, source_target_pairs={{0,4},{1,5},{2,6},{3,7},{4,12},{5,13},{6,14},{7,15},{12,8},{13,9},... | collective-permute-start | bytes 393224 | tf_op jit(solution)/shard_map/ppermute | solution.py:382
  91.7 8.2 %collective-permute-start.34 = (bf16[64,1024]{1,0:T(8,128)(2,1)S(1)}, bf16[64,1024]{1,0:T(8,128)(2,1)S(1)}, u32[]{:S(2)}, u32[]{:S(2)}) collective-permute-start(bf16[64,1024]{1,0:T(8,128)(2,1)S(1)} %get-tuple-element.115), channel_id=1, source_target_pairs={{4,0},{5,1},{6,2},{7,3},{12,4},{13,5},{14,6},{15,7},{8,12},{9,13},... | collective-permute-start | bytes 393224 | tf_op jit(solution)/shard_map/ppermute | solution.py:382

commit v2 on v0

--- a/solution.py
+++ b/solution.py
@@ -62,26 +62,30 @@
     twins = [(i, i ^ 1) for i in range(ep)]
     side = lax.axis_index("fsdp")
     lane = lax.axis_index("ep") % 2
-    rows = w_uv.shape[0] // 2
+    rows, depth = w_uv.shape[0] // 2, w_uv.shape[2]
+    heads = w_out.shape[0] // depth
+
+    def own_heads(array, which):
+        return lax.dynamic_slice_in_dim(array, which * heads, heads, 1)
+
     mine = lax.ppermute(
-        lax.dynamic_slice_in_dim(w_uv, lane * rows, rows, 0), "fsdp", pair
-    )
+        lax.dynamic_slice(
+            w_uv, (lane * rows, (1 - side) * heads, 0), (rows, heads, depth)
+        ),
+        "fsdp",
+        pair,
+    )
+    other = lax.ppermute(own_heads(mixed_latent, 1 - side), "fsdp", pair)
     theirs = lax.ppermute(mine, "ep", twins)
     far = jnp.where(
         lane == 0, jnp.concatenate([mine, theirs], 0), jnp.concatenate([theirs, mine], 0)
     )
-    full = jnp.where(side == 0, jnp.concatenate([w_uv, far], 0), jnp.concatenate([far, w_uv], 0))
-    heads_flat = up_project(mixed_latent, full)
-    width = w_out.shape[0]
-    count = heads_flat.shape[0]
-    keep = lax.dynamic_slice_in_dim(heads_flat, side * width, width, 1)
-    give = lax.dynamic_slice_in_dim(heads_flat, (1 - side) * width, width, 1)
-    other = lax.ppermute(give, "fsdp", pair)
-    both = jnp.dot(
-        jnp.concatenate([other, keep], 0), w_out, preferred_element_type=jnp.float32
-    )
-    back = lax.ppermute(both[:count].astype(jnp.bfloat16), "fsdp", pair)
-    return both, back
+    near = own_heads(w_uv, side)
+    full = jnp.where(side == 0, jnp.concatenate([near, far], 0), jnp.concatenate([far, near], 0))
+    partial = jnp.dot(up_project(other, full), w_out, preferred_element_type=jnp.float32)
+    back = lax.ppermute(partial.astype(jnp.bfloat16), "fsdp", pair)
+    kept = up_project(own_heads(mixed_latent, side), full)
+    return jnp.dot(kept, w_out, preferred_element_type=jnp.float32), back
 
 
 def experts(rows, w_gate, w_up, w_down):
@@ -234,10 +238,10 @@
         out[n][...] = found.T
 
 
-def norm_kernel(x_ref, both_ref, back_ref, gain_ref, hidden_ref, attended_ref, low_ref, high_ref):
-    count, width = hidden_ref.shape
+def norm_kernel(x_ref, part_ref, back_ref, gain_ref, hidden_ref, attended_ref, low_ref, high_ref):
+    width = hidden_ref.shape[1]
     hidden = x_ref[0].astype(jnp.float32) + (
-        both_ref[count:] + back_ref[...].astype(jnp.float32)
+        part_ref[...] + back_ref[...].astype(jnp.float32)
     )
     hidden_ref[...] = hidden
     attended_ref[0] = hidden.astype(jnp.bfloat16)
@@ -359,7 +363,8 @@
         )
 
     def trade(blocks):
-        return [blocks[0]] + [send(blocks[j], traded[j]) for j in (1, 2, 3)]
+        across = [send(blocks[j], traded[j]) for j in (2, 3)]
+        return [blocks[0], send(blocks[1], traded[1])] + across
 
     own_slots, before_slots, after_slots, far_slots = targets
     before_low, after_high = send(low, onward), send(high, backward)
@@ -500,15 +505,16 @@
     onward, backward = ring_steps()
     ids = [expert_ids[0].T]
     across = [(i, i ^ 12) for i in range(16)]
-    ids += [lax.ppermute(ids[0], "ep", steps) for steps in (onward, backward, across)]
+    ids += [lax.ppermute(ids[0], "ep", steps) for steps in (onward, backward)]
+    ids.append(lax.ppermute(ids[0], "ep", across))
     targets = fused(
         functools.partial(slot_kernel, expert_count, capacity),
         [(part.shape, jnp.int32) for part in ids],
         *ids,
     )
-    both, back = project_paired(mixed_latent, w_uv, w_out)
+    part, back = project_paired(mixed_latent, w_uv, w_out)
     back, targets = lax.optimization_barrier((back, targets))
-    width = both.shape[1]
+    width = part.shape[1]
     halves = (new_count, width // 2)
     hidden, attended, low, high = fused(
         norm_kernel,
@@ -519,7 +525,7 @@
             (halves, jnp.bfloat16),
         ],
         x_resid,
-        both,
+        part,
         back,
         norm_gain[None],
         flops=8 * new_count * width,

time: 93 us -> 96.3 us (1.035)
  waiting for transfers between devices: 29.3 us -> 30.5 us
  local copies, waits for them, and re-layouts: 1.26 us -> 2.38 us
    ppermute x6, waiting for transfers between devices: 8.66 us -> 12 us  [the longest x1 5.87 us: project_paired(): back = lax.ppermute(partial.astype(jnp.bfloat16), 'fsdp', pair)]
    ppermute x1, waiting for transfers between devices: 1.1 us -> 0.01 us  [project_paired(): theirs = lax.ppermute(mine, 'ep', twins)]
    ppermute x36, waiting for transfers between devices: 19.6 us -> 18.5 us  [send(): return lax.ppermute(value, 'ep', steps)]
  transfers between devices with their start and end apart: 43 -> 43, of which waited for: 20 -> 17; matrix products, arithmetic and copies ran while one was open for 3% -> 6% of each run, Pallas kernels for 6% -> 6%
where the time goes in v2:
time: 96.3 us; the launch traced here: 96.1 us
  starting transfers between devices  47.1 us (49%)
  waiting for transfers between devices  30.5 us (32%)
  Pallas kernels  9.8 us (10%)
  matrix products  4.38 us (5%)
  local copies, waits for them, and re-layouts  2.38 us (2%)
  between operations  1.03 us (1%)
    ppermute x36, starting transfers between devices, send(): return lax.ppermute(value, 'ep', steps)  35.3 us
    ppermute x36, waiting for transfers between devices, send(): return lax.ppermute(value, 'ep', steps)  18.5 us
    pallas_call x13, Pallas kernels, fused(): pl.pallas_call(body, out_shape=[jax.ShapeDtypeStruct(shape, dtype) for sh...  9.8 us
    ppermute x1, waiting for transfers between devices, project_paired(): back = lax.ppermute(partial.astype(jnp.bfloat16), 'fsdp', pair)  5.87 us
    ppermute x1, waiting for transfers between devices, project_paired(): other = lax.ppermute(own_heads(mixed_latent, 1 - side), 'fsdp', pair)  5.7 us
    ppermute x1, starting transfers between devices, per_device(): ids.append(lax.ppermute(ids[0], 'ep', across))  5.08 us
    ppermute x2, starting transfers between devices, per_device(): ids += [lax.ppermute(ids[0], 'ep', steps) for steps in (onward, backward)]  2.03 us
  transfers between devices with their start and end apart: 43, of which 17 were waited for; matrix products, arithmetic and copies ran while one was open for 6% of the time, Pallas kernels for 6%

profile of v2, /device:TPU:0, one launch (start us, length us, event | category | flops | bytes accessed | tf_op | source)
XLA Modules:
  0.0 96.1 jit_solution(1522469165599071738)
XLA Ops:
  0.7 0.8 copy.47
  1.5 5.1 %collective-permute-start.6 = (s32[6,64]{1,0:T(8,128)S(1)}, s32[6,64]{1,0:T(8,128)S(1)}, u32[]{:S(2)}, u32[]{:S(2)}) collective-permute-start(s32[6,64]{1,0:T(8,128)S(1)} %bitcast.53), channel_id=1, source_target_pairs={{0,12},{1,13},{2,14},{3,15},{4,8},{5,9},{6,10},{7,11},{8,4},{9,5},... | collective-permute-start | bytes 4616 | tf_op jit(solution)/shard_map/ppermute | solution.py:509
  6.6 2.0 %collective-permute-start.4 = (s32[6,64]{1,0:T(8,128)S(1)}, s32[6,64]{1,0:T(8,128)S(1)}, u32[]{:S(2)}, u32[]{:S(2)}) collective-permute-start(s32[6,64]{1,0:T(8,128)S(1)} %bitcast.55), channel_id=1, source_target_pairs={{0,4},{1,5},{2,6},{3,7},{4,12},{5,13},{6,14},{7,15},{12,8},{13,9},... | collective-permute-start | bytes 4616 | tf_op jit(solution)/shard_map/ppermute | solution.py:508
  8.6 1.0 %constant_dynamic-slice_fusion.2 = bf16[128,4,128]{2,1,0:T(4,128)(2,1)S(1)} fusion(bf16[256,8,128]{2,1,0:T(8,128)(2,1)} %param.22, s32[]{:T(128)S(6)} %select_n.56, s32[]{:T(128)S(6)} %select_n.57), kind=kLoop, calls=%fused_computation.47 | loop fusion | bytes 262152 | tf_op jit(solution)/shard_map/dynamic_slice | solution.py:72
  9.6 1.6 %collective-permute-start = (bf16[128,4,128]{2,1,0:T(4,128)(2,1)S(1)}, bf16[128,4,128]{2,1,0:T(4,128)(2,1)S(1)}, u32[]{:S(2)}, u32[]{:S(2)}) collective-permute-start(bf16[128,4,128]{2,1,0:T(4,128)(2,1)S(1)} %constant_dynamic-slice_fusion.2), channel_id=1, source_target_pairs={{0,16},{16,0},{1,17},{17,1},{2,18},{18,2},{3,19},{19,3},{4,20},{20... | collective-permute-start | bytes 393224 | tf_op jit(solution)/shard_map/ppermute | solution.py:71
  11.2 1.4 %fusion.5 = f32[128,512]{1,0:T(8,128)S(1)} fusion(bf16[1,64,8,512]{3,2,1,0:T(8,128)(2,1)} %param.16, bf16[64,512]{1,0:T(8,128)(2,1)} %bitcast.59, bf16[64,512]{1,0:T(8,128)(2,1)} %bitcast.61), kind=kOutput, calls=%fused_computation.11 | convolution fusion | flops 67371008 | bytes 917504 | tf_op jit(solution)/shard_map/dot_general | solution.py:22
  12.6 1.2 %select_reduce_fusion = (f32[512]{0:T(512)S(1)}, f32[512,128]{0,1:T(8,128)S(1)}) fusion(s32[512]{0:T(512)S(1)} %fusion.24, f32[128,512]{1,0:T(8,128)S(1)} %fusion.5, bf16[1,64,8,64]{3,2,1,0:T(8,128)(2,1)} %param.17, bf16[64,64]{1,0:T(8,128)(2,1)} %bitcast.63, bf16[64,64]{1,0:T(8,128)(2,1)} %bitcast.64), kind=kOutput, calls=%fused_computation.19 | convolution fusion | flops 8748544 | bytes 610304 | tf_op jit(solution)/shard_map/dot_general | solution.py:24
  13.9 0.3 fusion
  14.3 0.4 collective-permute-done
  15.0 1.6 %collective-permute-start.2 = (bf16[64,4,512]{2,0,1:T(8,128)(2,1)S(1)}, bf16[64,4,512]{2,0,1:T(8,128)(2,1)S(1)}, u32[]{:S(2)}, u32[]{:S(2)}) collective-permute-start(bf16[64,4,512]{2,0,1:T(8,128)(2,1)S(1)} %copy.29), channel_id=1, source_target_pairs={{0,16},{16,0},{1,17},{17,1},{2,18},{18,2},{3,19},{19,3},{4,20},{20... | collective-permute-start | bytes 786440 | tf_op jit(solution)/shard_map/ppermute | solution.py:78
  16.9 0.3 maximum_select_fusion.1
  17.3 0.6 maximum_select_fusion
  18.1 5.7 %collective-permute-done.2 = bf16[64,4,512]{2,0,1:T(8,128)(2,1)S(1)} collective-permute-done((bf16[64,4,512]{2,0,1:T(8,128)(2,1)S(1)}, bf16[64,4,512]{2,0,1:T(8,128)(2,1)S(1)}, u32[]{:S(2)}, u32[]{:S(2)}) %collective-permute-start.2) | collective-permute-done | bytes 262176 | tf_op jit(solution)/shard_map/ppermute | solution.py:78
  24.0 0.5 convolution_convert_fusion
  24.5 1.6 %collective-permute-start.3 = (bf16[64,2048]{1,0:T(8,128)(2,1)S(1)}, bf16[64,2048]{1,0:T(8,128)(2,1)S(1)}, u32[]{:S(2)}, u32[]{:S(2)}) collective-permute-start(bf16[64,2048]{1,0:T(8,128)(2,1)S(1)} %convolution_convert_fusion), channel_id=1, source_target_pairs={{0,16},{16,0},{1,17},{17,1},{2,18},{18,2},{3,19},{19,3},{4,20},{20... | collective-permute-start | bytes 786440 | tf_op jit(solution)/shard_map/ppermute | solution.py:86
  26.1 0.5 fusion.18.part_ref
  26.6 5.9 %collective-permute-done.3.back_ref = bf16[64,2048]{1,0:T(8,128)(2,1)S(1)} collective-permute-done((bf16[64,2048]{1,0:T(8,128)(2,1)S(1)}, bf16[64,2048]{1,0:T(8,128)(2,1)S(1)}, u32[]{:S(2)}, u32[]{:S(2)}) %collective-permute-start.3) | collective-permute-done | bytes 262176 | tf_op jit(solution)/shard_map/ppermute | solution.py:86
  32.5 0.8 shard_map.159
  33.3 0.9 collective-permute-start.13
  34.2 1.1 %collective-permute-start.12 = (bf16[64,1024]{1,0:T(8,128)(2,1)S(1)}, bf16[64,1024]{1,0:T(8,128)(2,1)S(1)}, u32[]{:S(2)}, u32[]{:S(2)}) collective-permute-start(bf16[64,1024]{1,0:T(8,128)(2,1)S(1)} %get-tuple-element.99.refs_1_), channel_id=1, source_target_pairs={{0,4},{1,5},{2,6},{3,7},{4,12},{5,13},{6,14},{7,15},{12,8},{13,9},... | collective-permute-start | bytes 393224 | tf_op jit(solution)/shard_map/ppermute | solution.py:352
  35.7 1.6 %collective-permute-start.10 = (bf16[24,2048]{1,0:T(8,128)(2,1)S(1)}, bf16[24,2048]{1,0:T(8,128)(2,1)S(1)}, u32[]{:S(2)}, u32[]{:S(2)}) collective-permute-start(bf16[24,2048]{1,0:T(8,128)(2,1)S(1)} %get-tuple-element.103), channel_id=1, source_target_pairs={{0,2},{1,3},{2,0},{3,1},{4,6},{5,7},{6,4},{7,5},{8,10},{9,11},{10,... | collective-permute-start | bytes 294920 | tf_op jit(solution)/shard_map/ppermute | solution.py:352
  37.6 1.3 %collective-permute-start.7 = (bf16[64,1024]{1,0:T(8,128)(2,1)S(1)}, bf16[64,1024]{1,0:T(8,128)(2,1)S(1)}, u32[]{:S(2)}, u32[]{:S(2)}) collective-permute-start(bf16[64,1024]{1,0:T(8,128)(2,1)S(1)} %get-tuple-element.98.refs_2_), channel_id=1, source_target_pairs={{0,4},{1,5},{2,6},{3,7},{4,12},{5,13},{6,14},{7,15},{12,8},{13,9},... | collective-permute-start | bytes 393224 | tf_op jit(solution)/shard_map/ppermute | solution.py:352
  38.9 2.5 %collective-permute-done.10.refs_10_ = bf16[24,2048]{1,0:T(8,128)(2,1)S(1)} collective-permute-done((bf16[24,2048]{1,0:T(8,128)(2,1)S(1)}, bf16[24,2048]{1,0:T(8,128)(2,1)S(1)}, u32[]{:S(2)}, u32[]{:S(2)}) %collective-permute-start.10) | collective-permute-done | bytes 98336 | tf_op jit(solution)/shard_map/ppermute | solution.py:352
  41.4 1.8 %collective-permute-start.8 = (bf16[64,1024]{1,0:T(8,128)(2,1)S(1)}, bf16[64,1024]{1,0:T(8,128)(2,1)S(1)}, u32[]{:S(2)}, u32[]{:S(2)}) collective-permute-start(bf16[64,1024]{1,0:T(8,128)(2,1)S(1)} %get-tuple-element.99.refs_1_), channel_id=1, source_target_pairs={{4,0},{5,1},{6,2},{7,3},{12,4},{13,5},{14,6},{15,7},{8,12},{9,13},... | collective-permute-start | bytes 393224 | tf_op jit(solution)/shard_map/ppermute | solution.py:352
  43.3 2.0 %collective-permute-start.14 = (bf16[64,1024]{1,0:T(8,128)(2,1)S(1)}, bf16[64,1024]{1,0:T(8,128)(2,1)S(1)}, u32[]{:S(2)}, u32[]{:S(2)}) collective-permute-start(bf16[64,1024]{1,0:T(8,128)(2,1)S(1)} %collective-permute-done.12.refs_1_.refs_4_), channel_id=1, source_target_pairs={{0,4},{1,5},{2,6},{3,7},{4,12},{5,13},{6,14},{7,15},{12,8},{13,9},... | collective-permute-start | bytes 393224 | tf_op jit(solution)/shard_map/ppermute | solution.py:352
  45.7 1.6 %collective-permute-start.17 = (bf16[48,1024]{1,0:T(8,128)(2,1)S(1)}, bf16[48,1024]{1,0:T(8,128)(2,1)S(1)}, u32[]{:S(2)}, u32[]{:S(2)}) collective-permute-start(bf16[48,1024]{1,0:T(8,128)(2,1)S(1)} %get-tuple-element.125), channel_id=1, source_target_pairs={{0,2},{1,3},{2,0},{3,1},{4,6},{5,7},{6,4},{7,5},{8,10},{9,11},{10,... | collective-permute-start | bytes 294920 | tf_op jit(solution)/shard_map/ppermute | solution.py:352
  47.2 0.7 collective-permute-done.8.refs_7_.refs_3_
  48.2 1.7 %collective-permute-start.19 = (bf16[48,1024]{1,0:T(8,128)(2,1)S(1)}, bf16[48,1024]{1,0:T(8,128)(2,1)S(1)}, u32[]{:S(2)}, u32[]{:S(2)}) collective-permute-start(bf16[48,1024]{1,0:T(8,128)(2,1)S(1)} %get-tuple-element.128), channel_id=1, source_target_pairs={{0,1},{1,0},{2,3},{3,2},{4,5},{5,4},{6,7},{7,6},{8,9},{9,8},{10,11... | collective-permute-start | bytes 294920 | tf_op jit(solution)/shard_map/ppermute | solution.py:352
  49.9 1.4 %collective-permute-done.15.refs_2_.refs_11_ = bf16[64,1024]{1,0:T(8,128)(2,1)S(1)} collective-permute-done((bf16[64,1024]{1,0:T(8,128)(2,1)S(1)}, bf16[64,1024]{1,0:T(8,128)(2,1)S(1)}, u32[]{:S(2)}, u32[]{:S(2)}) %collective-permute-start.15) | collective-permute-done | bytes 131104 | tf_op jit(solution)/shard_map/ppermute | solution.py:352
  51.3 1.5 %collective-permute-start.20 = (bf16[48,1024]{1,0:T(8,128)(2,1)S(1)}, bf16[48,1024]{1,0:T(8,128)(2,1)S(1)}, u32[]{:S(2)}, u32[]{:S(2)}) collective-permute-start(bf16[48,1024]{1,0:T(8,128)(2,1)S(1)} %get-tuple-element.129), channel_id=1, source_target_pairs={{0,2},{1,3},{2,0},{3,1},{4,6},{5,7},{6,4},{7,5},{8,10},{9,11},{10,... | collective-permute-start | bytes 294920 | tf_op jit(solution)/shard_map/ppermute | solution.py:352
  52.8 0.4 collective-permute-done.14.refs_1_.refs_10_
  53.2 1.1 %collective-permute-start.21 = (bf16[48,1024]{1,0:T(8,128)(2,1)S(1)}, bf16[48,1024]{1,0:T(8,128)(2,1)S(1)}, u32[]{:S(2)}, u32[]{:S(2)}) collective-permute-start(bf16[48,1024]{1,0:T(8,128)(2,1)S(1)} %get-tuple-element.130), channel_id=1, source_target_pairs={{0,3},{1,2},{2,1},{3,0},{4,7},{5,6},{6,5},{7,4},{8,11},{9,10},{10,... | collective-permute-start | bytes 294920 | tf_op jit(solution)/shard_map/ppermute | solution.py:352
  54.6 0.5 shard_map.163
  55.1 0.6 collective-permute-start.22
  55.7 0.5 collective-permute-start.23
  56.2 0.9 collective-permute-start.24
  57.2 0.9 collective-permute-done.21.refs_7_
  58.1 3.0 %shard_map.165 = (bf16[48,1024]{1,0:T(8,128)(2,1)S(1)}, bf16[48,1024]{1,0:T(8,128)(2,1)S(1)}, bf16[48,1024]{1,0:T(8,128)(2,1)S(1)}, bf16[48,1024]{1,0:T(8,128)(2...) custom-call(bf16[48,1024]{1,0:T(8,128)(2,1)S(1)} %get-tuple-element., ...), custom_call_target="tpu_custom_call" | custom-call | flops 2491416576 | bytes 11010048 | tf_op jit(solution)/shard_map/pallas_call | solution.py:142
  61.1 0.3 collective-permute-done.23.refs_2_
  61.4 0.3 collective-permute-done.24.refs_3_
  61.7 2.4 %shard_map.166 = (bf16[24,2048]{1,0:T(8,128)(2,1)S(1)}, bf16[24,2048]{1,0:T(8,128)(2,1)S(1)}, bf16[24,2048]{1,0:T(8,128)(2,1)S(1)}, bf16[24,2048]{1,0:T(8,128)(2,1)S(1)}) custom-call(bf16[24,2048]{1,0:T(8,128)(2,1)S(1)} %get-tuple-element.162.refs_0_, bf16[24,2048]{1,0:T(8,128)(2,1)S(1)} %collective-permute-done.22.refs_1_, ...), custom_call_target="tpu_custom_call" | custom-call | flops 830472192 | bytes 9437184 | tf_op jit(solution)/shard_map/pallas_call | solution.py:142
  64.1 0.8 collective-permute-start.31
  64.9 1.5 %collective-permute-start.32 = (bf16[24,2048]{1,0:T(8,128)(2,1)S(1)}, bf16[24,2048]{1,0:T(8,128)(2,1)S(1)}, u32[]{:S(2)}, u32[]{:S(2)}) collective-permute-start(bf16[24,2048]{1,0:T(8,128)(2,1)S(1)} %get-tuple-element.168), channel_id=1, source_target_pairs={{0,2},{1,3},{2,0},{3,1},{4,6},{5,7},{6,4},{7,5},{8,10},{9,11},{10,... | collective-permute-start | bytes 294920 | tf_op jit(solution)/shard_map/ppermute | solution.py:352
  66.4 0.6 collective-permute-start.28
  67.0 1.5 %collective-permute-start.29 = (bf16[48,1024]{1,0:T(8,128)(2,1)S(1)}, bf16[48,1024]{1,0:T(8,128)(2,1)S(1)}, u32[]{:S(2)}, u32[]{:S(2)}) collective-permute-start(bf16[48,1024]{1,0:T(8,128)(2,1)S(1)} %get-tuple-element.159), channel_id=1, source_target_pairs={{0,2},{1,3},{2,0},{3,1},{4,6},{5,7},{6,4},{7,5},{8,10},{9,11},{10,... | collective-permute-start | bytes 294920 | tf_op jit(solution)/shard_map/ppermute | solution.py:352
  68.5 1.6 %collective-permute-done.32.r2 = bf16[24,2048]{1,0:T(8,128)(2,1)S(1)} collective-permute-done((bf16[24,2048]{1,0:T(8,128)(2,1)S(1)}, bf16[24,2048]{1,0:T(8,128)(2,1)S(1)}, u32[]{:S(2)}, u32[]{:S(2)}) %collective-permute-start.32) | collective-permute-done | bytes 98336 | tf_op jit(solution)/shard_map/ppermute | solution.py:352
  70.1 2.0 %collective-permute-start.38 = (bf16[48,1024]{1,0:T(8,128)(2,1)S(1)}, bf16[48,1024]{1,0:T(8,128)(2,1)S(1)}, u32[]{:S(2)}, u32[]{:S(2)}) collective-permute-start(bf16[48,1024]{1,0:T(8,128)(2,1)S(1)} %get-tuple-element.175), channel_id=1, source_target_pairs={{0,2},{1,3},{2,0},{3,1},{4,6},{5,7},{6,4},{7,5},{8,10},{9,11},{10,... | collective-permute-start | bytes 294920 | tf_op jit(solution)/shard_map/ppermute | solution.py:352
  72.1 1.5 %collective-permute-start.39 = (bf16[48,1024]{1,0:T(8,128)(2,1)S(1)}, bf16[48,1024]{1,0:T(8,128)(2,1)S(1)}, u32[]{:S(2)}, u32[]{:S(2)}) collective-permute-start(bf16[48,1024]{1,0:T(8,128)(2,1)S(1)} %get-tuple-element.176), channel_id=1, source_target_pairs={{0,3},{1,2},{2,1},{3,0},{4,7},{5,6},{6,5},{7,4},{8,11},{9,10},{10,... | collective-permute-start | bytes 294920 | tf_op jit(solution)/shard_map/ppermute | solution.py:352
  73.9 1.2 %collective-permute-start.34 = (bf16[64,1024]{1,0:T(8,128)(2,1)S(1)}, bf16[64,1024]{1,0:T(8,128)(2,1)S(1)}, u32[]{:S(2)}, u32[]{:S(2)}) collective-permute-start(bf16[64,1024]{1,0:T(8,128)(2,1)S(1)} %get-tuple-element.170), channel_id=1, source_target_pairs={{4,0},{5,1},{6,2},{7,3},{12,4},{13,5},{14,6},{15,7},{8,12},{9,13},... | collective-permute-start | bytes 393224 | tf_op jit(solution)/shard_map/ppermute | solution.py:352
  75.1 0.8 collective-permute-start.35
  76.0 0.5 collective-permute-done.38.r2
  76.4 0.7 collective-permute-start.25
  77.1 0.7 collective-permute-done.39.r3
  77.8 1.5 %collective-permute-start.26 = (bf16[24,2048]{1,0:T(8,128)(2,1)S(1)}, bf16[24,2048]{1,0:T(8,128)(2,1)S(1)}, u32[]{:S(2)}, u32[]{:S(2)}) collective-permute-start(bf16[24,2048]{1,0:T(8,128)(2,1)S(1)} %get-tuple-element.153), channel_id=1, source_target_pairs={{0,2},{1,3},{2,0},{3,1},{4,6},{5,7},{6,4},{7,5},{8,10},{9,11},{10,... | collective-permute-start | bytes 294920 | tf_op jit(solution)/shard_map/ppermute | solution.py:352
  79.3 0.3 shard_map.169
  79.6 1.0 %collective-permute-done.30.r3 = bf16[48,1024]{1,0:T(8,128)(2,1)S(1)} collective-permute-done((bf16[48,1024]{1,0:T(8,128)(2,1)S(1)}, bf16[48,1024]{1,0:T(8,128)(2,1)S(1)}, u32[]{:S(2)}, u32[]{:S(2)}) %collective-permute-start.30) | collective-permute-done | bytes 98336 | tf_op jit(solution)/shard_map/ppermute | solution.py:352
  80.7 1.7 %collective-permute-start.40 = (bf16[64,1024]{1,0:T(8,128)(2,1)S(1)}, bf16[64,1024]{1,0:T(8,128)(2,1)S(1)}, u32[]{:S(2)}, u32[]{:S(2)}) collective-permute-start(bf16[64,1024]{1,0:T(8,128)(2,1)S(1)} %get-tuple-element.177), channel_id=1, source_target_pairs={{0,4},{1,5},{2,6},{3,7},{4,12},{5,13},{6,14},{7,15},{12,8},{13,9},... | collective-permute-start | bytes 393224 | tf_op jit(solution)/shard_map/ppermute | solution.py:352
  82.4 1.2 %collective-permute-start.41 = (bf16[64,1024]{1,0:T(8,128)(2,1)S(1)}, bf16[64,1024]{1,0:T(8,128)(2,1)S(1)}, u32[]{:S(2)}, u32[]{:S(2)}) collective-permute-start(bf16[64,1024]{1,0:T(8,128)(2,1)S(1)} %get-tuple-element.178), channel_id=1, source_target_pairs={{4,0},{5,1},{6,2},{7,3},{12,4},{13,5},{14,6},{15,7},{8,12},{9,13},... | collective-permute-start | bytes 393224 | tf_op jit(solution)/shard_map/ppermute | solution.py:352
  83.9 0.9 collective-permute-start.36
  84.8 2.1 %collective-permute-start.42 = (bf16[64,1024]{1,0:T(8,128)(2,1)S(1)}, bf16[64,1024]{1,0:T(8,128)(2,1)S(1)}, u32[]{:S(2)}, u32[]{:S(2)}) collective-permute-start(bf16[64,1024]{1,0:T(8,128)(2,1)S(1)} %get-tuple-element.179), channel_id=1, source_target_pairs={{4,0},{5,1},{6,2},{7,3},{12,4},{13,5},{14,6},{15,7},{8,12},{9,13},... | collective-permute-start | bytes 393224 | tf_op jit(solution)/shard_map/ppermute | solution.py:352
  86.9 5.0 %collective-permute-done.27.r3 = bf16[24,2048]{1,0:T(8,128)(2,1)S(1)} collective-permute-done((bf16[24,2048]{1,0:T(8,128)(2,1)S(1)}, bf16[24,2048]{1,0:T(8,128)(2,1)S(1)}, u32[]{:S(2)}, u32[]{:S(2)}) %collective-permute-start.27) | collective-permute-done | bytes 98336 | tf_op jit(solution)/shard_map/ppermute | solution.py:352
  91.9 0.8 collective-permute-done.36.x_low
  92.7 2.4 %collective-permute-done.42.y_high = bf16[64,1024]{1,0:T(8,128)(2,1)S(1)} collective-permute-done((bf16[64,1024]{1,0:T(8,128)(2,1)S(1)}, bf16[64,1024]{1,0:T(8,128)(2,1)S(1)}, u32[]{:S(2)}, u32[]{:S(2)}) %collective-permute-start.42) | collective-permute-done | bytes 131104 | tf_op jit(solution)/shard_map/ppermute | solution.py:352
  95.1 1.0 %shard_map.170 = bf16[64,2048]{1,0:T(8,128)(2,1)} custom-call(f32[64,2048]{1,0:T(8,128)S(1)} %get-tuple-element.97.hidden_ref, f32[64,96]{1,0:T(8,128)S(1)} %get-tuple-element.122.weights_ref, bf16[24,2048]{1,0:T(8,128)(2,1)S(1)} %get-tuple-element.151.r0, bf16[24,2048]{1,0:T(8,128)(2,1)S(1)} %collective-permute-done.25.r1, ...), custom_call_target="tpu_custom_call" | custom-call | flops 100663296 | bytes 2621440 | tf_op jit(solution)/shard_map/pallas_call | solution.py:142
  (71 shorter events, 3.4 us)
Async XLA Ops:
  0.6 23.4 %copy-start = (bf16[512,2048]{1,0:T(8,128)(2,1)S(1)}, bf16[512,2048]{1,0:T(8,128)(2,1)}, u32[]{:S(2)}) copy-start(bf16[512,2048]{1,0:T(8,128)(2,1)} %param.23) | copy-start | bytes 6291460
  0.6 13.3 %copy-start.8 = (bf16[1,64,512]{2,1,0:T(8,128)(2,1)S(1)}, bf16[1,64,512]{2,1,0:T(8,128)(2,1)}, u32[]{:S(2)}) copy-start(bf16[1,64,512]{2,1,0:T(8,128)(2,1)} %param.20) | copy-start | bytes 196612
  0.7 13.3 %copy-start.9 = (bf16[1,64,512]{2,1,0:T(8,128)(2,1)S(1)}, bf16[1,64,512]{2,1,0:T(8,128)(2,1)}, u32[]{:S(2)}) copy-start(bf16[1,64,512]{2,1,0:T(8,128)(2,1)} %param.18) | copy-start | bytes 196612
  1.5 15.2 %collective-permute-start.6 = (s32[6,64]{1,0:T(8,128)S(1)}, s32[6,64]{1,0:T(8,128)S(1)}, u32[]{:S(2)}, u32[]{:S(2)}) collective-permute-start(s32[6,64]{1,0:T(8,128)S(1)} %bitcast.53), channel_id=1, source_target_pairs={{0,12},{1,13},{2,14},{3,15},{4,8},{5,9},{6,10},{7,11},{8,4},{9,5},... | collective-permute-start | bytes 4616 | tf_op jit(solution)/shard_map/ppermute | solution.py:509
  6.6 10.1 %collective-permute-start.5 = (s32[6,64]{1,0:T(8,128)S(1)}, s32[6,64]{1,0:T(8,128)S(1)}, u32[]{:S(2)}, u32[]{:S(2)}) collective-permute-start(s32[6,64]{1,0:T(8,128)S(1)} %bitcast.54), channel_id=1, source_target_pairs={{4,0},{5,1},{6,2},{7,3},{12,4},{13,5},{14,6},{15,7},{8,12},{9,13},... | collective-permute-start | bytes 4616 | tf_op jit(solution)/shard_map/ppermute | solution.py:508
  6.6 10.2 %collective-permute-start.4 = (s32[6,64]{1,0:T(8,128)S(1)}, s32[6,64]{1,0:T(8,128)S(1)}, u32[]{:S(2)}, u32[]{:S(2)}) collective-permute-start(s32[6,64]{1,0:T(8,128)S(1)} %bitcast.55), channel_id=1, source_target_pairs={{0,4},{1,5},{2,6},{3,7},{4,12},{5,13},{6,14},{7,15},{12,8},{13,9},... | collective-permute-start | bytes 4616 | tf_op jit(solution)/shard_map/ppermute | solution.py:508
  9.6 5.0 %collective-permute-start = (bf16[128,4,128]{2,1,0:T(4,128)(2,1)S(1)}, bf16[128,4,128]{2,1,0:T(4,128)(2,1)S(1)}, u32[]{:S(2)}, u32[]{:S(2)}) collective-permute-start(bf16[128,4,128]{2,1,0:T(4,128)(2,1)S(1)} %constant_dynamic-slice_fusion.2), channel_id=1, source_target_pairs={{0,16},{16,0},{1,17},{17,1},{2,18},{18,2},{3,19},{19,3},{4,20},{20... | collective-permute-start | bytes 393224 | tf_op jit(solution)/shard_map/ppermute | solution.py:71
  12.6 3.9 %copy-start.7 = (bf16[256,8,128]{2,1,0:T(8,128)(2,1)S(1)}, bf16[256,8,128]{2,1,0:T(8,128)(2,1)}, u32[]{:S(2)}) copy-start(bf16[256,8,128]{2,1,0:T(8,128)(2,1)} %param.22) | copy-start | bytes 1572868
  14.7 2.3 %collective-permute-start.1 = (bf16[128,4,128]{2,1,0:T(4,128)(2,1)S(1)}, bf16[128,4,128]{2,1,0:T(4,128)(2,1)S(1)}, u32[]{:S(2)}, u32[]{:S(2)}) collective-permute-start(bf16[128,4,128]{2,1,0:T(4,128)(2,1)S(1)} %collective-permute-done), channel_id=1, source_target_pairs={{0,1},{1,0},{2,3},{3,2},{4,5},{5,4},{6,7},{7,6},{8,9},{9,8},{10,11... | collective-permute-start | bytes 393224 | tf_op jit(solution)/shard_map/ppermute | solution.py:79
  15.0 8.8 %collective-permute-start.2 = (bf16[64,4,512]{2,0,1:T(8,128)(2,1)S(1)}, bf16[64,4,512]{2,0,1:T(8,128)(2,1)S(1)}, u32[]{:S(2)}, u32[]{:S(2)}) collective-permute-start(bf16[64,4,512]{2,0,1:T(8,128)(2,1)S(1)} %copy.29), channel_id=1, source_target_pairs={{0,16},{16,0},{1,17},{17,1},{2,18},{18,2},{3,19},{19,3},{4,20},{20... | collective-permute-start | bytes 786440 | tf_op jit(solution)/shard_map/ppermute | solution.py:78
  23.8 34.3 %copy-start.3 = (bf16[1,704,2048]{2,1,0:T(8,128)(2,1)S(1)}, bf16[1,704,2048]{2,1,0:T(8,128)(2,1)}, u32[]{:S(2)}) copy-start(bf16[1,704,2048]{2,1,0:T(8,128)(2,1)} %param.29) | copy-start | bytes 8650756
  24.0 8.5 %copy-start.4 = (bf16[1,64,2048]{2,1,0:T(8,128)(2,1)S(1)}, bf16[1,64,2048]{2,1,0:T(8,128)(2,1)}, u32[]{:S(2)}) copy-start(bf16[1,64,2048]{2,1,0:T(8,128)(2,1)} %x_ref.1) | copy-start | bytes 786436
  24.0 8.4 %copy-start.6 = (f32[2048]{0:T(1024)S(1)}, f32[2048]{0:T(1024)}, u32[]{:S(2)}) copy-start(f32[2048]{0:T(1024)} %param.24) | copy-start | bytes 24580
  24.5 30.0 %copy-start.5 = (bf16[2048,16]{0,1:T(8,128)(2,1)S(1)}, bf16[2048,16]{0,1:T(8,128)(2,1)}, u32[]{:S(2)}) copy-start(bf16[2048,16]{0,1:T(8,128)(2,1)} %param.25) | copy-start | bytes 196612
  24.5 7.9 %collective-permute-start.3 = (bf16[64,2048]{1,0:T(8,128)(2,1)S(1)}, bf16[64,2048]{1,0:T(8,128)(2,1)S(1)}, u32[]{:S(2)}, u32[]{:S(2)}) collective-permute-start(bf16[64,2048]{1,0:T(8,128)(2,1)S(1)} %convolution_convert_fusion), channel_id=1, source_target_pairs={{0,16},{16,0},{1,17},{17,1},{2,18},{18,2},{3,19},{19,3},{4,20},{20... | collective-permute-start | bytes 786440 | tf_op jit(solution)/shard_map/ppermute | solution.py:86
  26.1 32.0 %copy-start.2 = (bf16[1,2048,704]{1,2,0:T(8,128)(2,1)S(1)}, bf16[1,2048,704]{1,2,0:T(8,128)(2,1)}, u32[]{:S(2)}) copy-start(bf16[1,2048,704]{1,2,0:T(8,128)(2,1)} %param.28) | copy-start | bytes 8650756
  26.6 31.5 %copy-start.1 = (bf16[1,2048,704]{1,2,0:T(8,128)(2,1)S(1)}, bf16[1,2048,704]{1,2,0:T(8,128)(2,1)}, u32[]{:S(2)}) copy-start(bf16[1,2048,704]{1,2,0:T(8,128)(2,1)} %param.27) | copy-start | bytes 8650756
  33.3 9.9 %collective-permute-start.13 = (bf16[64,1024]{1,0:T(8,128)(2,1)S(1)}, bf16[64,1024]{1,0:T(8,128)(2,1)S(1)}, u32[]{:S(2)}, u32[]{:S(2)}) collective-permute-start(bf16[64,1024]{1,0:T(8,128)(2,1)S(1)} %get-tuple-element.98.refs_2_), channel_id=1, source_target_pairs={{4,0},{5,1},{6,2},{7,3},{12,4},{13,5},{14,6},{15,7},{8,12},{9,13},... | collective-permute-start | bytes 393224 | tf_op jit(solution)/shard_map/ppermute | solution.py:352
  34.2 9.0 %collective-permute-start.12 = (bf16[64,1024]{1,0:T(8,128)(2,1)S(1)}, bf16[64,1024]{1,0:T(8,128)(2,1)S(1)}, u32[]{:S(2)}, u32[]{:S(2)}) collective-permute-start(bf16[64,1024]{1,0:T(8,128)(2,1)S(1)} %get-tuple-element.99.refs_1_), channel_id=1, source_target_pairs={{0,4},{1,5},{2,6},{3,7},{4,12},{5,13},{6,14},{7,15},{12,8},{13,9},... | collective-permute-start | bytes 393224 | tf_op jit(solution)/shard_map/ppermute | solution.py:352
  35.6 1.9 %collective-permute-start.9 = (bf16[24,2048]{1,0:T(8,128)(2,1)S(1)}, bf16[24,2048]{1,0:T(8,128)(2,1)S(1)}, u32[]{:S(2)}, u32[]{:S(2)}) collective-permute-start(bf16[24,2048]{1,0:T(8,128)(2,1)S(1)} %get-tuple-element.102), channel_id=1, source_target_pairs={{0,1},{1,0},{2,3},{3,2},{4,5},{5,4},{6,7},{7,6},{8,9},{9,8},{10,11... | collective-permute-start | bytes 294920 | tf_op jit(solution)/shard_map/ppermute | solution.py:352
  35.7 5.7 %collective-permute-start.10 = (bf16[24,2048]{1,0:T(8,128)(2,1)S(1)}, bf16[24,2048]{1,0:T(8,128)(2,1)S(1)}, u32[]{:S(2)}, u32[]{:S(2)}) collective-permute-start(bf16[24,2048]{1,0:T(8,128)(2,1)S(1)} %get-tuple-element.103), channel_id=1, source_target_pairs={{0,2},{1,3},{2,0},{3,1},{4,6},{5,7},{6,4},{7,5},{8,10},{9,11},{10,... | collective-permute-start | bytes 294920 | tf_op jit(solution)/shard_map/ppermute | solution.py:352
  37.3 8.3 %collective-permute-start.11 = (bf16[24,2048]{1,0:T(8,128)(2,1)S(1)}, bf16[24,2048]{1,0:T(8,128)(2,1)S(1)}, u32[]{:S(2)}, u32[]{:S(2)}) collective-permute-start(bf16[24,2048]{1,0:T(8,128)(2,1)S(1)} %get-tuple-element.104), channel_id=1, source_target_pairs={{0,3},{1,2},{2,1},{3,0},{4,7},{5,6},{6,5},{7,4},{8,11},{9,10},{10,... | collective-permute-start | bytes 294920 | tf_op jit(solution)/shard_map/ppermute | solution.py:352
  37.6 8.1 %collective-permute-start.7 = (bf16[64,1024]{1,0:T(8,128)(2,1)S(1)}, bf16[64,1024]{1,0:T(8,128)(2,1)S(1)}, u32[]{:S(2)}, u32[]{:S(2)}) collective-permute-start(bf16[64,1024]{1,0:T(8,128)(2,1)S(1)} %get-tuple-element.98.refs_2_), channel_id=1, source_target_pairs={{0,4},{1,5},{2,6},{3,7},{4,12},{5,13},{6,14},{7,15},{12,8},{13,9},... | collective-permute-start | bytes 393224 | tf_op jit(solution)/shard_map/ppermute | solution.py:352
  41.4 6.5 %collective-permute-start.8 = (bf16[64,1024]{1,0:T(8,128)(2,1)S(1)}, bf16[64,1024]{1,0:T(8,128)(2,1)S(1)}, u32[]{:S(2)}, u32[]{:S(2)}) collective-permute-start(bf16[64,1024]{1,0:T(8,128)(2,1)S(1)} %get-tuple-element.99.refs_1_), channel_id=1, source_target_pairs={{4,0},{5,1},{6,2},{7,3},{12,4},{13,5},{14,6},{15,7},{8,12},{9,13},... | collective-permute-start | bytes 393224 | tf_op jit(solution)/shard_map/ppermute | solution.py:352
  43.3 8.0 %collective-permute-start.15 = (bf16[64,1024]{1,0:T(8,128)(2,1)S(1)}, bf16[64,1024]{1,0:T(8,128)(2,1)S(1)}, u32[]{:S(2)}, u32[]{:S(2)}) collective-permute-start(bf16[64,1024]{1,0:T(8,128)(2,1)S(1)} %collective-permute-done.13.refs_3_.refs_8_), channel_id=1, source_target_pairs={{4,0},{5,1},{6,2},{7,3},{12,4},{13,5},{14,6},{15,7},{8,12},{9,13},... | collective-permute-start | bytes 393224 | tf_op jit(solution)/shard_map/ppermute | solution.py:352
  43.3 9.9 %collective-permute-start.14 = (bf16[64,1024]{1,0:T(8,128)(2,1)S(1)}, bf16[64,1024]{1,0:T(8,128)(2,1)S(1)}, u32[]{:S(2)}, u32[]{:S(2)}) collective-permute-start(bf16[64,1024]{1,0:T(8,128)(2,1)S(1)} %collective-permute-done.12.refs_1_.refs_4_), channel_id=1, source_target_pairs={{0,4},{1,5},{2,6},{3,7},{4,12},{5,13},{6,14},{7,15},{12,8},{13,9},... | collective-permute-start | bytes 393224 | tf_op jit(solution)/shard_map/ppermute | solution.py:352
  45.6 2.6 %collective-permute-start.16 = (bf16[48,1024]{1,0:T(8,128)(2,1)S(1)}, bf16[48,1024]{1,0:T(8,128)(2,1)S(1)}, u32[]{:S(2)}, u32[]{:S(2)}) collective-permute-start(bf16[48,1024]{1,0:T(8,128)(2,1)S(1)} %get-tuple-element.124), channel_id=1, source_target_pairs={{0,1},{1,0},{2,3},{3,2},{4,5},{5,4},{6,7},{7,6},{8,9},{9,8},{10,11... | collective-permute-start | bytes 294920 | tf_op jit(solution)/shard_map/ppermute | solution.py:352
  45.7 9.5 %collective-permute-start.17 = (bf16[48,1024]{1,0:T(8,128)(2,1)S(1)}, bf16[48,1024]{1,0:T(8,128)(2,1)S(1)}, u32[]{:S(2)}, u32[]{:S(2)}) collective-permute-start(bf16[48,1024]{1,0:T(8,128)(2,1)S(1)} %get-tuple-element.125), channel_id=1, source_target_pairs={{0,2},{1,3},{2,0},{3,1},{4,6},{5,7},{6,4},{7,5},{8,10},{9,11},{10,... | collective-permute-start | bytes 294920 | tf_op jit(solution)/shard_map/ppermute | solution.py:352
  47.9 7.8 %collective-permute-start.18 = (bf16[48,1024]{1,0:T(8,128)(2,1)S(1)}, bf16[48,1024]{1,0:T(8,128)(2,1)S(1)}, u32[]{:S(2)}, u32[]{:S(2)}) collective-permute-start(bf16[48,1024]{1,0:T(8,128)(2,1)S(1)} %get-tuple-element.126), channel_id=1, source_target_pairs={{0,3},{1,2},{2,1},{3,0},{4,7},{5,6},{6,5},{7,4},{8,11},{9,10},{10,... | collective-permute-start | bytes 294920 | tf_op jit(solution)/shard_map/ppermute | solution.py:352
  48.2 8.0 %collective-permute-start.19 = (bf16[48,1024]{1,0:T(8,128)(2,1)S(1)}, bf16[48,1024]{1,0:T(8,128)(2,1)S(1)}, u32[]{:S(2)}, u32[]{:S(2)}) collective-permute-start(bf16[48,1024]{1,0:T(8,128)(2,1)S(1)} %get-tuple-element.128), channel_id=1, source_target_pairs={{0,1},{1,0},{2,3},{3,2},{4,5},{5,4},{6,7},{7,6},{8,9},{9,8},{10,11... | collective-permute-start | bytes 294920 | tf_op jit(solution)/shard_map/ppermute | solution.py:352
  51.3 5.9 %collective-permute-start.20 = (bf16[48,1024]{1,0:T(8,128)(2,1)S(1)}, bf16[48,1024]{1,0:T(8,128)(2,1)S(1)}, u32[]{:S(2)}, u32[]{:S(2)}) collective-permute-start(bf16[48,1024]{1,0:T(8,128)(2,1)S(1)} %get-tuple-element.129), channel_id=1, source_target_pairs={{0,2},{1,3},{2,0},{3,1},{4,6},{5,7},{6,4},{7,5},{8,10},{9,11},{10,... | collective-permute-start | bytes 294920 | tf_op jit(solution)/shard_map/ppermute | solution.py:352
  53.2 4.9 %collective-permute-start.21 = (bf16[48,1024]{1,0:T(8,128)(2,1)S(1)}, bf16[48,1024]{1,0:T(8,128)(2,1)S(1)}, u32[]{:S(2)}, u32[]{:S(2)}) collective-permute-start(bf16[48,1024]{1,0:T(8,128)(2,1)S(1)} %get-tuple-element.130), channel_id=1, source_target_pairs={{0,3},{1,2},{2,1},{3,0},{4,7},{5,6},{6,5},{7,4},{8,11},{9,10},{10,... | collective-permute-start | bytes 294920 | tf_op jit(solution)/shard_map/ppermute | solution.py:352
  55.1 5.9 %collective-permute-start.22 = (bf16[24,2048]{1,0:T(8,128)(2,1)S(1)}, bf16[24,2048]{1,0:T(8,128)(2,1)S(1)}, u32[]{:S(2)}, u32[]{:S(2)}) collective-permute-start(bf16[24,2048]{1,0:T(8,128)(2,1)S(1)} %get-tuple-element.148), channel_id=1, source_target_pairs={{0,1},{1,0},{2,3},{3,2},{4,5},{5,4},{6,7},{7,6},{8,9},{9,8},{10,11... | collective-permute-start | bytes 294920 | tf_op jit(solution)/shard_map/ppermute | solution.py:352
  55.7 5.7 %collective-permute-start.23 = (bf16[24,2048]{1,0:T(8,128)(2,1)S(1)}, bf16[24,2048]{1,0:T(8,128)(2,1)S(1)}, u32[]{:S(2)}, u32[]{:S(2)}) collective-permute-start(bf16[24,2048]{1,0:T(8,128)(2,1)S(1)} %get-tuple-element.149), channel_id=1, source_target_pairs={{0,2},{1,3},{2,0},{3,1},{4,6},{5,7},{6,4},{7,5},{8,10},{9,11},{10,... | collective-permute-start | bytes 294920 | tf_op jit(solution)/shard_map/ppermute | solution.py:352
  56.2 5.5 %collective-permute-start.24 = (bf16[24,2048]{1,0:T(8,128)(2,1)S(1)}, bf16[24,2048]{1,0:T(8,128)(2,1)S(1)}, u32[]{:S(2)}, u32[]{:S(2)}) collective-permute-start(bf16[24,2048]{1,0:T(8,128)(2,1)S(1)} %get-tuple-element.150), channel_id=1, source_target_pairs={{0,3},{1,2},{2,1},{3,0},{4,7},{5,6},{6,5},{7,4},{8,11},{9,10},{10,... | collective-permute-start | bytes 294920 | tf_op jit(solution)/shard_map/ppermute | solution.py:352
  64.1 4.4 %collective-permute-start.31 = (bf16[24,2048]{1,0:T(8,128)(2,1)S(1)}, bf16[24,2048]{1,0:T(8,128)(2,1)S(1)}, u32[]{:S(2)}, u32[]{:S(2)}) collective-permute-start(bf16[24,2048]{1,0:T(8,128)(2,1)S(1)} %get-tuple-element.167), channel_id=1, source_target_pairs={{0,1},{1,0},{2,3},{3,2},{4,5},{5,4},{6,7},{7,6},{8,9},{9,8},{10,11... | collective-permute-start | bytes 294920 | tf_op jit(solution)/shard_map/ppermute | solution.py:352
  64.9 5.2 %collective-permute-start.32 = (bf16[24,2048]{1,0:T(8,128)(2,1)S(1)}, bf16[24,2048]{1,0:T(8,128)(2,1)S(1)}, u32[]{:S(2)}, u32[]{:S(2)}) collective-permute-start(bf16[24,2048]{1,0:T(8,128)(2,1)S(1)} %get-tuple-element.168), channel_id=1, source_target_pairs={{0,2},{1,3},{2,0},{3,1},{4,6},{5,7},{6,4},{7,5},{8,10},{9,11},{10,... | collective-permute-start | bytes 294920 | tf_op jit(solution)/shard_map/ppermute | solution.py:352
  66.4 5.7 %collective-permute-start.33 = (bf16[24,2048]{1,0:T(8,128)(2,1)S(1)}, bf16[24,2048]{1,0:T(8,128)(2,1)S(1)}, u32[]{:S(2)}, u32[]{:S(2)}) collective-permute-start(bf16[24,2048]{1,0:T(8,128)(2,1)S(1)} %get-tuple-element.169), channel_id=1, source_target_pairs={{0,3},{1,2},{2,1},{3,0},{4,7},{5,6},{6,5},{7,4},{8,11},{9,10},{10,... | collective-permute-start | bytes 294920 | tf_op jit(solution)/shard_map/ppermute | solution.py:352
  66.4 7.5 %collective-permute-start.28 = (bf16[48,1024]{1,0:T(8,128)(2,1)S(1)}, bf16[48,1024]{1,0:T(8,128)(2,1)S(1)}, u32[]{:S(2)}, u32[]{:S(2)}) collective-permute-start(bf16[48,1024]{1,0:T(8,128)(2,1)S(1)} %get-tuple-element.158), channel_id=1, source_target_pairs={{0,1},{1,0},{2,3},{3,2},{4,5},{5,4},{6,7},{7,6},{8,9},{9,8},{10,11... | collective-permute-start | bytes 294920 | tf_op jit(solution)/shard_map/ppermute | solution.py:352
  67.0 8.1 %collective-permute-start.29 = (bf16[48,1024]{1,0:T(8,128)(2,1)S(1)}, bf16[48,1024]{1,0:T(8,128)(2,1)S(1)}, u32[]{:S(2)}, u32[]{:S(2)}) collective-permute-start(bf16[48,1024]{1,0:T(8,128)(2,1)S(1)} %get-tuple-element.159), channel_id=1, source_target_pairs={{0,2},{1,3},{2,0},{3,1},{4,6},{5,7},{6,4},{7,5},{8,10},{9,11},{10,... | collective-permute-start | bytes 294920 | tf_op jit(solution)/shard_map/ppermute | solution.py:352
  68.5 7.4 %collective-permute-start.37 = (bf16[48,1024]{1,0:T(8,128)(2,1)S(1)}, bf16[48,1024]{1,0:T(8,128)(2,1)S(1)}, u32[]{:S(2)}, u32[]{:S(2)}) collective-permute-start(bf16[48,1024]{1,0:T(8,128)(2,1)S(1)} %get-tuple-element.174), channel_id=1, source_target_pairs={{0,1},{1,0},{2,3},{3,2},{4,5},{5,4},{6,7},{7,6},{8,9},{9,8},{10,11... | collective-permute-start | bytes 294920 | tf_op jit(solution)/shard_map/ppermute | solution.py:352
  70.1 6.3 %collective-permute-start.38 = (bf16[48,1024]{1,0:T(8,128)(2,1)S(1)}, bf16[48,1024]{1,0:T(8,128)(2,1)S(1)}, u32[]{:S(2)}, u32[]{:S(2)}) collective-permute-start(bf16[48,1024]{1,0:T(8,128)(2,1)S(1)} %get-tuple-element.175), channel_id=1, source_target_pairs={{0,2},{1,3},{2,0},{3,1},{4,6},{5,7},{6,4},{7,5},{8,10},{9,11},{10,... | collective-permute-start | bytes 294920 | tf_op jit(solution)/shard_map/ppermute | solution.py:352
  72.1 5.7 %collective-permute-start.39 = (bf16[48,1024]{1,0:T(8,128)(2,1)S(1)}, bf16[48,1024]{1,0:T(8,128)(2,1)S(1)}, u32[]{:S(2)}, u32[]{:S(2)}) collective-permute-start(bf16[48,1024]{1,0:T(8,128)(2,1)S(1)} %get-tuple-element.176), channel_id=1, source_target_pairs={{0,3},{1,2},{2,1},{3,0},{4,7},{5,6},{6,5},{7,4},{8,11},{9,10},{10,... | collective-permute-start | bytes 294920 | tf_op jit(solution)/shard_map/ppermute | solution.py:352
  73.9 8.5 %collective-permute-start.34 = (bf16[64,1024]{1,0:T(8,128)(2,1)S(1)}, bf16[64,1024]{1,0:T(8,128)(2,1)S(1)}, u32[]{:S(2)}, u32[]{:S(2)}) collective-permute-start(bf16[64,1024]{1,0:T(8,128)(2,1)S(1)} %get-tuple-element.170), channel_id=1, source_target_pairs={{4,0},{5,1},{6,2},{7,3},{12,4},{13,5},{14,6},{15,7},{8,12},{9,13},... | collective-permute-start | bytes 393224 | tf_op jit(solution)/shard_map/ppermute | solution.py:352
  75.1 8.5 %collective-permute-start.35 = (bf16[64,1024]{1,0:T(8,128)(2,1)S(1)}, bf16[64,1024]{1,0:T(8,128)(2,1)S(1)}, u32[]{:S(2)}, u32[]{:S(2)}) collective-permute-start(bf16[64,1024]{1,0:T(8,128)(2,1)S(1)} %get-tuple-element.171), channel_id=1, source_target_pairs={{0,4},{1,5},{2,6},{3,7},{4,12},{5,13},{6,14},{7,15},{12,8},{13,9},... | collective-permute-start | bytes 393224 | tf_op jit(solution)/shard_map/ppermute | solution.py:352
  76.0 4.7 %collective-permute-start.30 = (bf16[48,1024]{1,0:T(8,128)(2,1)S(1)}, bf16[48,1024]{1,0:T(8,128)(2,1)S(1)}, u32[]{:S(2)}, u32[]{:S(2)}) collective-permute-start(bf16[48,1024]{1,0:T(8,128)(2,1)S(1)} %get-tuple-element.160), channel_id=1, source_target_pairs={{0,3},{1,2},{2,1},{3,0},{4,7},{5,6},{6,5},{7,4},{8,11},{9,10},{10,... | collective-permute-start | bytes 294920 | tf_op jit(solution)/shard_map/ppermute | solution.py:352
  76.4 8.4 %collective-permute-start.25 = (bf16[24,2048]{1,0:T(8,128)(2,1)S(1)}, bf16[24,2048]{1,0:T(8,128)(2,1)S(1)}, u32[]{:S(2)}, u32[]{:S(2)}) collective-permute-start(bf16[24,2048]{1,0:T(8,128)(2,1)S(1)} %get-tuple-element.152), channel_id=1, source_target_pairs={{0,1},{1,0},{2,3},{3,2},{4,5},{5,4},{6,7},{7,6},{8,9},{9,8},{10,11... | collective-permute-start | bytes 294920 | tf_op jit(solution)/shard_map/ppermute | solution.py:352
  77.8 9.1 %collective-permute-start.26 = (bf16[24,2048]{1,0:T(8,128)(2,1)S(1)}, bf16[24,2048]{1,0:T(8,128)(2,1)S(1)}, u32[]{:S(2)}, u32[]{:S(2)}) collective-permute-start(bf16[24,2048]{1,0:T(8,128)(2,1)S(1)} %get-tuple-element.153), channel_id=1, source_target_pairs={{0,2},{1,3},{2,0},{3,1},{4,6},{5,7},{6,4},{7,5},{8,10},{9,11},{10,... | collective-permute-start | bytes 294920 | tf_op jit(solution)/shard_map/ppermute | solution.py:352
  80.7 11.2 %collective-permute-start.40 = (bf16[64,1024]{1,0:T(8,128)(2,1)S(1)}, bf16[64,1024]{1,0:T(8,128)(2,1)S(1)}, u32[]{:S(2)}, u32[]{:S(2)}) collective-permute-start(bf16[64,1024]{1,0:T(8,128)(2,1)S(1)} %get-tuple-element.177), channel_id=1, source_target_pairs={{0,4},{1,5},{2,6},{3,7},{4,12},{5,13},{6,14},{7,15},{12,8},{13,9},... | collective-permute-start | bytes 393224 | tf_op jit(solution)/shard_map/ppermute | solution.py:352
  82.4 9.5 %collective-permute-start.41 = (bf16[64,1024]{1,0:T(8,128)(2,1)S(1)}, bf16[64,1024]{1,0:T(8,128)(2,1)S(1)}, u32[]{:S(2)}, u32[]{:S(2)}) collective-permute-start(bf16[64,1024]{1,0:T(8,128)(2,1)S(1)} %get-tuple-element.178), channel_id=1, source_target_pairs={{4,0},{5,1},{6,2},{7,3},{12,4},{13,5},{14,6},{15,7},{8,12},{9,13},... | collective-permute-start | bytes 393224 | tf_op jit(solution)/shard_map/ppermute | solution.py:352
  83.9 8.8 %collective-permute-start.36 = (bf16[64,1024]{1,0:T(8,128)(2,1)S(1)}, bf16[64,1024]{1,0:T(8,128)(2,1)S(1)}, u32[]{:S(2)}, u32[]{:S(2)}) collective-permute-start(bf16[64,1024]{1,0:T(8,128)(2,1)S(1)} %get-tuple-element.172), channel_id=1, source_target_pairs={{0,4},{1,5},{2,6},{3,7},{4,12},{5,13},{6,14},{7,15},{12,8},{13,9},... | collective-permute-start | bytes 393224 | tf_op jit(solution)/shard_map/ppermute | solution.py:352
  84.8 10.3 %collective-permute-start.42 = (bf16[64,1024]{1,0:T(8,128)(2,1)S(1)}, bf16[64,1024]{1,0:T(8,128)(2,1)S(1)}, u32[]{:S(2)}, u32[]{:S(2)}) collective-permute-start(bf16[64,1024]{1,0:T(8,128)(2,1)S(1)} %get-tuple-element.179), channel_id=1, source_target_pairs={{4,0},{5,1},{6,2},{7,3},{12,4},{13,5},{14,6},{15,7},{8,12},{9,13},... | collective-permute-start | bytes 393224 | tf_op jit(solution)/shard_map/ppermute | solution.py:352
  86.9 5.0 %collective-permute-start.27 = (bf16[24,2048]{1,0:T(8,128)(2,1)S(1)}, bf16[24,2048]{1,0:T(8,128)(2,1)S(1)}, u32[]{:S(2)}, u32[]{:S(2)}) collective-permute-start(bf16[24,2048]{1,0:T(8,128)(2,1)S(1)} %get-tuple-element.154), channel_id=1, source_target_pairs={{0,3},{1,2},{2,1},{3,0},{4,7},{5,6},{6,5},{7,4},{8,11},{9,10},{10,... | collective-permute-start | bytes 294920 | tf_op jit(solution)/shard_map/ppermute | solution.py:352

commit v3 on v2

--- a/solution.py
+++ b/solution.py
@@ -75,17 +75,43 @@
         "fsdp",
         pair,
     )
-    other = lax.ppermute(own_heads(mixed_latent, 1 - side), "fsdp", pair)
+    by_head = jnp.swapaxes(mixed_latent, 0, 1)
+    give = lax.dynamic_slice_in_dim(by_head, (1 - side) * heads, heads, 0)
+    kept = lax.dynamic_slice_in_dim(by_head, side * heads, heads, 0)
+    other = lax.ppermute(give, "fsdp", pair)
     theirs = lax.ppermute(mine, "ep", twins)
     far = jnp.where(
         lane == 0, jnp.concatenate([mine, theirs], 0), jnp.concatenate([theirs, mine], 0)
     )
     near = own_heads(w_uv, side)
     full = jnp.where(side == 0, jnp.concatenate([near, far], 0), jnp.concatenate([far, near], 0))
-    partial = jnp.dot(up_project(other, full), w_out, preferred_element_type=jnp.float32)
-    back = lax.ppermute(partial.astype(jnp.bfloat16), "fsdp", pair)
-    kept = up_project(own_heads(mixed_latent, side), full)
-    return jnp.dot(kept, w_out, preferred_element_type=jnp.float32), back
+    full = jnp.swapaxes(full, 0, 1)
+    count, width = mixed_latent.shape[0], w_out.shape[1]
+
+    def project(mixed, dtype):
+        return fused(
+            project_kernel,
+            [((count, width), dtype)],
+            mixed,
+            full,
+            w_out,
+            flops=2 * count * w_out.shape[0] * (width + full.shape[1]),
+            bytes_accessed=2 * w_out.shape[0] * (width + full.shape[1]),
+        )[0]
+
+    partial = project(other, jnp.bfloat16)
+    back = lax.ppermute(partial, "fsdp", pair)
+    return project(kept, jnp.float32), back
+
+
+def project_kernel(mixed_ref, values_ref, out_w_ref, result_ref):
+    parts = [
+        jnp.dot(mixed_ref[h], values_ref[h], preferred_element_type=jnp.float32)
+        for h in range(values_ref.shape[0])
+    ]
+    flat = jnp.concatenate(parts, 1).astype(jnp.bfloat16)
+    total = jnp.dot(flat, out_w_ref[...], preferred_element_type=jnp.float32)
+    result_ref[...] = total.astype(result_ref.dtype)
 
 
 def experts(rows, w_gate, w_up, w_down):

time: 96.3 us -> 94.2 us (0.978)
  waiting for transfers between devices: 30.5 us -> 27.9 us
  Pallas kernels: 9.8 us -> 11 us
    ppermute x2, waiting for transfers between devices: 11.6 us -> 6.37 us  [the longest x1 6.37 us: project_paired(): other = lax.ppermute(give, 'fsdp', pair)]
    ppermute x2, waiting for transfers between devices: 0.01 us -> 2.41 us  [per_device(): ids += [lax.ppermute(ids[0], 'ep', steps) for steps in (onward, backward)]]
    ppermute x1, starting transfers between devices: 1.56 us -> 3.03 us  [project_paired(): lax.ppermute(lax.dynamic_slice(w_uv, (lane * rows, (1 - side) * heads, 0)...]
    ppermute x1, starting transfers between devices: 5.08 us -> 3.6 us  [per_device(): ids.append(lax.ppermute(ids[0], 'ep', across))]
    dot_general x4 -> x0, matrix products: 1.42 us -> none  [the longest x1 0.48 us: project_paired(): jnp.dot(up_project(other, full), w_out, preferred_element_type=jnp.float32)]
    pallas_call x13 -> x15, Pallas kernels: 9.8 us -> 11 us  [fused(): pl.pallas_call(body, out_shape=[jax.ShapeDtypeStruct(shape, dtype) for sh...]
    dot_general x1, matrix products: 0.33 us -> 1.36 us  [attend_local(): jnp.dot(weights_att, keys_latent, preferred_element_type=jnp.float32)]
    unnamed x22 -> x23, local copies, waits for them, and re-layouts: 0.94 us -> 1.92 us
  transfers between devices with their start and end apart: 43 -> 43, of which waited for: 17 -> 17; matrix products, arithmetic and copies ran while one was open for 6% -> 7% of each run, Pallas kernels for 6% -> 7%
where the time goes in v3:
time: 94.2 us; the launch traced here: 94 us
  starting transfers between devices  46.4 us (49%)
  waiting for transfers between devices  27.9 us (30%)
  Pallas kernels  11 us (12%)
  matrix products  3.93 us (4%)
  local copies, waits for them, and re-layouts  2.41 us (3%)
  other arithmetic  1.28 us (1%)
  between operations  1.04 us (1%)
    ppermute x36, starting transfers between devices, send(): return lax.ppermute(value, 'ep', steps)  35.4 us
    ppermute x36, waiting for transfers between devices, send(): return lax.ppermute(value, 'ep', steps)  19.1 us
    pallas_call x15, Pallas kernels, fused(): pl.pallas_call(body, out_shape=[jax.ShapeDtypeStruct(shape, dtype) for sh...  11 us
    ppermute x1, waiting for transfers between devices, project_paired(): other = lax.ppermute(give, 'fsdp', pair)  6.37 us
    ppermute x1, starting transfers between devices, per_device(): ids.append(lax.ppermute(ids[0], 'ep', across))  3.6 us
    ppermute x1, starting transfers between devices, project_paired(): lax.ppermute(lax.dynamic_slice(w_uv, (lane * rows, (1 - side) * heads, 0)...  3.03 us
    ppermute x2, waiting for transfers between devices, per_device(): ids += [lax.ppermute(ids[0], 'ep', steps) for steps in (onward, backward)]  2.41 us
    ppermute x2, starting transfers between devices, per_device(): ids += [lax.ppermute(ids[0], 'ep', steps) for steps in (onward, backward)]  2.03 us
  transfers between devices with their start and end apart: 43, of which 17 were waited for; matrix products, arithmetic and copies ran while one was open for 7% of the time, Pallas kernels for 7%

profile of v3, /device:TPU:0, one launch (start us, length us, event | category | flops | bytes accessed | tf_op | source)
XLA Modules:
  0.0 94.0 jit_solution(11512131263669095769)
XLA Ops:
  0.7 1.0 %copy-done = bf16[256,8,128]{2,1,0:T(8,128)(2,1)S(1)} copy-done((bf16[256,8,128]{2,1,0:T(8,128)(2,1)S(1)}, bf16[256,8,128]{2,1,0:T(8,128)(2,1)}, u32[]{:S(2)}) %copy-start) | copy-done | bytes 524312
  1.8 3.0 %collective-permute-start = (bf16[128,4,128]{2,0,1:T(8,128)(2,1)S(1)}, bf16[128,4,128]{2,0,1:T(8,128)(2,1)S(1)}, u32[]{:S(2)}, u32[]{:S(2)}) collective-permute-start(bf16[128,4,128]{2,0,1:T(8,128)(2,1)S(1)} %copy.26), channel_id=1, source_target_pairs={{0,16},{16,0},{1,17},{17,1},{2,18},{18,2},{3,19},{19,3},{4,20},{20... | collective-permute-start | bytes 393224 | tf_op jit(solution)/shard_map/ppermute | solution.py:71
  4.8 1.4 %fusion.4 = f32[128,512]{1,0:T(8,128)S(1)} fusion(bf16[1,64,8,512]{3,2,1,0:T(8,128)(2,1)} %param.16, bf16[64,512]{1,0:T(8,128)(2,1)} %bitcast.53, bf16[64,512]{1,0:T(8,128)(2,1)} %bitcast.55), kind=kOutput, calls=%fused_computation.7 | convolution fusion | flops 67371008 | bytes 917504 | tf_op jit(solution)/shard_map/dot_general | solution.py:22
  6.2 1.2 %select_reduce_fusion = (f32[512]{0:T(512)S(1)}, f32[512,128]{0,1:T(8,128)S(1)}) fusion(s32[512]{0:T(512)S(1)} %fusion.15, f32[128,512]{1,0:T(8,128)S(1)} %fusion.4, bf16[1,64,8,64]{3,2,1,0:T(8,128)(2,1)} %param.17, bf16[64,64]{1,0:T(8,128)(2,1)} %bitcast.57, bf16[64,64]{1,0:T(8,128)(2,1)} %bitcast.58), kind=kOutput, calls=%fused_computation.14 | convolution fusion | flops 8748544 | bytes 610304 | tf_op jit(solution)/shard_map/dot_general | solution.py:24
  7.5 1.4 %fusion = bf16[64,8,512]{2,1,0:T(8,128)(2,1)S(1)} fusion(f32[512,128]{0,1:T(8,128)S(1)} %get-tuple-element.183, f32[512]{0:T(512)S(1)} %fusion.6, f32[512]{0:T(512)S(1)} %get-tuple-element.182, s32[512]{0:T(512)S(1)} %fusion.15, bf16[64,512]{1,0:T(8,128)(2,1)} %bitcast.54, bf16[64,512]{1,0:T(8,128)(2,1)} %bitcast.56), kind=kOutput, calls=%fused_computation.1 | convolution fusion | flops 67960832 | bytes 923648 | tf_op jit(solution)/shard_map/dot_general | solution.py:32
  9.2 0.7 copy.31
  10.0 1.1 %collective-permute-start.2 = (bf16[4,64,512]{2,1,0:T(8,128)(2,1)}, bf16[4,64,512]{2,1,0:T(8,128)(2,1)S(1)}, u32[]{:S(2)}, u32[]{:S(2)}) collective-permute-start(bf16[4,64,512]{2,1,0:T(8,128)(2,1)} %bitcast.36), channel_id=1, source_target_pairs={{0,16},{16,0},{1,17},{17,1},{2,18},{18,2},{3,19},{19,3},{4,20},{20... | collective-permute-start | bytes 786440 | tf_op jit(solution)/shard_map/ppermute | solution.py:81
  11.3 1.1 %maximum_select_fusion.1 = bf16[256,4,128]{2,0,1:T(8,128)(2,1)S(1)} fusion(bf16[128,4,128]{2,0,1:T(8,128)(2,1)} %collective-permute-done.1, bf16[128,4,128]{2,0,1:T(8,128)(2,1)S(1)} %collective-permute-done, pred[]{:T(512)S(6)} %eq.9), kind=kLoop, calls=%fused_computation.9 | loop fusion | flops 1179648 | bytes 524289 | tf_op jit(solution)/shard_map/jit(_where)/select_n | solution.py:83
  12.5 6.4 %collective-permute-done.2.mixed_ref = bf16[4,64,512]{2,1,0:T(8,128)(2,1)S(1)} collective-permute-done((bf16[4,64,512]{2,1,0:T(8,128)(2,1)}, bf16[4,64,512]{2,1,0:T(8,128)(2,1)S(1)}, u32[]{:S(2)}, u32[]{:S(2)}) %collective-permute-start.2) | collective-permute-done | bytes 262176 | tf_op jit(solution)/shard_map/ppermute | solution.py:81
  18.9 0.6 shard_map.159
  19.5 1.2 %collective-permute-start.3 = (bf16[64,2048]{1,0:T(8,128)(2,1)S(1)}, bf16[64,2048]{1,0:T(8,128)(2,1)S(1)}, u32[]{:S(2)}, u32[]{:S(2)}) collective-permute-start(bf16[64,2048]{1,0:T(8,128)(2,1)S(1)} %shard_map.159), channel_id=1, source_target_pairs={{0,16},{16,0},{1,17},{17,1},{2,18},{18,2},{3,19},{19,3},{4,20},{20... | collective-permute-start | bytes 786440 | tf_op jit(solution)/shard_map/ppermute | solution.py:103
  20.7 3.6 %collective-permute-start.6 = (s32[6,64]{1,0:T(8,128)S(1)}, s32[6,64]{1,0:T(8,128)S(1)}, u32[]{:S(2)}, u32[]{:S(2)}) collective-permute-start(s32[6,64]{1,0:T(8,128)S(1)} %bitcast.47), channel_id=1, source_target_pairs={{0,12},{1,13},{2,14},{3,15},{4,8},{5,9},{6,10},{7,11},{8,4},{9,5},... | collective-permute-start | bytes 4616 | tf_op jit(solution)/shard_map/ppermute | solution.py:535
  24.3 2.0 %collective-permute-start.4 = (s32[6,64]{1,0:T(8,128)S(1)}, s32[6,64]{1,0:T(8,128)S(1)}, u32[]{:S(2)}, u32[]{:S(2)}) collective-permute-start(s32[6,64]{1,0:T(8,128)S(1)} %bitcast.49), channel_id=1, source_target_pairs={{0,4},{1,5},{2,6},{3,7},{4,12},{5,13},{6,14},{7,15},{12,8},{13,9},... | collective-permute-start | bytes 4616 | tf_op jit(solution)/shard_map/ppermute | solution.py:534
  26.4 1.5 %collective-permute-done.5.refs_2_ = s32[6,64]{1,0:T(8,128)S(1)} collective-permute-done((s32[6,64]{1,0:T(8,128)S(1)}, s32[6,64]{1,0:T(8,128)S(1)}, u32[]{:S(2)}, u32[]{:S(2)}) %collective-permute-start.5) | collective-permute-done | bytes 1568 | tf_op jit(solution)/shard_map/ppermute | solution.py:534
  27.9 0.9 collective-permute-done.4.refs_1_
  29.0 0.6 shard_map.158.part_ref
  29.7 0.9 shard_map.161
  30.5 0.3 collective-permute-start.13
  30.9 1.7 %collective-permute-start.12 = (bf16[64,1024]{1,0:T(8,128)(2,1)S(1)}, bf16[64,1024]{1,0:T(8,128)(2,1)S(1)}, u32[]{:S(2)}, u32[]{:S(2)}) collective-permute-start(bf16[64,1024]{1,0:T(8,128)(2,1)S(1)} %get-tuple-element.99.refs_1_), channel_id=1, source_target_pairs={{0,4},{1,5},{2,6},{3,7},{4,12},{5,13},{6,14},{7,15},{12,8},{13,9},... | collective-permute-start | bytes 393224 | tf_op jit(solution)/shard_map/ppermute | solution.py:378
  32.9 1.6 %collective-permute-start.10 = (bf16[24,2048]{1,0:T(8,128)(2,1)S(1)}, bf16[24,2048]{1,0:T(8,128)(2,1)S(1)}, u32[]{:S(2)}, u32[]{:S(2)}) collective-permute-start(bf16[24,2048]{1,0:T(8,128)(2,1)S(1)} %get-tuple-element.103), channel_id=1, source_target_pairs={{0,2},{1,3},{2,0},{3,1},{4,6},{5,7},{6,4},{7,5},{8,10},{9,11},{10,... | collective-permute-start | bytes 294920 | tf_op jit(solution)/shard_map/ppermute | solution.py:378
  34.8 2.0 %collective-permute-start.7 = (bf16[64,1024]{1,0:T(8,128)(2,1)S(1)}, bf16[64,1024]{1,0:T(8,128)(2,1)S(1)}, u32[]{:S(2)}, u32[]{:S(2)}) collective-permute-start(bf16[64,1024]{1,0:T(8,128)(2,1)S(1)} %get-tuple-element.98.refs_2_), channel_id=1, source_target_pairs={{0,4},{1,5},{2,6},{3,7},{4,12},{5,13},{6,14},{7,15},{12,8},{13,9},... | collective-permute-start | bytes 393224 | tf_op jit(solution)/shard_map/ppermute | solution.py:378
  36.8 1.9 %collective-permute-done.10.refs_10_ = bf16[24,2048]{1,0:T(8,128)(2,1)S(1)} collective-permute-done((bf16[24,2048]{1,0:T(8,128)(2,1)S(1)}, bf16[24,2048]{1,0:T(8,128)(2,1)S(1)}, u32[]{:S(2)}, u32[]{:S(2)}) %collective-permute-start.10) | collective-permute-done | bytes 98336 | tf_op jit(solution)/shard_map/ppermute | solution.py:378
  38.7 1.2 %collective-permute-start.8 = (bf16[64,1024]{1,0:T(8,128)(2,1)S(1)}, bf16[64,1024]{1,0:T(8,128)(2,1)S(1)}, u32[]{:S(2)}, u32[]{:S(2)}) collective-permute-start(bf16[64,1024]{1,0:T(8,128)(2,1)S(1)} %get-tuple-element.99.refs_1_), channel_id=1, source_target_pairs={{4,0},{5,1},{6,2},{7,3},{12,4},{13,5},{14,6},{15,7},{8,12},{9,13},... | collective-permute-start | bytes 393224 | tf_op jit(solution)/shard_map/ppermute | solution.py:378
  39.9 1.2 %collective-permute-start.15 = (bf16[64,1024]{1,0:T(8,128)(2,1)S(1)}, bf16[64,1024]{1,0:T(8,128)(2,1)S(1)}, u32[]{:S(2)}, u32[]{:S(2)}) collective-permute-start(bf16[64,1024]{1,0:T(8,128)(2,1)S(1)} %collective-permute-done.13.refs_3_.refs_8_), channel_id=1, source_target_pairs={{4,0},{5,1},{6,2},{7,3},{12,4},{13,5},{14,6},{15,7},{8,12},{9,13},... | collective-permute-start | bytes 393224 | tf_op jit(solution)/shard_map/ppermute | solution.py:378
  41.1 0.8 collective-permute-start.14
  42.3 1.6 %collective-permute-start.17 = (bf16[48,1024]{1,0:T(8,128)(2,1)S(1)}, bf16[48,1024]{1,0:T(8,128)(2,1)S(1)}, u32[]{:S(2)}, u32[]{:S(2)}) collective-permute-start(bf16[48,1024]{1,0:T(8,128)(2,1)S(1)} %get-tuple-element.125), channel_id=1, source_target_pairs={{0,2},{1,3},{2,0},{3,1},{4,6},{5,7},{6,4},{7,5},{8,10},{9,11},{10,... | collective-permute-start | bytes 294920 | tf_op jit(solution)/shard_map/ppermute | solution.py:378
  43.9 1.2 %collective-permute-done.8.refs_7_.refs_3_ = bf16[64,1024]{1,0:T(8,128)(2,1)S(1)} collective-permute-done((bf16[64,1024]{1,0:T(8,128)(2,1)S(1)}, bf16[64,1024]{1,0:T(8,128)(2,1)S(1)}, u32[]{:S(2)}, u32[]{:S(2)}) %collective-permute-start.8) | collective-permute-done | bytes 131104 | tf_op jit(solution)/shard_map/ppermute | solution.py:378
  45.4 1.7 %collective-permute-start.19 = (bf16[48,1024]{1,0:T(8,128)(2,1)S(1)}, bf16[48,1024]{1,0:T(8,128)(2,1)S(1)}, u32[]{:S(2)}, u32[]{:S(2)}) collective-permute-start(bf16[48,1024]{1,0:T(8,128)(2,1)S(1)} %get-tuple-element.128), channel_id=1, source_target_pairs={{0,1},{1,0},{2,3},{3,2},{4,5},{5,4},{6,7},{7,6},{8,9},{9,8},{10,11... | collective-permute-start | bytes 294920 | tf_op jit(solution)/shard_map/ppermute | solution.py:378
  47.1 0.7 collective-permute-done.15.refs_2_.refs_11_
  47.8 1.5 %collective-permute-start.20 = (bf16[48,1024]{1,0:T(8,128)(2,1)S(1)}, bf16[48,1024]{1,0:T(8,128)(2,1)S(1)}, u32[]{:S(2)}, u32[]{:S(2)}) collective-permute-start(bf16[48,1024]{1,0:T(8,128)(2,1)S(1)} %get-tuple-element.129), channel_id=1, source_target_pairs={{0,2},{1,3},{2,0},{3,1},{4,6},{5,7},{6,4},{7,5},{8,10},{9,11},{10,... | collective-permute-start | bytes 294920 | tf_op jit(solution)/shard_map/ppermute | solution.py:378
  49.3 1.7 %collective-permute-done.14.refs_1_.refs_10_ = bf16[64,1024]{1,0:T(8,128)(2,1)S(1)} collective-permute-done((bf16[64,1024]{1,0:T(8,128)(2,1)S(1)}, bf16[64,1024]{1,0:T(8,128)(2,1)S(1)}, u32[]{:S(2)}, u32[]{:S(2)}) %collective-permute-start.14) | collective-permute-done | bytes 131104 | tf_op jit(solution)/shard_map/ppermute | solution.py:378
  51.1 1.1 %collective-permute-start.21 = (bf16[48,1024]{1,0:T(8,128)(2,1)S(1)}, bf16[48,1024]{1,0:T(8,128)(2,1)S(1)}, u32[]{:S(2)}, u32[]{:S(2)}) collective-permute-start(bf16[48,1024]{1,0:T(8,128)(2,1)S(1)} %get-tuple-element.130), channel_id=1, source_target_pairs={{0,3},{1,2},{2,1},{3,0},{4,7},{5,6},{6,5},{7,4},{8,11},{9,10},{10,... | collective-permute-start | bytes 294920 | tf_op jit(solution)/shard_map/ppermute | solution.py:378
  52.5 0.5 shard_map.165
  53.0 0.6 collective-permute-start.22
  53.6 0.5 collective-permute-start.23
  54.1 0.9 collective-permute-start.24
  55.0 0.9 collective-permute-done.21.refs_7_
  56.0 3.0 %shard_map.167 = (bf16[48,1024]{1,0:T(8,128)(2,1)S(1)}, bf16[48,1024]{1,0:T(8,128)(2,1)S(1)}, bf16[48,1024]{1,0:T(8,128)(2,1)S(1)}, bf16[48,1024]{1,0:T(8,128)(2...) custom-call(bf16[48,1024]{1,0:T(8,128)(2,1)S(1)} %get-tuple-element., ...), custom_call_target="tpu_custom_call" | custom-call | flops 2491416576 | bytes 11010048 | tf_op jit(solution)/shard_map/pallas_call | solution.py:168
  59.0 0.3 collective-permute-done.23.refs_2_
  59.3 0.3 collective-permute-done.24.refs_3_
  59.6 2.4 %shard_map.168 = (bf16[24,2048]{1,0:T(8,128)(2,1)S(1)}, bf16[24,2048]{1,0:T(8,128)(2,1)S(1)}, bf16[24,2048]{1,0:T(8,128)(2,1)S(1)}, bf16[24,2048]{1,0:T(8,128)(2,1)S(1)}) custom-call(bf16[24,2048]{1,0:T(8,128)(2,1)S(1)} %get-tuple-element.162.refs_0_, bf16[24,2048]{1,0:T(8,128)(2,1)S(1)} %collective-permute-done.22.refs_1_, ...), custom_call_target="tpu_custom_call" | custom-call | flops 830472192 | bytes 9437184 | tf_op jit(solution)/shard_map/pallas_call | solution.py:168
  62.0 0.8 collective-permute-start.31
  62.8 1.5 %collective-permute-start.32 = (bf16[24,2048]{1,0:T(8,128)(2,1)S(1)}, bf16[24,2048]{1,0:T(8,128)(2,1)S(1)}, u32[]{:S(2)}, u32[]{:S(2)}) collective-permute-start(bf16[24,2048]{1,0:T(8,128)(2,1)S(1)} %get-tuple-element.168), channel_id=1, source_target_pairs={{0,2},{1,3},{2,0},{3,1},{4,6},{5,7},{6,4},{7,5},{8,10},{9,11},{10,... | collective-permute-start | bytes 294920 | tf_op jit(solution)/shard_map/ppermute | solution.py:378
  64.3 0.6 collective-permute-start.28
  64.9 1.5 %collective-permute-start.29 = (bf16[48,1024]{1,0:T(8,128)(2,1)S(1)}, bf16[48,1024]{1,0:T(8,128)(2,1)S(1)}, u32[]{:S(2)}, u32[]{:S(2)}) collective-permute-start(bf16[48,1024]{1,0:T(8,128)(2,1)S(1)} %get-tuple-element.159), channel_id=1, source_target_pairs={{0,2},{1,3},{2,0},{3,1},{4,6},{5,7},{6,4},{7,5},{8,10},{9,11},{10,... | collective-permute-start | bytes 294920 | tf_op jit(solution)/shard_map/ppermute | solution.py:378
  66.4 1.6 %collective-permute-done.32.r2 = bf16[24,2048]{1,0:T(8,128)(2,1)S(1)} collective-permute-done((bf16[24,2048]{1,0:T(8,128)(2,1)S(1)}, bf16[24,2048]{1,0:T(8,128)(2,1)S(1)}, u32[]{:S(2)}, u32[]{:S(2)}) %collective-permute-start.32) | collective-permute-done | bytes 98336 | tf_op jit(solution)/shard_map/ppermute | solution.py:378
  68.0 2.0 %collective-permute-start.38 = (bf16[48,1024]{1,0:T(8,128)(2,1)S(1)}, bf16[48,1024]{1,0:T(8,128)(2,1)S(1)}, u32[]{:S(2)}, u32[]{:S(2)}) collective-permute-start(bf16[48,1024]{1,0:T(8,128)(2,1)S(1)} %get-tuple-element.175), channel_id=1, source_target_pairs={{0,2},{1,3},{2,0},{3,1},{4,6},{5,7},{6,4},{7,5},{8,10},{9,11},{10,... | collective-permute-start | bytes 294920 | tf_op jit(solution)/shard_map/ppermute | solution.py:378
  69.9 1.5 %collective-permute-start.39 = (bf16[48,1024]{1,0:T(8,128)(2,1)S(1)}, bf16[48,1024]{1,0:T(8,128)(2,1)S(1)}, u32[]{:S(2)}, u32[]{:S(2)}) collective-permute-start(bf16[48,1024]{1,0:T(8,128)(2,1)S(1)} %get-tuple-element.176), channel_id=1, source_target_pairs={{0,3},{1,2},{2,1},{3,0},{4,7},{5,6},{6,5},{7,4},{8,11},{9,10},{10,... | collective-permute-start | bytes 294920 | tf_op jit(solution)/shard_map/ppermute | solution.py:378
  71.8 0.8 collective-permute-start.34
  72.6 1.3 %collective-permute-start.35 = (bf16[64,1024]{1,0:T(8,128)(2,1)S(1)}, bf16[64,1024]{1,0:T(8,128)(2,1)S(1)}, u32[]{:S(2)}, u32[]{:S(2)}) collective-permute-start(bf16[64,1024]{1,0:T(8,128)(2,1)S(1)} %get-tuple-element.171), channel_id=1, source_target_pairs={{0,4},{1,5},{2,6},{3,7},{4,12},{5,13},{6,14},{7,15},{12,8},{13,9},... | collective-permute-start | bytes 393224 | tf_op jit(solution)/shard_map/ppermute | solution.py:378
  73.9 0.5 collective-permute-done.38.r2
  74.3 0.7 collective-permute-start.25
  75.0 0.7 collective-permute-done.39.r3
  75.7 1.5 %collective-permute-start.26 = (bf16[24,2048]{1,0:T(8,128)(2,1)S(1)}, bf16[24,2048]{1,0:T(8,128)(2,1)S(1)}, u32[]{:S(2)}, u32[]{:S(2)}) collective-permute-start(bf16[24,2048]{1,0:T(8,128)(2,1)S(1)} %get-tuple-element.153), channel_id=1, source_target_pairs={{0,2},{1,3},{2,0},{3,1},{4,6},{5,7},{6,4},{7,5},{8,10},{9,11},{10,... | collective-permute-start | bytes 294920 | tf_op jit(solution)/shard_map/ppermute | solution.py:378
  77.2 0.3 shard_map.171
  77.5 1.0 %collective-permute-done.30.r3 = bf16[48,1024]{1,0:T(8,128)(2,1)S(1)} collective-permute-done((bf16[48,1024]{1,0:T(8,128)(2,1)S(1)}, bf16[48,1024]{1,0:T(8,128)(2,1)S(1)}, u32[]{:S(2)}, u32[]{:S(2)}) %collective-permute-start.30) | collective-permute-done | bytes 98336 | tf_op jit(solution)/shard_map/ppermute | solution.py:378
  78.5 1.5 %collective-permute-start.40 = (bf16[64,1024]{1,0:T(8,128)(2,1)S(1)}, bf16[64,1024]{1,0:T(8,128)(2,1)S(1)}, u32[]{:S(2)}, u32[]{:S(2)}) collective-permute-start(bf16[64,1024]{1,0:T(8,128)(2,1)S(1)} %get-tuple-element.177), channel_id=1, source_target_pairs={{0,4},{1,5},{2,6},{3,7},{4,12},{5,13},{6,14},{7,15},{12,8},{13,9},... | collective-permute-start | bytes 393224 | tf_op jit(solution)/shard_map/ppermute | solution.py:378
  80.1 1.4 %collective-permute-start.41 = (bf16[64,1024]{1,0:T(8,128)(2,1)S(1)}, bf16[64,1024]{1,0:T(8,128)(2,1)S(1)}, u32[]{:S(2)}, u32[]{:S(2)}) collective-permute-start(bf16[64,1024]{1,0:T(8,128)(2,1)S(1)} %get-tuple-element.178), channel_id=1, source_target_pairs={{4,0},{5,1},{6,2},{7,3},{12,4},{13,5},{14,6},{15,7},{8,12},{9,13},... | collective-permute-start | bytes 393224 | tf_op jit(solution)/shard_map/ppermute | solution.py:378
  81.8 0.7 collective-permute-start.36
  82.5 2.3 %collective-permute-start.42 = (bf16[64,1024]{1,0:T(8,128)(2,1)S(1)}, bf16[64,1024]{1,0:T(8,128)(2,1)S(1)}, u32[]{:S(2)}, u32[]{:S(2)}) collective-permute-start(bf16[64,1024]{1,0:T(8,128)(2,1)S(1)} %get-tuple-element.179), channel_id=1, source_target_pairs={{4,0},{5,1},{6,2},{7,3},{12,4},{13,5},{14,6},{15,7},{8,12},{9,13},... | collective-permute-start | bytes 393224 | tf_op jit(solution)/shard_map/ppermute | solution.py:378
  84.8 5.0 %collective-permute-done.27.r3 = bf16[24,2048]{1,0:T(8,128)(2,1)S(1)} collective-permute-done((bf16[24,2048]{1,0:T(8,128)(2,1)S(1)}, bf16[24,2048]{1,0:T(8,128)(2,1)S(1)}, u32[]{:S(2)}, u32[]{:S(2)}) %collective-permute-start.27) | collective-permute-done | bytes 98336 | tf_op jit(solution)/shard_map/ppermute | solution.py:378
  89.8 0.5 collective-permute-done.36.x_low
  90.3 2.7 %collective-permute-done.42.y_high = bf16[64,1024]{1,0:T(8,128)(2,1)S(1)} collective-permute-done((bf16[64,1024]{1,0:T(8,128)(2,1)S(1)}, bf16[64,1024]{1,0:T(8,128)(2,1)S(1)}, u32[]{:S(2)}, u32[]{:S(2)}) %collective-permute-start.42) | collective-permute-done | bytes 131104 | tf_op jit(solution)/shard_map/ppermute | solution.py:378
  93.0 1.0 %shard_map.172 = bf16[64,2048]{1,0:T(8,128)(2,1)} custom-call(f32[64,2048]{1,0:T(8,128)S(1)} %get-tuple-element.97.hidden_ref, f32[64,96]{1,0:T(8,128)S(1)} %get-tuple-element.122.weights_ref, bf16[24,2048]{1,0:T(8,128)(2,1)S(1)} %get-tuple-element.151.r0, bf16[24,2048]{1,0:T(8,128)(2,1)S(1)} %collective-permute-done.25.r1, ...), custom_call_target="tpu_custom_call" | custom-call | flops 100663296 | bytes 2621440 | tf_op jit(solution)/shard_map/pallas_call | solution.py:168
  (70 shorter events, 3.2 us)
Async XLA Ops:
  0.6 1.0 %copy-start = (bf16[256,8,128]{2,1,0:T(8,128)(2,1)S(1)}, bf16[256,8,128]{2,1,0:T(8,128)(2,1)}, u32[]{:S(2)}) copy-start(bf16[256,8,128]{2,1,0:T(8,128)(2,1)} %param.22) | copy-start | bytes 1572868
  1.8 7.1 %collective-permute-start = (bf16[128,4,128]{2,0,1:T(8,128)(2,1)S(1)}, bf16[128,4,128]{2,0,1:T(8,128)(2,1)S(1)}, u32[]{:S(2)}, u32[]{:S(2)}) collective-permute-start(bf16[128,4,128]{2,0,1:T(8,128)(2,1)S(1)} %copy.26), channel_id=1, source_target_pairs={{0,16},{16,0},{1,17},{17,1},{2,18},{18,2},{3,19},{19,3},{4,20},{20... | collective-permute-start | bytes 393224 | tf_op jit(solution)/shard_map/ppermute | solution.py:71
  7.5 11.4 %copy-start.4 = (bf16[512,2048]{1,0:T(8,128)(2,1)S(1)}, bf16[512,2048]{1,0:T(8,128)(2,1)}, u32[]{:S(2)}) copy-start(bf16[512,2048]{1,0:T(8,128)(2,1)} %out_w_ref.3) | copy-start | bytes 6291460
  8.9 2.4 %collective-permute-start.1 = (bf16[128,4,128]{2,0,1:T(8,128)(2,1)S(1)}, bf16[128,4,128]{2,0,1:T(8,128)(2,1)}, u32[]{:S(2)}, u32[]{:S(2)}) collective-permute-start(bf16[128,4,128]{2,0,1:T(8,128)(2,1)S(1)} %collective-permute-done), channel_id=1, source_target_pairs={{0,1},{1,0},{2,3},{3,2},{4,5},{5,4},{6,7},{7,6},{8,9},{9,8},{10,11... | collective-permute-start | bytes 393224 | tf_op jit(solution)/shard_map/ppermute | solution.py:82
  10.0 10.7 %copy-start.8 = (s32[1,64,6]{1,0,2:T(1,128)S(1)}, s32[1,64,6]{1,0,2:T(1,128)}, u32[]{:S(2)}) copy-start(s32[1,64,6]{1,0,2:T(1,128)} %param.26) | copy-start | bytes 4612
  10.0 8.9 %collective-permute-start.2 = (bf16[4,64,512]{2,1,0:T(8,128)(2,1)}, bf16[4,64,512]{2,1,0:T(8,128)(2,1)S(1)}, u32[]{:S(2)}, u32[]{:S(2)}) collective-permute-start(bf16[4,64,512]{2,1,0:T(8,128)(2,1)} %bitcast.36), channel_id=1, source_target_pairs={{0,16},{16,0},{1,17},{17,1},{2,18},{18,2},{3,19},{19,3},{4,20},{20... | collective-permute-start | bytes 786440 | tf_op jit(solution)/shard_map/ppermute | solution.py:81
  12.5 17.2 %copy-start.5 = (bf16[1,64,2048]{2,1,0:T(8,128)(2,1)S(1)}, bf16[1,64,2048]{2,1,0:T(8,128)(2,1)}, u32[]{:S(2)}) copy-start(bf16[1,64,2048]{2,1,0:T(8,128)(2,1)} %x_ref.1) | copy-start | bytes 786436
  12.5 17.2 %copy-start.7 = (f32[2048]{0:T(1024)S(1)}, f32[2048]{0:T(1024)}, u32[]{:S(2)}) copy-start(f32[2048]{0:T(1024)} %param.24) | copy-start | bytes 24580
  18.9 37.1 %copy-start.3 = (bf16[1,704,2048]{2,1,0:T(8,128)(2,1)S(1)}, bf16[1,704,2048]{2,1,0:T(8,128)(2,1)}, u32[]{:S(2)}) copy-start(bf16[1,704,2048]{2,1,0:T(8,128)(2,1)} %param.29) | copy-start | bytes 8650756
  19.5 10.1 %collective-permute-start.3 = (bf16[64,2048]{1,0:T(8,128)(2,1)S(1)}, bf16[64,2048]{1,0:T(8,128)(2,1)S(1)}, u32[]{:S(2)}, u32[]{:S(2)}) collective-permute-start(bf16[64,2048]{1,0:T(8,128)(2,1)S(1)} %shard_map.159), channel_id=1, source_target_pairs={{0,16},{16,0},{1,17},{17,1},{2,18},{18,2},{3,19},{19,3},{4,20},{20... | collective-permute-start | bytes 786440 | tf_op jit(solution)/shard_map/ppermute | solution.py:103
  20.7 5.7 %collective-permute-start.6 = (s32[6,64]{1,0:T(8,128)S(1)}, s32[6,64]{1,0:T(8,128)S(1)}, u32[]{:S(2)}, u32[]{:S(2)}) collective-permute-start(s32[6,64]{1,0:T(8,128)S(1)} %bitcast.47), channel_id=1, source_target_pairs={{0,12},{1,13},{2,14},{3,15},{4,8},{5,9},{6,10},{7,11},{8,4},{9,5},... | collective-permute-start | bytes 4616 | tf_op jit(solution)/shard_map/ppermute | solution.py:535
  24.3 3.6 %collective-permute-start.5 = (s32[6,64]{1,0:T(8,128)S(1)}, s32[6,64]{1,0:T(8,128)S(1)}, u32[]{:S(2)}, u32[]{:S(2)}) collective-permute-start(s32[6,64]{1,0:T(8,128)S(1)} %bitcast.48), channel_id=1, source_target_pairs={{4,0},{5,1},{6,2},{7,3},{12,4},{13,5},{14,6},{15,7},{8,12},{9,13},... | collective-permute-start | bytes 4616 | tf_op jit(solution)/shard_map/ppermute | solution.py:534
  24.3 4.5 %collective-permute-start.4 = (s32[6,64]{1,0:T(8,128)S(1)}, s32[6,64]{1,0:T(8,128)S(1)}, u32[]{:S(2)}, u32[]{:S(2)}) collective-permute-start(s32[6,64]{1,0:T(8,128)S(1)} %bitcast.49), channel_id=1, source_target_pairs={{0,4},{1,5},{2,6},{3,7},{4,12},{5,13},{6,14},{7,15},{12,8},{13,9},... | collective-permute-start | bytes 4616 | tf_op jit(solution)/shard_map/ppermute | solution.py:534
  26.4 26.1 %copy-start.6 = (bf16[2048,16]{0,1:T(8,128)(2,1)S(1)}, bf16[2048,16]{0,1:T(8,128)(2,1)}, u32[]{:S(2)}) copy-start(bf16[2048,16]{0,1:T(8,128)(2,1)} %param.25) | copy-start | bytes 196612
  29.0 27.0 %copy-start.1 = (bf16[1,2048,704]{1,2,0:T(8,128)(2,1)S(1)}, bf16[1,2048,704]{1,2,0:T(8,128)(2,1)}, u32[]{:S(2)}) copy-start(bf16[1,2048,704]{1,2,0:T(8,128)(2,1)} %param.27) | copy-start | bytes 8650756
  29.0 26.9 %copy-start.2 = (bf16[1,2048,704]{1,2,0:T(8,128)(2,1)S(1)}, bf16[1,2048,704]{1,2,0:T(8,128)(2,1)}, u32[]{:S(2)}) copy-start(bf16[1,2048,704]{1,2,0:T(8,128)(2,1)} %param.28) | copy-start | bytes 8650756
  30.5 9.4 %collective-permute-start.13 = (bf16[64,1024]{1,0:T(8,128)(2,1)S(1)}, bf16[64,1024]{1,0:T(8,128)(2,1)S(1)}, u32[]{:S(2)}, u32[]{:S(2)}) collective-permute-start(bf16[64,1024]{1,0:T(8,128)(2,1)S(1)} %get-tuple-element.98.refs_2_), channel_id=1, source_target_pairs={{4,0},{5,1},{6,2},{7,3},{12,4},{13,5},{14,6},{15,7},{8,12},{9,13},... | collective-permute-start | bytes 393224 | tf_op jit(solution)/shard_map/ppermute | solution.py:378
  30.9 10.2 %collective-permute-start.12 = (bf16[64,1024]{1,0:T(8,128)(2,1)S(1)}, bf16[64,1024]{1,0:T(8,128)(2,1)S(1)}, u32[]{:S(2)}, u32[]{:S(2)}) collective-permute-start(bf16[64,1024]{1,0:T(8,128)(2,1)S(1)} %get-tuple-element.99.refs_1_), channel_id=1, source_target_pairs={{0,4},{1,5},{2,6},{3,7},{4,12},{5,13},{6,14},{7,15},{12,8},{13,9},... | collective-permute-start | bytes 393224 | tf_op jit(solution)/shard_map/ppermute | solution.py:378
  32.8 1.9 %collective-permute-start.9 = (bf16[24,2048]{1,0:T(8,128)(2,1)S(1)}, bf16[24,2048]{1,0:T(8,128)(2,1)S(1)}, u32[]{:S(2)}, u32[]{:S(2)}) collective-permute-start(bf16[24,2048]{1,0:T(8,128)(2,1)S(1)} %get-tuple-element.102), channel_id=1, source_target_pairs={{0,1},{1,0},{2,3},{3,2},{4,5},{5,4},{6,7},{7,6},{8,9},{9,8},{10,11... | collective-permute-start | bytes 294920 | tf_op jit(solution)/shard_map/ppermute | solution.py:378
  32.9 5.7 %collective-permute-start.10 = (bf16[24,2048]{1,0:T(8,128)(2,1)S(1)}, bf16[24,2048]{1,0:T(8,128)(2,1)S(1)}, u32[]{:S(2)}, u32[]{:S(2)}) collective-permute-start(bf16[24,2048]{1,0:T(8,128)(2,1)S(1)} %get-tuple-element.103), channel_id=1, source_target_pairs={{0,2},{1,3},{2,0},{3,1},{4,6},{5,7},{6,4},{7,5},{8,10},{9,11},{10,... | collective-permute-start | bytes 294920 | tf_op jit(solution)/shard_map/ppermute | solution.py:378
  34.5 7.7 %collective-permute-start.11 = (bf16[24,2048]{1,0:T(8,128)(2,1)S(1)}, bf16[24,2048]{1,0:T(8,128)(2,1)S(1)}, u32[]{:S(2)}, u32[]{:S(2)}) collective-permute-start(bf16[24,2048]{1,0:T(8,128)(2,1)S(1)} %get-tuple-element.104), channel_id=1, source_target_pairs={{0,3},{1,2},{2,1},{3,0},{4,7},{5,6},{6,5},{7,4},{8,11},{9,10},{10,... | collective-permute-start | bytes 294920 | tf_op jit(solution)/shard_map/ppermute | solution.py:378
  34.8 7.5 %collective-permute-start.7 = (bf16[64,1024]{1,0:T(8,128)(2,1)S(1)}, bf16[64,1024]{1,0:T(8,128)(2,1)S(1)}, u32[]{:S(2)}, u32[]{:S(2)}) collective-permute-start(bf16[64,1024]{1,0:T(8,128)(2,1)S(1)} %get-tuple-element.98.refs_2_), channel_id=1, source_target_pairs={{0,4},{1,5},{2,6},{3,7},{4,12},{5,13},{6,14},{7,15},{12,8},{13,9},... | collective-permute-start | bytes 393224 | tf_op jit(solution)/shard_map/ppermute | solution.py:378
  38.7 6.5 %collective-permute-start.8 = (bf16[64,1024]{1,0:T(8,128)(2,1)S(1)}, bf16[64,1024]{1,0:T(8,128)(2,1)S(1)}, u32[]{:S(2)}, u32[]{:S(2)}) collective-permute-start(bf16[64,1024]{1,0:T(8,128)(2,1)S(1)} %get-tuple-element.99.refs_1_), channel_id=1, source_target_pairs={{4,0},{5,1},{6,2},{7,3},{12,4},{13,5},{14,6},{15,7},{8,12},{9,13},... | collective-permute-start | bytes 393224 | tf_op jit(solution)/shard_map/ppermute | solution.py:378
  39.9 7.9 %collective-permute-start.15 = (bf16[64,1024]{1,0:T(8,128)(2,1)S(1)}, bf16[64,1024]{1,0:T(8,128)(2,1)S(1)}, u32[]{:S(2)}, u32[]{:S(2)}) collective-permute-start(bf16[64,1024]{1,0:T(8,128)(2,1)S(1)} %collective-permute-done.13.refs_3_.refs_8_), channel_id=1, source_target_pairs={{4,0},{5,1},{6,2},{7,3},{12,4},{13,5},{14,6},{15,7},{8,12},{9,13},... | collective-permute-start | bytes 393224 | tf_op jit(solution)/shard_map/ppermute | solution.py:378
  41.1 9.9 %collective-permute-start.14 = (bf16[64,1024]{1,0:T(8,128)(2,1)S(1)}, bf16[64,1024]{1,0:T(8,128)(2,1)S(1)}, u32[]{:S(2)}, u32[]{:S(2)}) collective-permute-start(bf16[64,1024]{1,0:T(8,128)(2,1)S(1)} %collective-permute-done.12.refs_1_.refs_4_), channel_id=1, source_target_pairs={{0,4},{1,5},{2,6},{3,7},{4,12},{5,13},{6,14},{7,15},{12,8},{13,9},... | collective-permute-start | bytes 393224 | tf_op jit(solution)/shard_map/ppermute | solution.py:378
  42.2 3.2 %collective-permute-start.16 = (bf16[48,1024]{1,0:T(8,128)(2,1)S(1)}, bf16[48,1024]{1,0:T(8,128)(2,1)S(1)}, u32[]{:S(2)}, u32[]{:S(2)}) collective-permute-start(bf16[48,1024]{1,0:T(8,128)(2,1)S(1)} %get-tuple-element.124), channel_id=1, source_target_pairs={{0,1},{1,0},{2,3},{3,2},{4,5},{5,4},{6,7},{7,6},{8,9},{9,8},{10,11... | collective-permute-start | bytes 294920 | tf_op jit(solution)/shard_map/ppermute | solution.py:378
  42.3 10.7 %collective-permute-start.17 = (bf16[48,1024]{1,0:T(8,128)(2,1)S(1)}, bf16[48,1024]{1,0:T(8,128)(2,1)S(1)}, u32[]{:S(2)}, u32[]{:S(2)}) collective-permute-start(bf16[48,1024]{1,0:T(8,128)(2,1)S(1)} %get-tuple-element.125), channel_id=1, source_target_pairs={{0,2},{1,3},{2,0},{3,1},{4,6},{5,7},{6,4},{7,5},{8,10},{9,11},{10,... | collective-permute-start | bytes 294920 | tf_op jit(solution)/shard_map/ppermute | solution.py:378
  45.1 8.5 %collective-permute-start.18 = (bf16[48,1024]{1,0:T(8,128)(2,1)S(1)}, bf16[48,1024]{1,0:T(8,128)(2,1)S(1)}, u32[]{:S(2)}, u32[]{:S(2)}) collective-permute-start(bf16[48,1024]{1,0:T(8,128)(2,1)S(1)} %get-tuple-element.126), channel_id=1, source_target_pairs={{0,3},{1,2},{2,1},{3,0},{4,7},{5,6},{6,5},{7,4},{8,11},{9,10},{10,... | collective-permute-start | bytes 294920 | tf_op jit(solution)/shard_map/ppermute | solution.py:378
  45.4 8.7 %collective-permute-start.19 = (bf16[48,1024]{1,0:T(8,128)(2,1)S(1)}, bf16[48,1024]{1,0:T(8,128)(2,1)S(1)}, u32[]{:S(2)}, u32[]{:S(2)}) collective-permute-start(bf16[48,1024]{1,0:T(8,128)(2,1)S(1)} %get-tuple-element.128), channel_id=1, source_target_pairs={{0,1},{1,0},{2,3},{3,2},{4,5},{5,4},{6,7},{7,6},{8,9},{9,8},{10,11... | collective-permute-start | bytes 294920 | tf_op jit(solution)/shard_map/ppermute | solution.py:378
  47.8 7.2 %collective-permute-start.20 = (bf16[48,1024]{1,0:T(8,128)(2,1)S(1)}, bf16[48,1024]{1,0:T(8,128)(2,1)S(1)}, u32[]{:S(2)}, u32[]{:S(2)}) collective-permute-start(bf16[48,1024]{1,0:T(8,128)(2,1)S(1)} %get-tuple-element.129), channel_id=1, source_target_pairs={{0,2},{1,3},{2,0},{3,1},{4,6},{5,7},{6,4},{7,5},{8,10},{9,11},{10,... | collective-permute-start | bytes 294920 | tf_op jit(solution)/shard_map/ppermute | solution.py:378
  51.1 4.9 %collective-permute-start.21 = (bf16[48,1024]{1,0:T(8,128)(2,1)S(1)}, bf16[48,1024]{1,0:T(8,128)(2,1)S(1)}, u32[]{:S(2)}, u32[]{:S(2)}) collective-permute-start(bf16[48,1024]{1,0:T(8,128)(2,1)S(1)} %get-tuple-element.130), channel_id=1, source_target_pairs={{0,3},{1,2},{2,1},{3,0},{4,7},{5,6},{6,5},{7,4},{8,11},{9,10},{10,... | collective-permute-start | bytes 294920 | tf_op jit(solution)/shard_map/ppermute | solution.py:378
  53.0 5.9 %collective-permute-start.22 = (bf16[24,2048]{1,0:T(8,128)(2,1)S(1)}, bf16[24,2048]{1,0:T(8,128)(2,1)S(1)}, u32[]{:S(2)}, u32[]{:S(2)}) collective-permute-start(bf16[24,2048]{1,0:T(8,128)(2,1)S(1)} %get-tuple-element.148), channel_id=1, source_target_pairs={{0,1},{1,0},{2,3},{3,2},{4,5},{5,4},{6,7},{7,6},{8,9},{9,8},{10,11... | collective-permute-start | bytes 294920 | tf_op jit(solution)/shard_map/ppermute | solution.py:378
  53.6 5.7 %collective-permute-start.23 = (bf16[24,2048]{1,0:T(8,128)(2,1)S(1)}, bf16[24,2048]{1,0:T(8,128)(2,1)S(1)}, u32[]{:S(2)}, u32[]{:S(2)}) collective-permute-start(bf16[24,2048]{1,0:T(8,128)(2,1)S(1)} %get-tuple-element.149), channel_id=1, source_target_pairs={{0,2},{1,3},{2,0},{3,1},{4,6},{5,7},{6,4},{7,5},{8,10},{9,11},{10,... | collective-permute-start | bytes 294920 | tf_op jit(solution)/shard_map/ppermute | solution.py:378
  54.1 5.5 %collective-permute-start.24 = (bf16[24,2048]{1,0:T(8,128)(2,1)S(1)}, bf16[24,2048]{1,0:T(8,128)(2,1)S(1)}, u32[]{:S(2)}, u32[]{:S(2)}) collective-permute-start(bf16[24,2048]{1,0:T(8,128)(2,1)S(1)} %get-tuple-element.150), channel_id=1, source_target_pairs={{0,3},{1,2},{2,1},{3,0},{4,7},{5,6},{6,5},{7,4},{8,11},{9,10},{10,... | collective-permute-start | bytes 294920 | tf_op jit(solution)/shard_map/ppermute | solution.py:378
  62.0 4.4 %collective-permute-start.31 = (bf16[24,2048]{1,0:T(8,128)(2,1)S(1)}, bf16[24,2048]{1,0:T(8,128)(2,1)S(1)}, u32[]{:S(2)}, u32[]{:S(2)}) collective-permute-start(bf16[24,2048]{1,0:T(8,128)(2,1)S(1)} %get-tuple-element.167), channel_id=1, source_target_pairs={{0,1},{1,0},{2,3},{3,2},{4,5},{5,4},{6,7},{7,6},{8,9},{9,8},{10,11... | collective-permute-start | bytes 294920 | tf_op jit(solution)/shard_map/ppermute | solution.py:378
  62.8 5.2 %collective-permute-start.32 = (bf16[24,2048]{1,0:T(8,128)(2,1)S(1)}, bf16[24,2048]{1,0:T(8,128)(2,1)S(1)}, u32[]{:S(2)}, u32[]{:S(2)}) collective-permute-start(bf16[24,2048]{1,0:T(8,128)(2,1)S(1)} %get-tuple-element.168), channel_id=1, source_target_pairs={{0,2},{1,3},{2,0},{3,1},{4,6},{5,7},{6,4},{7,5},{8,10},{9,11},{10,... | collective-permute-start | bytes 294920 | tf_op jit(solution)/shard_map/ppermute | solution.py:378
  64.3 5.7 %collective-permute-start.33 = (bf16[24,2048]{1,0:T(8,128)(2,1)S(1)}, bf16[24,2048]{1,0:T(8,128)(2,1)S(1)}, u32[]{:S(2)}, u32[]{:S(2)}) collective-permute-start(bf16[24,2048]{1,0:T(8,128)(2,1)S(1)} %get-tuple-element.169), channel_id=1, source_target_pairs={{0,3},{1,2},{2,1},{3,0},{4,7},{5,6},{6,5},{7,4},{8,11},{9,10},{10,... | collective-permute-start | bytes 294920 | tf_op jit(solution)/shard_map/ppermute | solution.py:378
  64.3 7.5 %collective-permute-start.28 = (bf16[48,1024]{1,0:T(8,128)(2,1)S(1)}, bf16[48,1024]{1,0:T(8,128)(2,1)S(1)}, u32[]{:S(2)}, u32[]{:S(2)}) collective-permute-start(bf16[48,1024]{1,0:T(8,128)(2,1)S(1)} %get-tuple-element.158), channel_id=1, source_target_pairs={{0,1},{1,0},{2,3},{3,2},{4,5},{5,4},{6,7},{7,6},{8,9},{9,8},{10,11... | collective-permute-start | bytes 294920 | tf_op jit(solution)/shard_map/ppermute | solution.py:378
  64.9 7.6 %collective-permute-start.29 = (bf16[48,1024]{1,0:T(8,128)(2,1)S(1)}, bf16[48,1024]{1,0:T(8,128)(2,1)S(1)}, u32[]{:S(2)}, u32[]{:S(2)}) collective-permute-start(bf16[48,1024]{1,0:T(8,128)(2,1)S(1)} %get-tuple-element.159), channel_id=1, source_target_pairs={{0,2},{1,3},{2,0},{3,1},{4,6},{5,7},{6,4},{7,5},{8,10},{9,11},{10,... | collective-permute-start | bytes 294920 | tf_op jit(solution)/shard_map/ppermute | solution.py:378
  66.4 7.4 %collective-permute-start.37 = (bf16[48,1024]{1,0:T(8,128)(2,1)S(1)}, bf16[48,1024]{1,0:T(8,128)(2,1)S(1)}, u32[]{:S(2)}, u32[]{:S(2)}) collective-permute-start(bf16[48,1024]{1,0:T(8,128)(2,1)S(1)} %get-tuple-element.174), channel_id=1, source_target_pairs={{0,1},{1,0},{2,3},{3,2},{4,5},{5,4},{6,7},{7,6},{8,9},{9,8},{10,11... | collective-permute-start | bytes 294920 | tf_op jit(solution)/shard_map/ppermute | solution.py:378
  68.0 6.3 %collective-permute-start.38 = (bf16[48,1024]{1,0:T(8,128)(2,1)S(1)}, bf16[48,1024]{1,0:T(8,128)(2,1)S(1)}, u32[]{:S(2)}, u32[]{:S(2)}) collective-permute-start(bf16[48,1024]{1,0:T(8,128)(2,1)S(1)} %get-tuple-element.175), channel_id=1, source_target_pairs={{0,2},{1,3},{2,0},{3,1},{4,6},{5,7},{6,4},{7,5},{8,10},{9,11},{10,... | collective-permute-start | bytes 294920 | tf_op jit(solution)/shard_map/ppermute | solution.py:378
  69.9 5.7 %collective-permute-start.39 = (bf16[48,1024]{1,0:T(8,128)(2,1)S(1)}, bf16[48,1024]{1,0:T(8,128)(2,1)S(1)}, u32[]{:S(2)}, u32[]{:S(2)}) collective-permute-start(bf16[48,1024]{1,0:T(8,128)(2,1)S(1)} %get-tuple-element.176), channel_id=1, source_target_pairs={{0,3},{1,2},{2,1},{3,0},{4,7},{5,6},{6,5},{7,4},{8,11},{9,10},{10,... | collective-permute-start | bytes 294920 | tf_op jit(solution)/shard_map/ppermute | solution.py:378
  71.8 8.3 %collective-permute-start.34 = (bf16[64,1024]{1,0:T(8,128)(2,1)S(1)}, bf16[64,1024]{1,0:T(8,128)(2,1)S(1)}, u32[]{:S(2)}, u32[]{:S(2)}) collective-permute-start(bf16[64,1024]{1,0:T(8,128)(2,1)S(1)} %get-tuple-element.170), channel_id=1, source_target_pairs={{4,0},{5,1},{6,2},{7,3},{12,4},{13,5},{14,6},{15,7},{8,12},{9,13},... | collective-permute-start | bytes 393224 | tf_op jit(solution)/shard_map/ppermute | solution.py:378
  72.6 8.9 %collective-permute-start.35 = (bf16[64,1024]{1,0:T(8,128)(2,1)S(1)}, bf16[64,1024]{1,0:T(8,128)(2,1)S(1)}, u32[]{:S(2)}, u32[]{:S(2)}) collective-permute-start(bf16[64,1024]{1,0:T(8,128)(2,1)S(1)} %get-tuple-element.171), channel_id=1, source_target_pairs={{0,4},{1,5},{2,6},{3,7},{4,12},{5,13},{6,14},{7,15},{12,8},{13,9},... | collective-permute-start | bytes 393224 | tf_op jit(solution)/shard_map/ppermute | solution.py:378
  73.9 4.7 %collective-permute-start.30 = (bf16[48,1024]{1,0:T(8,128)(2,1)S(1)}, bf16[48,1024]{1,0:T(8,128)(2,1)S(1)}, u32[]{:S(2)}, u32[]{:S(2)}) collective-permute-start(bf16[48,1024]{1,0:T(8,128)(2,1)S(1)} %get-tuple-element.160), channel_id=1, source_target_pairs={{0,3},{1,2},{2,1},{3,0},{4,7},{5,6},{6,5},{7,4},{8,11},{9,10},{10,... | collective-permute-start | bytes 294920 | tf_op jit(solution)/shard_map/ppermute | solution.py:378
  74.3 8.2 %collective-permute-start.25 = (bf16[24,2048]{1,0:T(8,128)(2,1)S(1)}, bf16[24,2048]{1,0:T(8,128)(2,1)S(1)}, u32[]{:S(2)}, u32[]{:S(2)}) collective-permute-start(bf16[24,2048]{1,0:T(8,128)(2,1)S(1)} %get-tuple-element.152), channel_id=1, source_target_pairs={{0,1},{1,0},{2,3},{3,2},{4,5},{5,4},{6,7},{7,6},{8,9},{9,8},{10,11... | collective-permute-start | bytes 294920 | tf_op jit(solution)/shard_map/ppermute | solution.py:378
  75.7 9.1 %collective-permute-start.26 = (bf16[24,2048]{1,0:T(8,128)(2,1)S(1)}, bf16[24,2048]{1,0:T(8,128)(2,1)S(1)}, u32[]{:S(2)}, u32[]{:S(2)}) collective-permute-start(bf16[24,2048]{1,0:T(8,128)(2,1)S(1)} %get-tuple-element.153), channel_id=1, source_target_pairs={{0,2},{1,3},{2,0},{3,1},{4,6},{5,7},{6,4},{7,5},{8,10},{9,11},{10,... | collective-permute-start | bytes 294920 | tf_op jit(solution)/shard_map/ppermute | solution.py:378
  78.5 11.2 %collective-permute-start.40 = (bf16[64,1024]{1,0:T(8,128)(2,1)S(1)}, bf16[64,1024]{1,0:T(8,128)(2,1)S(1)}, u32[]{:S(2)}, u32[]{:S(2)}) collective-permute-start(bf16[64,1024]{1,0:T(8,128)(2,1)S(1)} %get-tuple-element.177), channel_id=1, source_target_pairs={{0,4},{1,5},{2,6},{3,7},{4,12},{5,13},{6,14},{7,15},{12,8},{13,9},... | collective-permute-start | bytes 393224 | tf_op jit(solution)/shard_map/ppermute | solution.py:378
  80.1 9.7 %collective-permute-start.41 = (bf16[64,1024]{1,0:T(8,128)(2,1)S(1)}, bf16[64,1024]{1,0:T(8,128)(2,1)S(1)}, u32[]{:S(2)}, u32[]{:S(2)}) collective-permute-start(bf16[64,1024]{1,0:T(8,128)(2,1)S(1)} %get-tuple-element.178), channel_id=1, source_target_pairs={{4,0},{5,1},{6,2},{7,3},{12,4},{13,5},{14,6},{15,7},{8,12},{9,13},... | collective-permute-start | bytes 393224 | tf_op jit(solution)/shard_map/ppermute | solution.py:378
  81.8 8.5 %collective-permute-start.36 = (bf16[64,1024]{1,0:T(8,128)(2,1)S(1)}, bf16[64,1024]{1,0:T(8,128)(2,1)S(1)}, u32[]{:S(2)}, u32[]{:S(2)}) collective-permute-start(bf16[64,1024]{1,0:T(8,128)(2,1)S(1)} %get-tuple-element.172), channel_id=1, source_target_pairs={{0,4},{1,5},{2,6},{3,7},{4,12},{5,13},{6,14},{7,15},{12,8},{13,9},... | collective-permute-start | bytes 393224 | tf_op jit(solution)/shard_map/ppermute | solution.py:378
  82.5 10.5 %collective-permute-start.42 = (bf16[64,1024]{1,0:T(8,128)(2,1)S(1)}, bf16[64,1024]{1,0:T(8,128)(2,1)S(1)}, u32[]{:S(2)}, u32[]{:S(2)}) collective-permute-start(bf16[64,1024]{1,0:T(8,128)(2,1)S(1)} %get-tuple-element.179), channel_id=1, source_target_pairs={{4,0},{5,1},{6,2},{7,3},{12,4},{13,5},{14,6},{15,7},{8,12},{9,13},... | collective-permute-start | bytes 393224 | tf_op jit(solution)/shard_map/ppermute | solution.py:378
  84.8 5.0 %collective-permute-start.27 = (bf16[24,2048]{1,0:T(8,128)(2,1)S(1)}, bf16[24,2048]{1,0:T(8,128)(2,1)S(1)}, u32[]{:S(2)}, u32[]{:S(2)}) collective-permute-start(bf16[24,2048]{1,0:T(8,128)(2,1)S(1)} %get-tuple-element.154), channel_id=1, source_target_pairs={{0,3},{1,2},{2,1},{3,0},{4,7},{5,6},{6,5},{7,4},{8,11},{9,10},{10,... | collective-permute-start | bytes 294920 | tf_op jit(solution)/shard_map/ppermute | solution.py:378

commit v4 on v3

--- a/solution.py
+++ b/solution.py
@@ -56,7 +56,7 @@
     )
 
 
-def project_paired(mixed_latent, w_uv, w_out):
+def project_paired(give, kept, w_uv, w_out):
     pair = [(0, 1), (1, 0)]
     ep = lax.axis_size("ep")
     twins = [(i, i ^ 1) for i in range(ep)]
@@ -75,9 +75,6 @@
         "fsdp",
         pair,
     )
-    by_head = jnp.swapaxes(mixed_latent, 0, 1)
-    give = lax.dynamic_slice_in_dim(by_head, (1 - side) * heads, heads, 0)
-    kept = lax.dynamic_slice_in_dim(by_head, side * heads, heads, 0)
     other = lax.ppermute(give, "fsdp", pair)
     theirs = lax.ppermute(mine, "ep", twins)
     far = jnp.where(
@@ -86,7 +83,7 @@
     near = own_heads(w_uv, side)
     full = jnp.where(side == 0, jnp.concatenate([near, far], 0), jnp.concatenate([far, near], 0))
     full = jnp.swapaxes(full, 0, 1)
-    count, width = mixed_latent.shape[0], w_out.shape[1]
+    count, width = kept.shape[1], w_out.shape[1]
 
     def project(mixed, dtype):
         return fused(
@@ -102,6 +99,79 @@
     partial = project(other, jnp.bfloat16)
     back = lax.ppermute(partial, "fsdp", pair)
     return project(kept, jnp.float32), back
+
+
+def attend_kernel(head_count, *refs):
+    sources, (give_ref, kept_ref) = refs[:6], refs[6:8]
+    q_ref, rope_ref, keys_ref, ropes_ref, sem = refs[8:]
+    cached = sources[2].shape[0]
+    targets = (
+        q_ref,
+        rope_ref,
+        keys_ref.at[:cached],
+        ropes_ref.at[:cached],
+        keys_ref.at[cached:],
+        ropes_ref.at[cached:],
+    )
+    copies = [
+        pltpu.make_async_copy(source, target, sem.at[n])
+        for n, (source, target) in enumerate(zip(sources, targets))
+    ]
+    for copy in copies:
+        copy.start()
+    side = lax.axis_index("fsdp")
+    heads, count, _ = kept_ref.shape
+    for copy in copies:
+        copy.wait()
+    keys = keys_ref[...]
+    ropes = ropes_ref[...]
+    scores = dot_rows(q_ref[...], keys) + dot_rows(rope_ref[...], ropes)
+    scores = scores * softmax_scale
+    row = lax.broadcasted_iota(jnp.int32, scores.shape, 0)
+    key = lax.broadcasted_iota(jnp.int32, scores.shape, 1)
+    visible = (key - cached) * head_count <= row
+    top = jnp.max(jnp.where(visible, scores, -jnp.inf), axis=1, keepdims=True)
+    exponent = jnp.where(visible, jnp.exp(scores - top), 0.0)
+    weights = (exponent / jnp.sum(exponent, axis=1, keepdims=True)).astype(jnp.bfloat16)
+    mixed = jnp.dot(weights, keys, preferred_element_type=jnp.float32).astype(jnp.bfloat16)
+    token = lax.broadcasted_iota(jnp.int32, (count, count * head_count), 0)
+    source = lax.broadcasted_iota(jnp.int32, (count, count * head_count), 1)
+    for which, out in ((1 - side, give_ref), (side, kept_ref)):
+        for h in range(heads):
+            found = (source == token * head_count + which * heads + h).astype(jnp.float32)
+            rows = jnp.dot(
+                found.astype(jnp.bfloat16), mixed, preferred_element_type=jnp.float32
+            )
+            out[h] = rows.astype(jnp.bfloat16)
+
+
+def attend_by_head(heads, q_latent, q_rope, cache_latent, cache_rope, new_latent, new_rope):
+    count, head_count, width = q_latent.shape
+    keys = cache_latent.shape[0] + new_latent.shape[0]
+    rows = count * head_count
+    rope_width = q_rope.shape[2]
+    shapes = ((rows, width), (rows, rope_width), (keys, width), (keys, rope_width))
+    return pl.pallas_call(
+        functools.partial(attend_kernel, head_count),
+        out_shape=[jax.ShapeDtypeStruct((heads, count, width), jnp.bfloat16)] * 2,
+        in_specs=[pl.BlockSpec(memory_space=pltpu.HBM)] * 6,
+        out_specs=[pl.BlockSpec(memory_space=pltpu.VMEM)] * 2,
+        scratch_shapes=[pltpu.VMEM(shape, jnp.bfloat16) for shape in shapes]
+        + [pltpu.SemaphoreType.DMA((6,))],
+        cost_estimate=pl.CostEstimate(
+            flops=2 * rows * width * (2 * keys + rows),
+            bytes_accessed=8 * rows * width,
+            transcendentals=rows * keys,
+        ),
+        compiler_params=pltpu.CompilerParams(vmem_limit_bytes=12 << 20),
+    )(
+        q_latent.reshape(rows, width),
+        q_rope.reshape(rows, rope_width),
+        cache_latent,
+        cache_rope,
+        new_latent,
+        new_rope,
+    )
 
 
 def project_kernel(mixed_ref, values_ref, out_w_ref, result_ref):
@@ -511,14 +581,19 @@
     w_up,
     w_down,
 ):
-    mixed_latent = attend_local(
-        q_latent[0], q_rope[0], cache_latent[0], cache_rope[0], new_latent[0], new_rope[0]
-    )
-    new_count = mixed_latent.shape[0]
+    sequence = (
+        q_latent[0],
+        q_rope[0],
+        cache_latent[0],
+        cache_rope[0],
+        new_latent[0],
+        new_rope[0],
+    )
+    new_count = q_latent.shape[1]
     expert_count = lax.axis_size("ep")
     capacity = new_count * expert_ids.shape[2] // expert_count
     if lax.axis_size("fsdp") != 2 or expert_count != 16:
-        projected = project_gathered(mixed_latent, w_uv, w_out)
+        projected = project_gathered(attend_local(*sequence), w_uv, w_out)
         hidden = x_resid[0].astype(jnp.float32) + projected
         normed = hidden * lax.rsqrt(jnp.mean(hidden * hidden, axis=-1, keepdims=True) + epsilon)
         normed = (normed * norm_gain).astype(jnp.bfloat16)
@@ -538,7 +613,8 @@
         [(part.shape, jnp.int32) for part in ids],
         *ids,
     )
-    part, back = project_paired(mixed_latent, w_uv, w_out)
+    give, kept = attend_by_head(w_out.shape[0] // w_uv.shape[2], *sequence)
+    part, back = project_paired(give, kept, w_uv, w_out)
     back, targets = lax.optimization_barrier((back, targets))
     width = part.shape[1]
     halves = (new_count, width // 2)

time: 94.2 us -> 100 us (1.062)
  local copies, waits for them, and re-layouts: 2.41 us -> 8.03 us
  matrix products: 3.93 us -> 0 us
  Pallas kernels: 11 us -> 13 us
  waiting for transfers between devices: 27.9 us -> 29.5 us
    unnamed x23 -> x33, local copies, waits for them, and re-layouts: 1.92 us -> 7.12 us
    dot_general x3 -> x0, matrix products: 3.93 us -> none  [the longest x1 1.42 us: attend_local(): jnp.dot(query_rows, keys_latent.T, preferred_element_type=jnp.float32)]
    ppermute x1, waiting for transfers between devices: 0.01 us -> 3.5 us  [project_paired(): lax.ppermute(lax.dynamic_slice(w_uv, (lane * rows, (1 - side) * heads, 0)...]
    ppermute x1, waiting for transfers between devices: 6.37 us -> 3.91 us  [project_paired(): other = lax.ppermute(give, 'fsdp', pair)]
    pallas_call x0 -> x1, Pallas kernels: none -> 1.99 us  [attend_by_head(): pl.pallas_call(functools.partial(attend_kernel, head_count), out_shape=[j...]
  transfers between devices with their start and end apart: 43 -> 43, of which waited for: 17 -> 19; matrix products, arithmetic and copies ran while one was open for 7% -> 3% of each run, Pallas kernels for 7% -> 8%
where the time goes in v4:
time: 100 us; the launch traced here: 99.9 us
  starting transfers between devices  47.1 us (47%)
  waiting for transfers between devices  29.5 us (30%)
  Pallas kernels  13 us (13%)
  local copies, waits for them, and re-layouts  8.03 us (8%)
  other arithmetic  1.2 us (1%)
    ppermute x36, starting transfers between devices, send(): return lax.ppermute(value, 'ep', steps)  34.9 us
    ppermute x36, waiting for transfers between devices, send(): return lax.ppermute(value, 'ep', steps)  19.6 us
    pallas_call x15, Pallas kernels, fused(): pl.pallas_call(body, out_shape=[jax.ShapeDtypeStruct(shape, dtype) for sh...  11 us
    unnamed x33, local copies, waits for them, and re-layouts  7.12 us
    ppermute x1, waiting for transfers between devices, project_paired(): other = lax.ppermute(give, 'fsdp', pair)  3.91 us
    ppermute x1, starting transfers between devices, per_device(): ids.append(lax.ppermute(ids[0], 'ep', across))  3.6 us
    ppermute x1, waiting for transfers between devices, project_paired(): lax.ppermute(lax.dynamic_slice(w_uv, (lane * rows, (1 - side) * heads, 0)...  3.5 us
    ppermute x1, starting transfers between devices, project_paired(): lax.ppermute(lax.dynamic_slice(w_uv, (lane * rows, (1 - side) * heads, 0)...  3.03 us
  transfers between devices with their start and end apart: 43, of which 19 were waited for; matrix products, arithmetic and copies ran while one was open for 3% of the time, Pallas kernels for 8%

profile of v4, /device:TPU:0, one launch (start us, length us, event | category | flops | bytes accessed | tf_op | source)
XLA Modules:
  0.0 99.9 jit_solution(12193552536006033676)
XLA Ops:
  0.7 1.0 %copy-done = bf16[256,8,128]{2,1,0:T(8,128)(2,1)S(1)} copy-done((bf16[256,8,128]{2,1,0:T(8,128)(2,1)S(1)}, bf16[256,8,128]{2,1,0:T(8,128)(2,1)}, u32[]{:S(2)}) %copy-start) | copy-done | bytes 524312
  1.8 3.0 %collective-permute-start = (bf16[128,4,128]{2,0,1:T(8,128)(2,1)S(1)}, bf16[128,4,128]{2,0,1:T(8,128)(2,1)S(1)}, u32[]{:S(2)}, u32[]{:S(2)}) collective-permute-start(bf16[128,4,128]{2,0,1:T(8,128)(2,1)S(1)} %copy.21), channel_id=1, source_target_pairs={{0,16},{16,0},{1,17},{17,1},{2,18},{18,2},{3,19},{19,3},{4,20},{20... | collective-permute-start | bytes 393224 | tf_op jit(solution)/shard_map/ppermute | solution.py:71
  4.8 3.5 %collective-permute-done = bf16[128,4,128]{2,0,1:T(8,128)(2,1)S(1)} collective-permute-done((bf16[128,4,128]{2,0,1:T(8,128)(2,1)S(1)}, bf16[128,4,128]{2,0,1:T(8,128)(2,1)S(1)}, u32[]{:S(2)}, u32[]{:S(2)}) %collective-permute-start) | collective-permute-done | bytes 131104 | tf_op jit(solution)/shard_map/ppermute | solution.py:71
  8.3 1.0 %copy-done.8 = bf16[1,64,8,512]{3,2,1,0:T(8,128)(2,1)S(1)} copy-done((bf16[1,64,8,512]{3,2,1,0:T(8,128)(2,1)S(1)}, bf16[1,64,8,512]{3,2,1,0:T(8,128)(2,1)}, u32[]{:S(2)}) %copy-start.8) | copy-done | bytes 524312
  9.4 0.9 copy-done.9
  10.3 0.8 copy-done.10
  11.1 0.8 copy-done.11
  11.9 0.7 copy-done.12
  12.7 0.7 copy-done.13
  13.4 2.0 %shard_map.158 = (bf16[4,64,512]{2,1,0:T(8,128)(2,1)S(1)}, bf16[4,64,512]{2,1,0:T(8,128)(2,1)S(1)}) custom-call(bf16[512,512]{1,0:T(8,128)(2,1)S(1)} %bitcast.35, bf16[512,64]{1,0:T(8,128)(2,1)S(1)} %bitcast.36, bf16[64,512]{1,0:T(8,128)(2,1)S(1)} %bitcast.37, bf16[64,64]{1,0:T(8,128)(2,1)S(1)} %bitcast.39, bf16[64,512]{1,0:T(8,128)(2,1)S(1)} %bitcast.38, ...), custom_call_target="tpu_custom_call" | custom-call | flops 402653184 | bytes 2097152 | tf_op jit(solution)/shard_map/pallas_call | solution.py:154
  15.4 1.8 %collective-permute-start.2 = (bf16[4,64,512]{2,1,0:T(8,128)(2,1)S(1)}, bf16[4,64,512]{2,1,0:T(8,128)(2,1)S(1)}, u32[]{:S(2)}, u32[]{:S(2)}) collective-permute-start(bf16[4,64,512]{2,1,0:T(8,128)(2,1)S(1)} %get-tuple-element.94), channel_id=1, source_target_pairs={{0,16},{16,0},{1,17},{17,1},{2,18},{18,2},{3,19},{19,3},{4,20},{20... | collective-permute-start | bytes 786440 | tf_op jit(solution)/shard_map/ppermute | solution.py:78
  17.2 0.8 constant_dynamic-slice_fusion.1
  18.0 1.0 copy.20
  19.0 1.1 %maximum_select_fusion.1 = bf16[256,4,128]{2,0,1:T(8,128)(2,1)S(1)} fusion(bf16[128,4,128]{2,0,1:T(8,128)(2,1)} %collective-permute-done.1, bf16[128,4,128]{2,0,1:T(8,128)(2,1)S(1)} %collective-permute-done, pred[]{:T(512)S(6)} %eq.9), kind=kLoop, calls=%fused_computation.2 | loop fusion | flops 1179648 | bytes 524289 | tf_op jit(solution)/shard_map/jit(_where)/select_n | solution.py:80
  20.3 3.9 %collective-permute-done.2.mixed_ref = bf16[4,64,512]{2,1,0:T(8,128)(2,1)S(1)} collective-permute-done((bf16[4,64,512]{2,1,0:T(8,128)(2,1)S(1)}, bf16[4,64,512]{2,1,0:T(8,128)(2,1)S(1)}, u32[]{:S(2)}, u32[]{:S(2)}) %collective-permute-start.2) | collective-permute-done | bytes 262176 | tf_op jit(solution)/shard_map/ppermute | solution.py:78
  24.2 0.6 shard_map.160
  24.8 1.8 %collective-permute-start.3 = (bf16[64,2048]{1,0:T(8,128)(2,1)S(1)}, bf16[64,2048]{1,0:T(8,128)(2,1)S(1)}, u32[]{:S(2)}, u32[]{:S(2)}) collective-permute-start(bf16[64,2048]{1,0:T(8,128)(2,1)S(1)} %shard_map.160), channel_id=1, source_target_pairs={{0,16},{16,0},{1,17},{17,1},{2,18},{18,2},{3,19},{19,3},{4,20},{20... | collective-permute-start | bytes 786440 | tf_op jit(solution)/shard_map/ppermute | solution.py:100
  26.6 3.6 %collective-permute-start.6 = (s32[6,64]{1,0:T(8,128)S(1)}, s32[6,64]{1,0:T(8,128)S(1)}, u32[]{:S(2)}, u32[]{:S(2)}) collective-permute-start(s32[6,64]{1,0:T(8,128)S(1)} %bitcast.30), channel_id=1, source_target_pairs={{0,12},{1,13},{2,14},{3,15},{4,8},{5,9},{6,10},{7,11},{8,4},{9,5},... | collective-permute-start | bytes 4616 | tf_op jit(solution)/shard_map/ppermute | solution.py:610
  30.2 2.0 %collective-permute-start.4 = (s32[6,64]{1,0:T(8,128)S(1)}, s32[6,64]{1,0:T(8,128)S(1)}, u32[]{:S(2)}, u32[]{:S(2)}) collective-permute-start(s32[6,64]{1,0:T(8,128)S(1)} %bitcast.32), channel_id=1, source_target_pairs={{0,4},{1,5},{2,6},{3,7},{4,12},{5,13},{6,14},{7,15},{12,8},{13,9},... | collective-permute-start | bytes 4616 | tf_op jit(solution)/shard_map/ppermute | solution.py:609
  32.2 1.6 %collective-permute-done.5.refs_2_ = s32[6,64]{1,0:T(8,128)S(1)} collective-permute-done((s32[6,64]{1,0:T(8,128)S(1)}, s32[6,64]{1,0:T(8,128)S(1)}, u32[]{:S(2)}, u32[]{:S(2)}) %collective-permute-start.5) | collective-permute-done | bytes 1568 | tf_op jit(solution)/shard_map/ppermute | solution.py:609
  33.8 0.9 collective-permute-done.4.refs_1_
  34.9 0.6 shard_map.159.part_ref
  35.6 0.9 shard_map.162
  36.5 2.0 %collective-permute-start.12 = (bf16[64,1024]{1,0:T(8,128)(2,1)S(1)}, bf16[64,1024]{1,0:T(8,128)(2,1)S(1)}, u32[]{:S(2)}, u32[]{:S(2)}) collective-permute-start(bf16[64,1024]{1,0:T(8,128)(2,1)S(1)} %get-tuple-element.103.refs_1_), channel_id=1, source_target_pairs={{0,4},{1,5},{2,6},{3,7},{4,12},{5,13},{6,14},{7,15},{12,8},{13,9},... | collective-permute-start | bytes 393224 | tf_op jit(solution)/shard_map/ppermute | solution.py:448
  38.8 1.6 %collective-permute-start.10 = (bf16[24,2048]{1,0:T(8,128)(2,1)S(1)}, bf16[24,2048]{1,0:T(8,128)(2,1)S(1)}, u32[]{:S(2)}, u32[]{:S(2)}) collective-permute-start(bf16[24,2048]{1,0:T(8,128)(2,1)S(1)} %get-tuple-element.107), channel_id=1, source_target_pairs={{0,2},{1,3},{2,0},{3,1},{4,6},{5,7},{6,4},{7,5},{8,10},{9,11},{10,... | collective-permute-start | bytes 294920 | tf_op jit(solution)/shard_map/ppermute | solution.py:448
  40.7 2.0 %collective-permute-start.7 = (bf16[64,1024]{1,0:T(8,128)(2,1)S(1)}, bf16[64,1024]{1,0:T(8,128)(2,1)S(1)}, u32[]{:S(2)}, u32[]{:S(2)}) collective-permute-start(bf16[64,1024]{1,0:T(8,128)(2,1)S(1)} %get-tuple-element.102.refs_2_), channel_id=1, source_target_pairs={{0,4},{1,5},{2,6},{3,7},{4,12},{5,13},{6,14},{7,15},{12,8},{13,9},... | collective-permute-start | bytes 393224 | tf_op jit(solution)/shard_map/ppermute | solution.py:448
  42.7 1.9 %collective-permute-done.10.refs_10_ = bf16[24,2048]{1,0:T(8,128)(2,1)S(1)} collective-permute-done((bf16[24,2048]{1,0:T(8,128)(2,1)S(1)}, bf16[24,2048]{1,0:T(8,128)(2,1)S(1)}, u32[]{:S(2)}, u32[]{:S(2)}) %collective-permute-start.10) | collective-permute-done | bytes 98336 | tf_op jit(solution)/shard_map/ppermute | solution.py:448
  44.6 0.9 collective-permute-start.8
  45.5 1.5 %collective-permute-start.15 = (bf16[64,1024]{1,0:T(8,128)(2,1)S(1)}, bf16[64,1024]{1,0:T(8,128)(2,1)S(1)}, u32[]{:S(2)}, u32[]{:S(2)}) collective-permute-start(bf16[64,1024]{1,0:T(8,128)(2,1)S(1)} %collective-permute-done.13.refs_3_.refs_8_), channel_id=1, source_target_pairs={{4,0},{5,1},{6,2},{7,3},{12,4},{13,5},{14,6},{15,7},{8,12},{9,13},... | collective-permute-start | bytes 393224 | tf_op jit(solution)/shard_map/ppermute | solution.py:448
  47.0 0.5 collective-permute-start.14
  47.9 1.6 %collective-permute-start.17 = (bf16[48,1024]{1,0:T(8,128)(2,1)S(1)}, bf16[48,1024]{1,0:T(8,128)(2,1)S(1)}, u32[]{:S(2)}, u32[]{:S(2)}) collective-permute-start(bf16[48,1024]{1,0:T(8,128)(2,1)S(1)} %get-tuple-element.129), channel_id=1, source_target_pairs={{0,2},{1,3},{2,0},{3,1},{4,6},{5,7},{6,4},{7,5},{8,10},{9,11},{10,... | collective-permute-start | bytes 294920 | tf_op jit(solution)/shard_map/ppermute | solution.py:448
  49.5 1.5 %collective-permute-done.8.refs_7_.refs_3_ = bf16[64,1024]{1,0:T(8,128)(2,1)S(1)} collective-permute-done((bf16[64,1024]{1,0:T(8,128)(2,1)S(1)}, bf16[64,1024]{1,0:T(8,128)(2,1)S(1)}, u32[]{:S(2)}, u32[]{:S(2)}) %collective-permute-start.8) | collective-permute-done | bytes 131104 | tf_op jit(solution)/shard_map/ppermute | solution.py:448
  51.3 1.7 %collective-permute-start.19 = (bf16[48,1024]{1,0:T(8,128)(2,1)S(1)}, bf16[48,1024]{1,0:T(8,128)(2,1)S(1)}, u32[]{:S(2)}, u32[]{:S(2)}) collective-permute-start(bf16[48,1024]{1,0:T(8,128)(2,1)S(1)} %get-tuple-element.132), channel_id=1, source_target_pairs={{0,1},{1,0},{2,3},{3,2},{4,5},{5,4},{6,7},{7,6},{8,9},{9,8},{10,11... | collective-permute-start | bytes 294920 | tf_op jit(solution)/shard_map/ppermute | solution.py:448
  53.0 0.7 collective-permute-done.15.refs_2_.refs_11_
  53.7 1.5 %collective-permute-start.20 = (bf16[48,1024]{1,0:T(8,128)(2,1)S(1)}, bf16[48,1024]{1,0:T(8,128)(2,1)S(1)}, u32[]{:S(2)}, u32[]{:S(2)}) collective-permute-start(bf16[48,1024]{1,0:T(8,128)(2,1)S(1)} %get-tuple-element.133), channel_id=1, source_target_pairs={{0,2},{1,3},{2,0},{3,1},{4,6},{5,7},{6,4},{7,5},{8,10},{9,11},{10,... | collective-permute-start | bytes 294920 | tf_op jit(solution)/shard_map/ppermute | solution.py:448
  55.2 1.7 %collective-permute-done.14.refs_1_.refs_10_ = bf16[64,1024]{1,0:T(8,128)(2,1)S(1)} collective-permute-done((bf16[64,1024]{1,0:T(8,128)(2,1)S(1)}, bf16[64,1024]{1,0:T(8,128)(2,1)S(1)}, u32[]{:S(2)}, u32[]{:S(2)}) %collective-permute-start.14) | collective-permute-done | bytes 131104 | tf_op jit(solution)/shard_map/ppermute | solution.py:448
  57.0 1.1 %collective-permute-start.21 = (bf16[48,1024]{1,0:T(8,128)(2,1)S(1)}, bf16[48,1024]{1,0:T(8,128)(2,1)S(1)}, u32[]{:S(2)}, u32[]{:S(2)}) collective-permute-start(bf16[48,1024]{1,0:T(8,128)(2,1)S(1)} %get-tuple-element.134), channel_id=1, source_target_pairs={{0,3},{1,2},{2,1},{3,0},{4,7},{5,6},{6,5},{7,4},{8,11},{9,10},{10,... | collective-permute-start | bytes 294920 | tf_op jit(solution)/shard_map/ppermute | solution.py:448
  58.4 0.5 shard_map.166
  58.9 0.6 collective-permute-start.22
  59.5 0.5 collective-permute-start.23
  60.0 0.9 collective-permute-start.24
  60.9 0.9 collective-permute-done.21.refs_7_
  61.9 3.0 %shard_map.168 = (bf16[48,1024]{1,0:T(8,128)(2,1)S(1)}, bf16[48,1024]{1,0:T(8,128)(2,1)S(1)}, bf16[48,1024]{1,0:T(8,128)(2,1)S(1)}, bf16[48,1024]{1,0:T(8,128)(2...) custom-call(bf16[48,1024]{1,0:T(8,128)(2,1)S(1)} %get-tuple-element., ...), custom_call_target="tpu_custom_call" | custom-call | flops 2491416576 | bytes 11010048 | tf_op jit(solution)/shard_map/pallas_call | solution.py:238
  65.5 2.4 %shard_map.169 = (bf16[24,2048]{1,0:T(8,128)(2,1)S(1)}, bf16[24,2048]{1,0:T(8,128)(2,1)S(1)}, bf16[24,2048]{1,0:T(8,128)(2,1)S(1)}, bf16[24,2048]{1,0:T(8,128)(2,1)S(1)}) custom-call(bf16[24,2048]{1,0:T(8,128)(2,1)S(1)} %get-tuple-element.166.refs_0_, bf16[24,2048]{1,0:T(8,128)(2,1)S(1)} %collective-permute-done.22.refs_1_, ...), custom_call_target="tpu_custom_call" | custom-call | flops 830472192 | bytes 9437184 | tf_op jit(solution)/shard_map/pallas_call | solution.py:238
  67.9 0.8 collective-permute-start.31
  68.7 1.5 %collective-permute-start.32 = (bf16[24,2048]{1,0:T(8,128)(2,1)S(1)}, bf16[24,2048]{1,0:T(8,128)(2,1)S(1)}, u32[]{:S(2)}, u32[]{:S(2)}) collective-permute-start(bf16[24,2048]{1,0:T(8,128)(2,1)S(1)} %get-tuple-element.172), channel_id=1, source_target_pairs={{0,2},{1,3},{2,0},{3,1},{4,6},{5,7},{6,4},{7,5},{8,10},{9,11},{10,... | collective-permute-start | bytes 294920 | tf_op jit(solution)/shard_map/ppermute | solution.py:448
  70.2 0.6 collective-permute-start.28
  70.8 1.5 %collective-permute-start.29 = (bf16[48,1024]{1,0:T(8,128)(2,1)S(1)}, bf16[48,1024]{1,0:T(8,128)(2,1)S(1)}, u32[]{:S(2)}, u32[]{:S(2)}) collective-permute-start(bf16[48,1024]{1,0:T(8,128)(2,1)S(1)} %get-tuple-element.163), channel_id=1, source_target_pairs={{0,2},{1,3},{2,0},{3,1},{4,6},{5,7},{6,4},{7,5},{8,10},{9,11},{10,... | collective-permute-start | bytes 294920 | tf_op jit(solution)/shard_map/ppermute | solution.py:448
  72.3 1.6 %collective-permute-done.32.r2 = bf16[24,2048]{1,0:T(8,128)(2,1)S(1)} collective-permute-done((bf16[24,2048]{1,0:T(8,128)(2,1)S(1)}, bf16[24,2048]{1,0:T(8,128)(2,1)S(1)}, u32[]{:S(2)}, u32[]{:S(2)}) %collective-permute-start.32) | collective-permute-done | bytes 98336 | tf_op jit(solution)/shard_map/ppermute | solution.py:448
  73.9 2.0 %collective-permute-start.38 = (bf16[48,1024]{1,0:T(8,128)(2,1)S(1)}, bf16[48,1024]{1,0:T(8,128)(2,1)S(1)}, u32[]{:S(2)}, u32[]{:S(2)}) collective-permute-start(bf16[48,1024]{1,0:T(8,128)(2,1)S(1)} %get-tuple-element.179), channel_id=1, source_target_pairs={{0,2},{1,3},{2,0},{3,1},{4,6},{5,7},{6,4},{7,5},{8,10},{9,11},{10,... | collective-permute-start | bytes 294920 | tf_op jit(solution)/shard_map/ppermute | solution.py:448
  75.8 1.5 %collective-permute-start.39 = (bf16[48,1024]{1,0:T(8,128)(2,1)S(1)}, bf16[48,1024]{1,0:T(8,128)(2,1)S(1)}, u32[]{:S(2)}, u32[]{:S(2)}) collective-permute-start(bf16[48,1024]{1,0:T(8,128)(2,1)S(1)} %get-tuple-element.180), channel_id=1, source_target_pairs={{0,3},{1,2},{2,1},{3,0},{4,7},{5,6},{6,5},{7,4},{8,11},{9,10},{10,... | collective-permute-start | bytes 294920 | tf_op jit(solution)/shard_map/ppermute | solution.py:448
  78.1 1.6 %collective-permute-start.35 = (bf16[64,1024]{1,0:T(8,128)(2,1)S(1)}, bf16[64,1024]{1,0:T(8,128)(2,1)S(1)}, u32[]{:S(2)}, u32[]{:S(2)}) collective-permute-start(bf16[64,1024]{1,0:T(8,128)(2,1)S(1)} %get-tuple-element.175), channel_id=1, source_target_pairs={{0,4},{1,5},{2,6},{3,7},{4,12},{5,13},{6,14},{7,15},{12,8},{13,9},... | collective-permute-start | bytes 393224 | tf_op jit(solution)/shard_map/ppermute | solution.py:448
  80.2 0.7 collective-permute-start.25
  80.9 0.7 collective-permute-done.39.r3
  81.6 1.5 %collective-permute-start.26 = (bf16[24,2048]{1,0:T(8,128)(2,1)S(1)}, bf16[24,2048]{1,0:T(8,128)(2,1)S(1)}, u32[]{:S(2)}, u32[]{:S(2)}) collective-permute-start(bf16[24,2048]{1,0:T(8,128)(2,1)S(1)} %get-tuple-element.157), channel_id=1, source_target_pairs={{0,2},{1,3},{2,0},{3,1},{4,6},{5,7},{6,4},{7,5},{8,10},{9,11},{10,... | collective-permute-start | bytes 294920 | tf_op jit(solution)/shard_map/ppermute | solution.py:448
  83.4 1.0 %collective-permute-done.30.r3 = bf16[48,1024]{1,0:T(8,128)(2,1)S(1)} collective-permute-done((bf16[48,1024]{1,0:T(8,128)(2,1)S(1)}, bf16[48,1024]{1,0:T(8,128)(2,1)S(1)}, u32[]{:S(2)}, u32[]{:S(2)}) %collective-permute-start.30) | collective-permute-done | bytes 98336 | tf_op jit(solution)/shard_map/ppermute | solution.py:448
  84.4 1.5 %collective-permute-start.40 = (bf16[64,1024]{1,0:T(8,128)(2,1)S(1)}, bf16[64,1024]{1,0:T(8,128)(2,1)S(1)}, u32[]{:S(2)}, u32[]{:S(2)}) collective-permute-start(bf16[64,1024]{1,0:T(8,128)(2,1)S(1)} %get-tuple-element.181), channel_id=1, source_target_pairs={{0,4},{1,5},{2,6},{3,7},{4,12},{5,13},{6,14},{7,15},{12,8},{13,9},... | collective-permute-start | bytes 393224 | tf_op jit(solution)/shard_map/ppermute | solution.py:448
  86.0 1.4 %collective-permute-start.41 = (bf16[64,1024]{1,0:T(8,128)(2,1)S(1)}, bf16[64,1024]{1,0:T(8,128)(2,1)S(1)}, u32[]{:S(2)}, u32[]{:S(2)}) collective-permute-start(bf16[64,1024]{1,0:T(8,128)(2,1)S(1)} %get-tuple-element.182), channel_id=1, source_target_pairs={{4,0},{5,1},{6,2},{7,3},{12,4},{13,5},{14,6},{15,7},{8,12},{9,13},... | collective-permute-start | bytes 393224 | tf_op jit(solution)/shard_map/ppermute | solution.py:448
  87.7 0.7 collective-permute-start.36
  88.4 2.3 %collective-permute-start.42 = (bf16[64,1024]{1,0:T(8,128)(2,1)S(1)}, bf16[64,1024]{1,0:T(8,128)(2,1)S(1)}, u32[]{:S(2)}, u32[]{:S(2)}) collective-permute-start(bf16[64,1024]{1,0:T(8,128)(2,1)S(1)} %get-tuple-element.183), channel_id=1, source_target_pairs={{4,0},{5,1},{6,2},{7,3},{12,4},{13,5},{14,6},{15,7},{8,12},{9,13},... | collective-permute-start | bytes 393224 | tf_op jit(solution)/shard_map/ppermute | solution.py:448
  90.7 5.0 %collective-permute-done.27.r3 = bf16[24,2048]{1,0:T(8,128)(2,1)S(1)} collective-permute-done((bf16[24,2048]{1,0:T(8,128)(2,1)S(1)}, bf16[24,2048]{1,0:T(8,128)(2,1)S(1)}, u32[]{:S(2)}, u32[]{:S(2)}) %collective-permute-start.27) | collective-permute-done | bytes 98336 | tf_op jit(solution)/shard_map/ppermute | solution.py:448
  95.7 0.5 collective-permute-done.36.x_low
  96.2 2.7 %collective-permute-done.42.y_high = bf16[64,1024]{1,0:T(8,128)(2,1)S(1)} collective-permute-done((bf16[64,1024]{1,0:T(8,128)(2,1)S(1)}, bf16[64,1024]{1,0:T(8,128)(2,1)S(1)}, u32[]{:S(2)}, u32[]{:S(2)}) %collective-permute-start.42) | collective-permute-done | bytes 131104 | tf_op jit(solution)/shard_map/ppermute | solution.py:448
  98.9 1.0 shard_map.173
  (75 shorter events, 4.4 us)
Async XLA Ops:
  0.6 1.0 %copy-start = (bf16[256,8,128]{2,1,0:T(8,128)(2,1)S(1)}, bf16[256,8,128]{2,1,0:T(8,128)(2,1)}, u32[]{:S(2)}) copy-start(bf16[256,8,128]{2,1,0:T(8,128)(2,1)} %param.22) | copy-start | bytes 1572868
  0.6 23.5 %copy-start.4 = (bf16[512,2048]{1,0:T(8,128)(2,1)S(1)}, bf16[512,2048]{1,0:T(8,128)(2,1)}, u32[]{:S(2)}) copy-start(bf16[512,2048]{1,0:T(8,128)(2,1)} %out_w_ref.3) | copy-start | bytes 6291460
  1.8 6.5 %collective-permute-start = (bf16[128,4,128]{2,0,1:T(8,128)(2,1)S(1)}, bf16[128,4,128]{2,0,1:T(8,128)(2,1)S(1)}, u32[]{:S(2)}, u32[]{:S(2)}) collective-permute-start(bf16[128,4,128]{2,0,1:T(8,128)(2,1)S(1)} %copy.21), channel_id=1, source_target_pairs={{0,16},{16,0},{1,17},{17,1},{2,18},{18,2},{3,19},{19,3},{4,20},{20... | collective-permute-start | bytes 393224 | tf_op jit(solution)/shard_map/ppermute | solution.py:71
  8.3 10.7 %collective-permute-start.1 = (bf16[128,4,128]{2,0,1:T(8,128)(2,1)S(1)}, bf16[128,4,128]{2,0,1:T(8,128)(2,1)}, u32[]{:S(2)}, u32[]{:S(2)}) collective-permute-start(bf16[128,4,128]{2,0,1:T(8,128)(2,1)S(1)} %collective-permute-done), channel_id=1, source_target_pairs={{0,1},{1,0},{2,3},{3,2},{4,5},{5,4},{6,7},{7,6},{8,9},{9,8},{10,11... | collective-permute-start | bytes 393224 | tf_op jit(solution)/shard_map/ppermute | solution.py:79
  8.3 1.0 %copy-start.8 = (bf16[1,64,8,512]{3,2,1,0:T(8,128)(2,1)S(1)}, bf16[1,64,8,512]{3,2,1,0:T(8,128)(2,1)}, u32[]{:S(2)}) copy-start(bf16[1,64,8,512]{3,2,1,0:T(8,128)(2,1)} %param.16) | copy-start | bytes 1572868
  9.4 0.9 copy-start.9
  10.3 0.8 copy-start.10
  11.1 0.8 copy-start.11
  11.9 0.7 copy-start.12
  12.7 0.7 copy-start.13
  15.4 8.8 %collective-permute-start.2 = (bf16[4,64,512]{2,1,0:T(8,128)(2,1)S(1)}, bf16[4,64,512]{2,1,0:T(8,128)(2,1)S(1)}, u32[]{:S(2)}, u32[]{:S(2)}) collective-permute-start(bf16[4,64,512]{2,1,0:T(8,128)(2,1)S(1)} %get-tuple-element.94), channel_id=1, source_target_pairs={{0,16},{16,0},{1,17},{17,1},{2,18},{18,2},{3,19},{19,3},{4,20},{20... | collective-permute-start | bytes 786440 | tf_op jit(solution)/shard_map/ppermute | solution.py:78
  17.2 9.4 %copy-start.14 = (s32[1,64,6]{1,0,2:T(1,128)S(1)}, s32[1,64,6]{1,0,2:T(1,128)}, u32[]{:S(2)}) copy-start(s32[1,64,6]{1,0,2:T(1,128)} %param.26) | copy-start | bytes 4612
  20.2 15.3 %copy-start.5 = (bf16[1,64,2048]{2,1,0:T(8,128)(2,1)S(1)}, bf16[1,64,2048]{2,1,0:T(8,128)(2,1)}, u32[]{:S(2)}) copy-start(bf16[1,64,2048]{2,1,0:T(8,128)(2,1)} %x_ref.1) | copy-start | bytes 786436
  20.2 15.3 %copy-start.7 = (f32[2048]{0:T(1024)S(1)}, f32[2048]{0:T(1024)}, u32[]{:S(2)}) copy-start(f32[2048]{0:T(1024)} %param.24) | copy-start | bytes 24580
  24.2 37.7 %copy-start.3 = (bf16[1,704,2048]{2,1,0:T(8,128)(2,1)S(1)}, bf16[1,704,2048]{2,1,0:T(8,128)(2,1)}, u32[]{:S(2)}) copy-start(bf16[1,704,2048]{2,1,0:T(8,128)(2,1)} %param.29) | copy-start | bytes 8650756
  24.8 33.6 %copy-start.6 = (bf16[2048,16]{0,1:T(8,128)(2,1)S(1)}, bf16[2048,16]{0,1:T(8,128)(2,1)}, u32[]{:S(2)}) copy-start(bf16[2048,16]{0,1:T(8,128)(2,1)} %param.25) | copy-start | bytes 196612
  24.8 10.8 %collective-permute-start.3 = (bf16[64,2048]{1,0:T(8,128)(2,1)S(1)}, bf16[64,2048]{1,0:T(8,128)(2,1)S(1)}, u32[]{:S(2)}, u32[]{:S(2)}) collective-permute-start(bf16[64,2048]{1,0:T(8,128)(2,1)S(1)} %shard_map.160), channel_id=1, source_target_pairs={{0,16},{16,0},{1,17},{17,1},{2,18},{18,2},{3,19},{19,3},{4,20},{20... | collective-permute-start | bytes 786440 | tf_op jit(solution)/shard_map/ppermute | solution.py:100
  26.6 5.6 %collective-permute-start.6 = (s32[6,64]{1,0:T(8,128)S(1)}, s32[6,64]{1,0:T(8,128)S(1)}, u32[]{:S(2)}, u32[]{:S(2)}) collective-permute-start(s32[6,64]{1,0:T(8,128)S(1)} %bitcast.30), channel_id=1, source_target_pairs={{0,12},{1,13},{2,14},{3,15},{4,8},{5,9},{6,10},{7,11},{8,4},{9,5},... | collective-permute-start | bytes 4616 | tf_op jit(solution)/shard_map/ppermute | solution.py:610
  30.2 3.6 %collective-permute-start.5 = (s32[6,64]{1,0:T(8,128)S(1)}, s32[6,64]{1,0:T(8,128)S(1)}, u32[]{:S(2)}, u32[]{:S(2)}) collective-permute-start(s32[6,64]{1,0:T(8,128)S(1)} %bitcast.31), channel_id=1, source_target_pairs={{4,0},{5,1},{6,2},{7,3},{12,4},{13,5},{14,6},{15,7},{8,12},{9,13},... | collective-permute-start | bytes 4616 | tf_op jit(solution)/shard_map/ppermute | solution.py:609
  30.2 4.5 %collective-permute-start.4 = (s32[6,64]{1,0:T(8,128)S(1)}, s32[6,64]{1,0:T(8,128)S(1)}, u32[]{:S(2)}, u32[]{:S(2)}) collective-permute-start(s32[6,64]{1,0:T(8,128)S(1)} %bitcast.32), channel_id=1, source_target_pairs={{0,4},{1,5},{2,6},{3,7},{4,12},{5,13},{6,14},{7,15},{12,8},{13,9},... | collective-permute-start | bytes 4616 | tf_op jit(solution)/shard_map/ppermute | solution.py:609
  34.9 27.0 %copy-start.1 = (bf16[1,2048,704]{1,2,0:T(8,128)(2,1)S(1)}, bf16[1,2048,704]{1,2,0:T(8,128)(2,1)}, u32[]{:S(2)}) copy-start(bf16[1,2048,704]{1,2,0:T(8,128)(2,1)} %param.27) | copy-start | bytes 8650756
  34.9 26.9 %copy-start.2 = (bf16[1,2048,704]{1,2,0:T(8,128)(2,1)S(1)}, bf16[1,2048,704]{1,2,0:T(8,128)(2,1)}, u32[]{:S(2)}) copy-start(bf16[1,2048,704]{1,2,0:T(8,128)(2,1)} %param.28) | copy-start | bytes 8650756
  36.4 9.1 %collective-permute-start.13 = (bf16[64,1024]{1,0:T(8,128)(2,1)S(1)}, bf16[64,1024]{1,0:T(8,128)(2,1)S(1)}, u32[]{:S(2)}, u32[]{:S(2)}) collective-permute-start(bf16[64,1024]{1,0:T(8,128)(2,1)S(1)} %get-tuple-element.102.refs_2_), channel_id=1, source_target_pairs={{4,0},{5,1},{6,2},{7,3},{12,4},{13,5},{14,6},{15,7},{8,12},{9,13},... | collective-permute-start | bytes 393224 | tf_op jit(solution)/shard_map/ppermute | solution.py:448
  36.5 10.5 %collective-permute-start.12 = (bf16[64,1024]{1,0:T(8,128)(2,1)S(1)}, bf16[64,1024]{1,0:T(8,128)(2,1)S(1)}, u32[]{:S(2)}, u32[]{:S(2)}) collective-permute-start(bf16[64,1024]{1,0:T(8,128)(2,1)S(1)} %get-tuple-element.103.refs_1_), channel_id=1, source_target_pairs={{0,4},{1,5},{2,6},{3,7},{4,12},{5,13},{6,14},{7,15},{12,8},{13,9},... | collective-permute-start | bytes 393224 | tf_op jit(solution)/shard_map/ppermute | solution.py:448
  38.7 1.9 %collective-permute-start.9 = (bf16[24,2048]{1,0:T(8,128)(2,1)S(1)}, bf16[24,2048]{1,0:T(8,128)(2,1)S(1)}, u32[]{:S(2)}, u32[]{:S(2)}) collective-permute-start(bf16[24,2048]{1,0:T(8,128)(2,1)S(1)} %get-tuple-element.106), channel_id=1, source_target_pairs={{0,1},{1,0},{2,3},{3,2},{4,5},{5,4},{6,7},{7,6},{8,9},{9,8},{10,11... | collective-permute-start | bytes 294920 | tf_op jit(solution)/shard_map/ppermute | solution.py:448
  38.8 5.7 %collective-permute-start.10 = (bf16[24,2048]{1,0:T(8,128)(2,1)S(1)}, bf16[24,2048]{1,0:T(8,128)(2,1)S(1)}, u32[]{:S(2)}, u32[]{:S(2)}) collective-permute-start(bf16[24,2048]{1,0:T(8,128)(2,1)S(1)} %get-tuple-element.107), channel_id=1, source_target_pairs={{0,2},{1,3},{2,0},{3,1},{4,6},{5,7},{6,4},{7,5},{8,10},{9,11},{10,... | collective-permute-start | bytes 294920 | tf_op jit(solution)/shard_map/ppermute | solution.py:448
  40.4 7.4 %collective-permute-start.11 = (bf16[24,2048]{1,0:T(8,128)(2,1)S(1)}, bf16[24,2048]{1,0:T(8,128)(2,1)S(1)}, u32[]{:S(2)}, u32[]{:S(2)}) collective-permute-start(bf16[24,2048]{1,0:T(8,128)(2,1)S(1)} %get-tuple-element.108), channel_id=1, source_target_pairs={{0,3},{1,2},{2,1},{3,0},{4,7},{5,6},{6,5},{7,4},{8,11},{9,10},{10,... | collective-permute-start | bytes 294920 | tf_op jit(solution)/shard_map/ppermute | solution.py:448
  40.7 7.2 %collective-permute-start.7 = (bf16[64,1024]{1,0:T(8,128)(2,1)S(1)}, bf16[64,1024]{1,0:T(8,128)(2,1)S(1)}, u32[]{:S(2)}, u32[]{:S(2)}) collective-permute-start(bf16[64,1024]{1,0:T(8,128)(2,1)S(1)} %get-tuple-element.102.refs_2_), channel_id=1, source_target_pairs={{0,4},{1,5},{2,6},{3,7},{4,12},{5,13},{6,14},{7,15},{12,8},{13,9},... | collective-permute-start | bytes 393224 | tf_op jit(solution)/shard_map/ppermute | solution.py:448
  44.6 6.5 %collective-permute-start.8 = (bf16[64,1024]{1,0:T(8,128)(2,1)S(1)}, bf16[64,1024]{1,0:T(8,128)(2,1)S(1)}, u32[]{:S(2)}, u32[]{:S(2)}) collective-permute-start(bf16[64,1024]{1,0:T(8,128)(2,1)S(1)} %get-tuple-element.103.refs_1_), channel_id=1, source_target_pairs={{4,0},{5,1},{6,2},{7,3},{12,4},{13,5},{14,6},{15,7},{8,12},{9,13},... | collective-permute-start | bytes 393224 | tf_op jit(solution)/shard_map/ppermute | solution.py:448
  45.5 8.2 %collective-permute-start.15 = (bf16[64,1024]{1,0:T(8,128)(2,1)S(1)}, bf16[64,1024]{1,0:T(8,128)(2,1)S(1)}, u32[]{:S(2)}, u32[]{:S(2)}) collective-permute-start(bf16[64,1024]{1,0:T(8,128)(2,1)S(1)} %collective-permute-done.13.refs_3_.refs_8_), channel_id=1, source_target_pairs={{4,0},{5,1},{6,2},{7,3},{12,4},{13,5},{14,6},{15,7},{8,12},{9,13},... | collective-permute-start | bytes 393224 | tf_op jit(solution)/shard_map/ppermute | solution.py:448
  47.0 9.9 %collective-permute-start.14 = (bf16[64,1024]{1,0:T(8,128)(2,1)S(1)}, bf16[64,1024]{1,0:T(8,128)(2,1)S(1)}, u32[]{:S(2)}, u32[]{:S(2)}) collective-permute-start(bf16[64,1024]{1,0:T(8,128)(2,1)S(1)} %collective-permute-done.12.refs_1_.refs_4_), channel_id=1, source_target_pairs={{0,4},{1,5},{2,6},{3,7},{4,12},{5,13},{6,14},{7,15},{12,8},{13,9},... | collective-permute-start | bytes 393224 | tf_op jit(solution)/shard_map/ppermute | solution.py:448
  47.8 3.5 %collective-permute-start.16 = (bf16[48,1024]{1,0:T(8,128)(2,1)S(1)}, bf16[48,1024]{1,0:T(8,128)(2,1)S(1)}, u32[]{:S(2)}, u32[]{:S(2)}) collective-permute-start(bf16[48,1024]{1,0:T(8,128)(2,1)S(1)} %get-tuple-element.128), channel_id=1, source_target_pairs={{0,1},{1,0},{2,3},{3,2},{4,5},{5,4},{6,7},{7,6},{8,9},{9,8},{10,11... | collective-permute-start | bytes 294920 | tf_op jit(solution)/shard_map/ppermute | solution.py:448
  47.9 11.0 %collective-permute-start.17 = (bf16[48,1024]{1,0:T(8,128)(2,1)S(1)}, bf16[48,1024]{1,0:T(8,128)(2,1)S(1)}, u32[]{:S(2)}, u32[]{:S(2)}) collective-permute-start(bf16[48,1024]{1,0:T(8,128)(2,1)S(1)} %get-tuple-element.129), channel_id=1, source_target_pairs={{0,2},{1,3},{2,0},{3,1},{4,6},{5,7},{6,4},{7,5},{8,10},{9,11},{10,... | collective-permute-start | bytes 294920 | tf_op jit(solution)/shard_map/ppermute | solution.py:448
  51.0 8.5 %collective-permute-start.18 = (bf16[48,1024]{1,0:T(8,128)(2,1)S(1)}, bf16[48,1024]{1,0:T(8,128)(2,1)S(1)}, u32[]{:S(2)}, u32[]{:S(2)}) collective-permute-start(bf16[48,1024]{1,0:T(8,128)(2,1)S(1)} %get-tuple-element.130), channel_id=1, source_target_pairs={{0,3},{1,2},{2,1},{3,0},{4,7},{5,6},{6,5},{7,4},{8,11},{9,10},{10,... | collective-permute-start | bytes 294920 | tf_op jit(solution)/shard_map/ppermute | solution.py:448
  51.3 8.7 %collective-permute-start.19 = (bf16[48,1024]{1,0:T(8,128)(2,1)S(1)}, bf16[48,1024]{1,0:T(8,128)(2,1)S(1)}, u32[]{:S(2)}, u32[]{:S(2)}) collective-permute-start(bf16[48,1024]{1,0:T(8,128)(2,1)S(1)} %get-tuple-element.132), channel_id=1, source_target_pairs={{0,1},{1,0},{2,3},{3,2},{4,5},{5,4},{6,7},{7,6},{8,9},{9,8},{10,11... | collective-permute-start | bytes 294920 | tf_op jit(solution)/shard_map/ppermute | solution.py:448
  53.7 7.2 %collective-permute-start.20 = (bf16[48,1024]{1,0:T(8,128)(2,1)S(1)}, bf16[48,1024]{1,0:T(8,128)(2,1)S(1)}, u32[]{:S(2)}, u32[]{:S(2)}) collective-permute-start(bf16[48,1024]{1,0:T(8,128)(2,1)S(1)} %get-tuple-element.133), channel_id=1, source_target_pairs={{0,2},{1,3},{2,0},{3,1},{4,6},{5,7},{6,4},{7,5},{8,10},{9,11},{10,... | collective-permute-start | bytes 294920 | tf_op jit(solution)/shard_map/ppermute | solution.py:448
  57.0 4.9 %collective-permute-start.21 = (bf16[48,1024]{1,0:T(8,128)(2,1)S(1)}, bf16[48,1024]{1,0:T(8,128)(2,1)S(1)}, u32[]{:S(2)}, u32[]{:S(2)}) collective-permute-start(bf16[48,1024]{1,0:T(8,128)(2,1)S(1)} %get-tuple-element.134), channel_id=1, source_target_pairs={{0,3},{1,2},{2,1},{3,0},{4,7},{5,6},{6,5},{7,4},{8,11},{9,10},{10,... | collective-permute-start | bytes 294920 | tf_op jit(solution)/shard_map/ppermute | solution.py:448
  58.9 5.9 %collective-permute-start.22 = (bf16[24,2048]{1,0:T(8,128)(2,1)S(1)}, bf16[24,2048]{1,0:T(8,128)(2,1)S(1)}, u32[]{:S(2)}, u32[]{:S(2)}) collective-permute-start(bf16[24,2048]{1,0:T(8,128)(2,1)S(1)} %get-tuple-element.152), channel_id=1, source_target_pairs={{0,1},{1,0},{2,3},{3,2},{4,5},{5,4},{6,7},{7,6},{8,9},{9,8},{10,11... | collective-permute-start | bytes 294920 | tf_op jit(solution)/shard_map/ppermute | solution.py:448
  59.5 5.7 %collective-permute-start.23 = (bf16[24,2048]{1,0:T(8,128)(2,1)S(1)}, bf16[24,2048]{1,0:T(8,128)(2,1)S(1)}, u32[]{:S(2)}, u32[]{:S(2)}) collective-permute-start(bf16[24,2048]{1,0:T(8,128)(2,1)S(1)} %get-tuple-element.153), channel_id=1, source_target_pairs={{0,2},{1,3},{2,0},{3,1},{4,6},{5,7},{6,4},{7,5},{8,10},{9,11},{10,... | collective-permute-start | bytes 294920 | tf_op jit(solution)/shard_map/ppermute | solution.py:448
  60.0 5.5 %collective-permute-start.24 = (bf16[24,2048]{1,0:T(8,128)(2,1)S(1)}, bf16[24,2048]{1,0:T(8,128)(2,1)S(1)}, u32[]{:S(2)}, u32[]{:S(2)}) collective-permute-start(bf16[24,2048]{1,0:T(8,128)(2,1)S(1)} %get-tuple-element.154), channel_id=1, source_target_pairs={{0,3},{1,2},{2,1},{3,0},{4,7},{5,6},{6,5},{7,4},{8,11},{9,10},{10,... | collective-permute-start | bytes 294920 | tf_op jit(solution)/shard_map/ppermute | solution.py:448
  67.9 4.4 %collective-permute-start.31 = (bf16[24,2048]{1,0:T(8,128)(2,1)S(1)}, bf16[24,2048]{1,0:T(8,128)(2,1)S(1)}, u32[]{:S(2)}, u32[]{:S(2)}) collective-permute-start(bf16[24,2048]{1,0:T(8,128)(2,1)S(1)} %get-tuple-element.171), channel_id=1, source_target_pairs={{0,1},{1,0},{2,3},{3,2},{4,5},{5,4},{6,7},{7,6},{8,9},{9,8},{10,11... | collective-permute-start | bytes 294920 | tf_op jit(solution)/shard_map/ppermute | solution.py:448
  68.7 5.2 %collective-permute-start.32 = (bf16[24,2048]{1,0:T(8,128)(2,1)S(1)}, bf16[24,2048]{1,0:T(8,128)(2,1)S(1)}, u32[]{:S(2)}, u32[]{:S(2)}) collective-permute-start(bf16[24,2048]{1,0:T(8,128)(2,1)S(1)} %get-tuple-element.172), channel_id=1, source_target_pairs={{0,2},{1,3},{2,0},{3,1},{4,6},{5,7},{6,4},{7,5},{8,10},{9,11},{10,... | collective-permute-start | bytes 294920 | tf_op jit(solution)/shard_map/ppermute | solution.py:448
  70.2 5.7 %collective-permute-start.33 = (bf16[24,2048]{1,0:T(8,128)(2,1)S(1)}, bf16[24,2048]{1,0:T(8,128)(2,1)S(1)}, u32[]{:S(2)}, u32[]{:S(2)}) collective-permute-start(bf16[24,2048]{1,0:T(8,128)(2,1)S(1)} %get-tuple-element.173), channel_id=1, source_target_pairs={{0,3},{1,2},{2,1},{3,0},{4,7},{5,6},{6,5},{7,4},{8,11},{9,10},{10,... | collective-permute-start | bytes 294920 | tf_op jit(solution)/shard_map/ppermute | solution.py:448
  70.2 7.5 %collective-permute-start.28 = (bf16[48,1024]{1,0:T(8,128)(2,1)S(1)}, bf16[48,1024]{1,0:T(8,128)(2,1)S(1)}, u32[]{:S(2)}, u32[]{:S(2)}) collective-permute-start(bf16[48,1024]{1,0:T(8,128)(2,1)S(1)} %get-tuple-element.162), channel_id=1, source_target_pairs={{0,1},{1,0},{2,3},{3,2},{4,5},{5,4},{6,7},{7,6},{8,9},{9,8},{10,11... | collective-permute-start | bytes 294920 | tf_op jit(solution)/shard_map/ppermute | solution.py:448
  70.8 7.3 %collective-permute-start.29 = (bf16[48,1024]{1,0:T(8,128)(2,1)S(1)}, bf16[48,1024]{1,0:T(8,128)(2,1)S(1)}, u32[]{:S(2)}, u32[]{:S(2)}) collective-permute-start(bf16[48,1024]{1,0:T(8,128)(2,1)S(1)} %get-tuple-element.163), channel_id=1, source_target_pairs={{0,2},{1,3},{2,0},{3,1},{4,6},{5,7},{6,4},{7,5},{8,10},{9,11},{10,... | collective-permute-start | bytes 294920 | tf_op jit(solution)/shard_map/ppermute | solution.py:448
  72.3 7.4 %collective-permute-start.37 = (bf16[48,1024]{1,0:T(8,128)(2,1)S(1)}, bf16[48,1024]{1,0:T(8,128)(2,1)S(1)}, u32[]{:S(2)}, u32[]{:S(2)}) collective-permute-start(bf16[48,1024]{1,0:T(8,128)(2,1)S(1)} %get-tuple-element.178), channel_id=1, source_target_pairs={{0,1},{1,0},{2,3},{3,2},{4,5},{5,4},{6,7},{7,6},{8,9},{9,8},{10,11... | collective-permute-start | bytes 294920 | tf_op jit(solution)/shard_map/ppermute | solution.py:448
  73.9 6.3 %collective-permute-start.38 = (bf16[48,1024]{1,0:T(8,128)(2,1)S(1)}, bf16[48,1024]{1,0:T(8,128)(2,1)S(1)}, u32[]{:S(2)}, u32[]{:S(2)}) collective-permute-start(bf16[48,1024]{1,0:T(8,128)(2,1)S(1)} %get-tuple-element.179), channel_id=1, source_target_pairs={{0,2},{1,3},{2,0},{3,1},{4,6},{5,7},{6,4},{7,5},{8,10},{9,11},{10,... | collective-permute-start | bytes 294920 | tf_op jit(solution)/shard_map/ppermute | solution.py:448
  75.8 5.7 %collective-permute-start.39 = (bf16[48,1024]{1,0:T(8,128)(2,1)S(1)}, bf16[48,1024]{1,0:T(8,128)(2,1)S(1)}, u32[]{:S(2)}, u32[]{:S(2)}) collective-permute-start(bf16[48,1024]{1,0:T(8,128)(2,1)S(1)} %get-tuple-element.180), channel_id=1, source_target_pairs={{0,3},{1,2},{2,1},{3,0},{4,7},{5,6},{6,5},{7,4},{8,11},{9,10},{10,... | collective-permute-start | bytes 294920 | tf_op jit(solution)/shard_map/ppermute | solution.py:448
  77.7 8.3 %collective-permute-start.34 = (bf16[64,1024]{1,0:T(8,128)(2,1)S(1)}, bf16[64,1024]{1,0:T(8,128)(2,1)S(1)}, u32[]{:S(2)}, u32[]{:S(2)}) collective-permute-start(bf16[64,1024]{1,0:T(8,128)(2,1)S(1)} %get-tuple-element.174), channel_id=1, source_target_pairs={{4,0},{5,1},{6,2},{7,3},{12,4},{13,5},{14,6},{15,7},{8,12},{9,13},... | collective-permute-start | bytes 393224 | tf_op jit(solution)/shard_map/ppermute | solution.py:448
  78.1 9.3 %collective-permute-start.35 = (bf16[64,1024]{1,0:T(8,128)(2,1)S(1)}, bf16[64,1024]{1,0:T(8,128)(2,1)S(1)}, u32[]{:S(2)}, u32[]{:S(2)}) collective-permute-start(bf16[64,1024]{1,0:T(8,128)(2,1)S(1)} %get-tuple-element.175), channel_id=1, source_target_pairs={{0,4},{1,5},{2,6},{3,7},{4,12},{5,13},{6,14},{7,15},{12,8},{13,9},... | collective-permute-start | bytes 393224 | tf_op jit(solution)/shard_map/ppermute | solution.py:448
  79.8 4.7 %collective-permute-start.30 = (bf16[48,1024]{1,0:T(8,128)(2,1)S(1)}, bf16[48,1024]{1,0:T(8,128)(2,1)S(1)}, u32[]{:S(2)}, u32[]{:S(2)}) collective-permute-start(bf16[48,1024]{1,0:T(8,128)(2,1)S(1)} %get-tuple-element.164), channel_id=1, source_target_pairs={{0,3},{1,2},{2,1},{3,0},{4,7},{5,6},{6,5},{7,4},{8,11},{9,10},{10,... | collective-permute-start | bytes 294920 | tf_op jit(solution)/shard_map/ppermute | solution.py:448
  80.2 8.2 %collective-permute-start.25 = (bf16[24,2048]{1,0:T(8,128)(2,1)S(1)}, bf16[24,2048]{1,0:T(8,128)(2,1)S(1)}, u32[]{:S(2)}, u32[]{:S(2)}) collective-permute-start(bf16[24,2048]{1,0:T(8,128)(2,1)S(1)} %get-tuple-element.156), channel_id=1, source_target_pairs={{0,1},{1,0},{2,3},{3,2},{4,5},{5,4},{6,7},{7,6},{8,9},{9,8},{10,11... | collective-permute-start | bytes 294920 | tf_op jit(solution)/shard_map/ppermute | solution.py:448
  81.6 9.1 %collective-permute-start.26 = (bf16[24,2048]{1,0:T(8,128)(2,1)S(1)}, bf16[24,2048]{1,0:T(8,128)(2,1)S(1)}, u32[]{:S(2)}, u32[]{:S(2)}) collective-permute-start(bf16[24,2048]{1,0:T(8,128)(2,1)S(1)} %get-tuple-element.157), channel_id=1, source_target_pairs={{0,2},{1,3},{2,0},{3,1},{4,6},{5,7},{6,4},{7,5},{8,10},{9,11},{10,... | collective-permute-start | bytes 294920 | tf_op jit(solution)/shard_map/ppermute | solution.py:448
  84.4 11.2 %collective-permute-start.40 = (bf16[64,1024]{1,0:T(8,128)(2,1)S(1)}, bf16[64,1024]{1,0:T(8,128)(2,1)S(1)}, u32[]{:S(2)}, u32[]{:S(2)}) collective-permute-start(bf16[64,1024]{1,0:T(8,128)(2,1)S(1)} %get-tuple-element.181), channel_id=1, source_target_pairs={{0,4},{1,5},{2,6},{3,7},{4,12},{5,13},{6,14},{7,15},{12,8},{13,9},... | collective-permute-start | bytes 393224 | tf_op jit(solution)/shard_map/ppermute | solution.py:448
  86.0 9.7 %collective-permute-start.41 = (bf16[64,1024]{1,0:T(8,128)(2,1)S(1)}, bf16[64,1024]{1,0:T(8,128)(2,1)S(1)}, u32[]{:S(2)}, u32[]{:S(2)}) collective-permute-start(bf16[64,1024]{1,0:T(8,128)(2,1)S(1)} %get-tuple-element.182), channel_id=1, source_target_pairs={{4,0},{5,1},{6,2},{7,3},{12,4},{13,5},{14,6},{15,7},{8,12},{9,13},... | collective-permute-start | bytes 393224 | tf_op jit(solution)/shard_map/ppermute | solution.py:448
  87.7 8.5 %collective-permute-start.36 = (bf16[64,1024]{1,0:T(8,128)(2,1)S(1)}, bf16[64,1024]{1,0:T(8,128)(2,1)S(1)}, u32[]{:S(2)}, u32[]{:S(2)}) collective-permute-start(bf16[64,1024]{1,0:T(8,128)(2,1)S(1)} %get-tuple-element.176), channel_id=1, source_target_pairs={{0,4},{1,5},{2,6},{3,7},{4,12},{5,13},{6,14},{7,15},{12,8},{13,9},... | collective-permute-start | bytes 393224 | tf_op jit(solution)/shard_map/ppermute | solution.py:448
  88.4 10.5 %collective-permute-start.42 = (bf16[64,1024]{1,0:T(8,128)(2,1)S(1)}, bf16[64,1024]{1,0:T(8,128)(2,1)S(1)}, u32[]{:S(2)}, u32[]{:S(2)}) collective-permute-start(bf16[64,1024]{1,0:T(8,128)(2,1)S(1)} %get-tuple-element.183), channel_id=1, source_target_pairs={{4,0},{5,1},{6,2},{7,3},{12,4},{13,5},{14,6},{15,7},{8,12},{9,13},... | collective-permute-start | bytes 393224 | tf_op jit(solution)/shard_map/ppermute | solution.py:448
  90.7 5.0 %collective-permute-start.27 = (bf16[24,2048]{1,0:T(8,128)(2,1)S(1)}, bf16[24,2048]{1,0:T(8,128)(2,1)S(1)}, u32[]{:S(2)}, u32[]{:S(2)}) collective-permute-start(bf16[24,2048]{1,0:T(8,128)(2,1)S(1)} %get-tuple-element.158), channel_id=1, source_target_pairs={{0,3},{1,2},{2,1},{3,0},{4,7},{5,6},{6,5},{7,4},{8,11},{9,10},{10,... | collective-permute-start | bytes 294920 | tf_op jit(solution)/shard_map/ppermute | solution.py:448
